TPU v7x, 256 devices: a whole 4x4x8 slice. The times are simulated.
256 devices in a mesh: ctx: 32 (over x_lo, z, core), head: 8 (over x_hi, y).
Axes of the slice: x: 4 (x_hi: 2, x_lo: 2; x = x_hi * 2 + x_lo), y: 4, z: 8, core: 2. Of those that a mesh axis runs over, the one named last changes fastest.
Arguments:
- queries: bfloat16 [2, 8192, 32, 128], P(None, 'ctx', 'head')
- key_rows: bfloat16 [8192, 8, 128], P('ctx', 'head')
- value_rows: bfloat16 [8192, 8, 128], P('ctx', 'head'), may hold values from -6 to 6
- attn_out: bfloat16 [2, 8192, 32, 128], P(None, 'ctx', 'head'), may hold values from -3 to 3
- out_grad: bfloat16 [2, 8192, 32, 128], P(None, 'ctx', 'head'), may hold values from -6 to 6
- log_norm: float32 [2, 32, 8192], P(None, 'head', 'ctx'), as said below
- positions: int32 [8192], P('ctx'), may hold values from 0 to 8191, as said below
- key_weight: bfloat16 [8192, 8, 128], P(None, 'head'), may hold values from -0.25 to 0.25
- value_weight: bfloat16 [8192, 8, 128], P(None, 'head'), may hold values from -0.1875 to 0.1875
Outputs:
- query_grad: bfloat16 [2, 8192, 32, 128], P(None, 'ctx', 'head')
- key_grad: bfloat16 [8192, 8, 128], P('ctx', 'head')
- value_grad: bfloat16 [8192, 8, 128], P('ctx', 'head')
- input_grad: bfloat16 [8192, 8192], P('head', 'ctx')
Inputs may be any that keep to these rules, and one draw needn't show every extreme that they name: positions is a permutation of the sequence's positions; the stored tokens come in runs of 128 consecutive positions in rising order, and the run of rows k * 256 to k * 256 + 256 / 2 - 1 holds run j of the sequence while the next 128 rows hold run 2 * 32 - 1 - j. log_norm is the log of the total of the softmax row that probs describes, so each row of probs sums to one.
All inputs are finite; a program needn't handle non-finite values.
Results may differ from a plain program's by a relative error of at most 0.0057.
Values may be sent and summed in bfloat16 or wider, within the bound.
No kernel may reach another device: no remote copies, remote signals or barrier semaphores. Data moves between devices by JAX's collectives and lax.ppermute only.
A program may use at most 128 MiB of HBM per device.

v0:
```python
import jax
import jax.numpy as jnp
from jax import lax
from jax.sharding import PartitionSpec as P


def shifted(block, axis, distance):
    devices = range(lax.axis_size(axis))
    route = [((i - distance) % len(devices), i) for i in devices]
    return lax.ppermute(block, axis, route)


def on_device(
    queries, key_rows, value_rows, attn_out, out_grad, log_norm, positions, key_weight, value_weight
):
    members = lax.axis_size("ctx")
    rank_self = lax.axis_index("ctx")
    layers, tokens, head_count, head_dim = queries.shape
    kv_heads = key_rows.shape[1]
    per_group = head_count // kv_heads
    half_rows = tokens // 2
    scaling = head_dim ** (-0.5)
    split_shape = (layers, tokens, kv_heads, per_group, head_dim)
    query_split = queries.reshape(split_shape)
    grad_split = out_grad.reshape(split_shape)
    deltas = jnp.einsum(
        "ltgqd,ltgqd->lgqt",
        grad_split,
        attn_out.reshape(split_shape),
        preferred_element_type=jnp.float32,
    )
    norm_rows = log_norm.reshape(layers, kv_heads, per_group, tokens)
    every_position = lax.all_gather(positions, "ctx", axis=0, tiled=True)

    def tile_grads(query_part, key_piece, value_piece, key_pos):
        low = query_part * half_rows
        high = low + half_rows
        query_pos = positions[low:high]
        query_tile = query_split[:, low:high]
        grad_tile = grad_split[:, low:high]
        delta_tile = deltas[..., low:high]
        norm_tile = norm_rows[..., low:high]

        def compute(unused):
            scores = jnp.einsum(
                "lrgqd,kgd->lgqrk", query_tile, key_piece, preferred_element_type=jnp.float32
            )
            allowed = key_pos[None, :] <= query_pos[:, None]
            probs = jnp.exp(jnp.where(allowed, scores * scaling - norm_tile[..., None], -jnp.inf))
            dprobs = jnp.einsum(
                "lrgqd,kgd->lgqrk", grad_tile, value_piece, preferred_element_type=jnp.float32
            )
            dscore = (scaling * probs * (dprobs - delta_tile[..., None])).astype(jnp.bfloat16)
            prob_half = probs.astype(jnp.bfloat16)
            query_term = jnp.einsum(
                "lgqrk,kgd->lrgqd", dscore, key_piece, preferred_element_type=jnp.float32
            )
            key_term = jnp.einsum(
                "lgqrk,lrgqd->kgd", dscore, query_tile, preferred_element_type=jnp.float32
            )
            value_term = jnp.einsum(
                "lgqrk,lrgqd->kgd", prob_half, grad_tile, preferred_element_type=jnp.float32
            )
            return (query_term, key_term, value_term)

        def skipped(unused):
            return (
                jnp.zeros(query_tile.shape, jnp.float32),
                jnp.zeros(key_piece.shape, jnp.float32),
                jnp.zeros(key_piece.shape, jnp.float32),
            )

        return lax.cond(jnp.min(key_pos) <= jnp.max(query_pos), compute, skipped, 0)

    def visit_piece(query_grad, key_piece, value_piece, start):
        key_pos = lax.dynamic_slice_in_dim(every_position, start, half_rows)
        key_part = jnp.zeros(key_piece.shape, jnp.float32)
        value_part = jnp.zeros(key_piece.shape, jnp.float32)
        for query_part in range(2):
            query_term, key_term, value_term = tile_grads(
                query_part, key_piece, value_piece, key_pos
            )
            low = query_part * half_rows
            query_grad = query_grad.at[:, low : low + half_rows].add(query_term)
            key_part = key_part + key_term
            value_part = value_part + value_term
        return (query_grad, jnp.stack([key_part, value_part], 1))

    grad_start = jnp.zeros(split_shape, jnp.float32)

    def advance(step_index, loop_state):
        query_grad, key_block, value_block, grad_store = loop_state
        block_id = (rank_self - step_index) % members
        query_grad, first = visit_piece(
            query_grad, key_block[:half_rows], value_block[:half_rows], block_id * tokens
        )
        query_grad, second = visit_piece(
            query_grad,
            key_block[half_rows:],
            value_block[half_rows:],
            block_id * tokens + half_rows,
        )
        grads_here = jnp.concatenate([first, second], 0)
        grad_store = shifted(grad_store + grads_here, "ctx", 1)
        key_block, value_block = shifted((key_block, value_block), "ctx", 1)
        return (query_grad, key_block, value_block, grad_store)

    start_state = (
        grad_start,
        key_rows,
        value_rows,
        jnp.zeros((tokens, 2, kv_heads, head_dim), jnp.float32),
    )
    final_state = lax.fori_loop(0, members, advance, start_state)
    query_grad = final_state[0]
    grad_store = final_state[3]
    key_grad = grad_store[:, 0].astype(jnp.bfloat16)
    value_grad = grad_store[:, 1].astype(jnp.bfloat16)
    query_out = query_grad.reshape(layers, tokens, head_count, head_dim).astype(jnp.bfloat16)
    term = jnp.einsum("cgd,tgd->ct", key_weight, key_grad, preferred_element_type=jnp.float32)
    input_grad = lax.psum_scatter(
        term
        + jnp.einsum("cgd,tgd->ct", value_weight, value_grad, preferred_element_type=jnp.float32),
        "head",
        scatter_dimension=0,
        tiled=True,
    ).astype(jnp.bfloat16)
    return (query_out, key_grad, value_grad, input_grad)


def solution(mesh):
    placed = (
        P(None, "ctx", "head", None),
        P("ctx", "head", None),
        P("ctx", "head", None),
        P(None, "ctx", "head", None),
        P(None, "ctx", "head", None),
        P(None, "head", "ctx"),
        P("ctx"),
        P(None, "head", None),
        P(None, "head", None),
    )
    return jax.shard_map(
        on_device,
        mesh=mesh,
        in_specs=placed,
        out_specs=(
            P(None, "ctx", "head", None),
            P("ctx", "head", None),
            P("ctx", "head", None),
            P("head", "ctx"),
        ),
        check_vma=False,
    )
```

profile of v0, /device:TPU:1, one launch (start us, length us, event | category | flops | bytes accessed | tf_op | source)
XLA Modules:
  0.0 1259.8 jit_solution(13954482791168575938)
XLA Ops:
  11.8 38.7 %all-gather = s32[32,1,256]{2,1,0:T(1,128)S(1)} all-gather(s32[1,1,256]{2,1,0:T(1,128)} %bitcast.394), channel_id=1, replica_groups=mesh['ctx'=32,'head'=8] {'ctx'}, dimensions={0}, use_global_device_ids=true | all-gather | bytes 33792 | tf_op jit(solution)/shard_map/all_gather | solution.py:33
  55.4 1074.5 %while.25 = (s32[]{:T(128)}, f32[2,256,1,4,128]{4,1,3,0,2:T(8,128)}, bf16[256,1,128]{2,0,1:T(8,128)(2,1)}, bf16[256,1,128]{2,0,1:T(8,128)(2,1)}, f32[256,2,1,128...) while((s32[]{:T(128)}, ...), condition=%wide.region_13.14_spmd, body=%wide.region_2.13_spmd.sunk | while | flops 676200704 | bytes 42876300 | solution.py:114
  82.8 2.0 fusion.108
  86.8 2.0 fusion.110
  114.5 2.0 fusion.108
  118.5 2.0 fusion.110
  147.4 2.0 fusion.108
  181.1 2.0 fusion.108
  185.0 2.0 fusion.110
  211.9 4.8 collective-permute-start.2
  218.7 2.0 fusion.108
  250.6 2.0 fusion.108
  282.3 2.0 fusion.108
  315.0 2.0 fusion.108
  345.0 2.3 collective-permute-start.2
  349.3 2.0 fusion.108
  382.7 2.0 fusion.108
  390.2 4.7 collective-permute-start
  419.4 2.0 fusion.108
  451.1 2.0 fusion.108
  483.4 2.0 fusion.108
  515.5 2.0 fusion.108
  550.3 2.0 fusion.108
  559.4 4.7 collective-permute-start.1
  587.1 2.0 fusion.108
  618.8 2.0 fusion.108
  650.5 2.0 fusion.108
  683.2 2.0 fusion.108
  692.4 2.4 collective-permute-start.1
  717.7 2.0 fusion.108
  748.6 4.8 collective-permute-start.2
  755.4 2.0 fusion.108
  787.5 2.0 fusion.108
  819.2 2.0 fusion.108
  851.9 2.0 fusion.108
  885.1 2.0 fusion.108
  918.4 2.0 fusion.108
  925.9 4.8 collective-permute-start
  955.2 2.0 fusion.108
  986.9 2.0 fusion.108
  1019.3 2.0 fusion.108
  1051.3 2.0 fusion.108
  1058.8 2.6 collective-permute-start
  1086.9 2.0 fusion.108
  1096.0 4.9 collective-permute-start.1
  1123.9 2.0 fusion.108
  1131.5 4.5 fusion.71
  1139.2 111.5 %reduce-scatter.2.cloned.1.call-done = f32[1024,256]{0,1:T(8,128)} async-done(((f32[8192,256]{0,1:T(8,128)}), f32[1024,256]{0,1:T(8,128)}) %reduce-scatter.2.cloned.1.call-update) | async-done | bytes 1048592 | tf_op jit(solution)/shard_map/reduce_scatter | solution.py:121
  (2391 shorter events, 940.4 us)
Async XLA Ops:
  7.2 1243.5 %reduce-scatter.2.cloned.1.call-start = ((), (), s32[]{:S(2)}) async-start(), calls=%async_computation.1 | async-start | bytes 9437184 | tf_op jit(solution)/shard_map/reduce_scatter | solution.py:121
  56.9 31.8 %collective-permute-start = (bf16[256,1,128]{2,0,1:T(8,128)(2,1)}, bf16[256,1,128]{2,0,1:T(8,128)(2,1)}, u32[]{:S(2)}, u32[]{:S(2)}) collective-permute-start(bf16[256,1,128]{2,0,1:T(8,128)(2,1)} %copy.97), channel_id=1, source_target_pairs={{248,0},{0,8},{8,16},{16,24},{24,32},{32,40},{40,48},{48,56},{56,6... | collective-permute-start | bytes 196616 | tf_op jit(solution)/shard_map/while/body/eval_jaxpr/ppermute | solution.py:10
  58.4 30.4 %collective-permute-start.1 = (bf16[256,1,128]{2,0,1:T(8,128)(2,1)}, bf16[256,1,128]{2,0,1:T(8,128)(2,1)}, u32[]{:S(2)}, u32[]{:S(2)}) collective-permute-start(bf16[256,1,128]{2,0,1:T(8,128)(2,1)} %copy.98), channel_id=1, source_target_pairs={{248,0},{0,8},{8,16},{16,24},{24,32},{32,40},{40,48},{48,56},{56,6... | collective-permute-start | bytes 196616 | tf_op jit(solution)/shard_map/while/body/eval_jaxpr/ppermute | solution.py:10
  90.3 30.2 %collective-permute-start = (bf16[256,1,128]{2,0,1:T(8,128)(2,1)}, bf16[256,1,128]{2,0,1:T(8,128)(2,1)}, u32[]{:S(2)}, u32[]{:S(2)}) collective-permute-start(bf16[256,1,128]{2,0,1:T(8,128)(2,1)} %copy.97), channel_id=1, source_target_pairs={{248,0},{0,8},{8,16},{16,24},{24,32},{32,40},{40,48},{48,56},{56,6... | collective-permute-start | bytes 196616 | tf_op jit(solution)/shard_map/while/body/eval_jaxpr/ppermute | solution.py:10
  122.0 31.3 %collective-permute-start = (bf16[256,1,128]{2,0,1:T(8,128)(2,1)}, bf16[256,1,128]{2,0,1:T(8,128)(2,1)}, u32[]{:S(2)}, u32[]{:S(2)}) collective-permute-start(bf16[256,1,128]{2,0,1:T(8,128)(2,1)} %copy.97), channel_id=1, source_target_pairs={{248,0},{0,8},{8,16},{16,24},{24,32},{32,40},{40,48},{48,56},{56,6... | collective-permute-start | bytes 196616 | tf_op jit(solution)/shard_map/while/body/eval_jaxpr/ppermute | solution.py:10
  154.9 32.1 %collective-permute-start = (bf16[256,1,128]{2,0,1:T(8,128)(2,1)}, bf16[256,1,128]{2,0,1:T(8,128)(2,1)}, u32[]{:S(2)}, u32[]{:S(2)}) collective-permute-start(bf16[256,1,128]{2,0,1:T(8,128)(2,1)} %copy.97), channel_id=1, source_target_pairs={{248,0},{0,8},{8,16},{16,24},{24,32},{32,40},{40,48},{48,56},{56,6... | collective-permute-start | bytes 196616 | tf_op jit(solution)/shard_map/while/body/eval_jaxpr/ppermute | solution.py:10
  156.4 30.7 %collective-permute-start.1 = (bf16[256,1,128]{2,0,1:T(8,128)(2,1)}, bf16[256,1,128]{2,0,1:T(8,128)(2,1)}, u32[]{:S(2)}, u32[]{:S(2)}) collective-permute-start(bf16[256,1,128]{2,0,1:T(8,128)(2,1)} %copy.98), channel_id=1, source_target_pairs={{248,0},{0,8},{8,16},{16,24},{24,32},{32,40},{40,48},{48,56},{56,6... | collective-permute-start | bytes 196616 | tf_op jit(solution)/shard_map/while/body/eval_jaxpr/ppermute | solution.py:10
  188.6 36.1 %collective-permute-start = (bf16[256,1,128]{2,0,1:T(8,128)(2,1)}, bf16[256,1,128]{2,0,1:T(8,128)(2,1)}, u32[]{:S(2)}, u32[]{:S(2)}) collective-permute-start(bf16[256,1,128]{2,0,1:T(8,128)(2,1)} %copy.97), channel_id=1, source_target_pairs={{248,0},{0,8},{8,16},{16,24},{24,32},{32,40},{40,48},{48,56},{56,6... | collective-permute-start | bytes 196616 | tf_op jit(solution)/shard_map/while/body/eval_jaxpr/ppermute | solution.py:10
  191.3 33.4 %collective-permute-start.1 = (bf16[256,1,128]{2,0,1:T(8,128)(2,1)}, bf16[256,1,128]{2,0,1:T(8,128)(2,1)}, u32[]{:S(2)}, u32[]{:S(2)}) collective-permute-start(bf16[256,1,128]{2,0,1:T(8,128)(2,1)} %copy.98), channel_id=1, source_target_pairs={{248,0},{0,8},{8,16},{16,24},{24,32},{32,40},{40,48},{48,56},{56,6... | collective-permute-start | bytes 196616 | tf_op jit(solution)/shard_map/while/body/eval_jaxpr/ppermute | solution.py:10
  226.3 30.3 %collective-permute-start = (bf16[256,1,128]{2,0,1:T(8,128)(2,1)}, bf16[256,1,128]{2,0,1:T(8,128)(2,1)}, u32[]{:S(2)}, u32[]{:S(2)}) collective-permute-start(bf16[256,1,128]{2,0,1:T(8,128)(2,1)} %copy.97), channel_id=1, source_target_pairs={{248,0},{0,8},{8,16},{16,24},{24,32},{32,40},{40,48},{48,56},{56,6... | collective-permute-start | bytes 196616 | tf_op jit(solution)/shard_map/while/body/eval_jaxpr/ppermute | solution.py:10
  258.1 30.1 %collective-permute-start = (bf16[256,1,128]{2,0,1:T(8,128)(2,1)}, bf16[256,1,128]{2,0,1:T(8,128)(2,1)}, u32[]{:S(2)}, u32[]{:S(2)}) collective-permute-start(bf16[256,1,128]{2,0,1:T(8,128)(2,1)} %copy.97), channel_id=1, source_target_pairs={{248,0},{0,8},{8,16},{16,24},{24,32},{32,40},{40,48},{48,56},{56,6... | collective-permute-start | bytes 196616 | tf_op jit(solution)/shard_map/while/body/eval_jaxpr/ppermute | solution.py:10
  289.8 31.2 %collective-permute-start = (bf16[256,1,128]{2,0,1:T(8,128)(2,1)}, bf16[256,1,128]{2,0,1:T(8,128)(2,1)}, u32[]{:S(2)}, u32[]{:S(2)}) collective-permute-start(bf16[256,1,128]{2,0,1:T(8,128)(2,1)} %copy.97), channel_id=1, source_target_pairs={{248,0},{0,8},{8,16},{16,24},{24,32},{32,40},{40,48},{48,56},{56,6... | collective-permute-start | bytes 196616 | tf_op jit(solution)/shard_map/while/body/eval_jaxpr/ppermute | solution.py:10
  291.3 29.7 %collective-permute-start.1 = (bf16[256,1,128]{2,0,1:T(8,128)(2,1)}, bf16[256,1,128]{2,0,1:T(8,128)(2,1)}, u32[]{:S(2)}, u32[]{:S(2)}) collective-permute-start(bf16[256,1,128]{2,0,1:T(8,128)(2,1)} %copy.98), channel_id=1, source_target_pairs={{248,0},{0,8},{8,16},{16,24},{24,32},{32,40},{40,48},{48,56},{56,6... | collective-permute-start | bytes 196616 | tf_op jit(solution)/shard_map/while/body/eval_jaxpr/ppermute | solution.py:10
  322.6 32.7 %collective-permute-start = (bf16[256,1,128]{2,0,1:T(8,128)(2,1)}, bf16[256,1,128]{2,0,1:T(8,128)(2,1)}, u32[]{:S(2)}, u32[]{:S(2)}) collective-permute-start(bf16[256,1,128]{2,0,1:T(8,128)(2,1)} %copy.97), channel_id=1, source_target_pairs={{248,0},{0,8},{8,16},{16,24},{24,32},{32,40},{40,48},{48,56},{56,6... | collective-permute-start | bytes 196616 | tf_op jit(solution)/shard_map/while/body/eval_jaxpr/ppermute | solution.py:10
  324.3 31.0 %collective-permute-start.1 = (bf16[256,1,128]{2,0,1:T(8,128)(2,1)}, bf16[256,1,128]{2,0,1:T(8,128)(2,1)}, u32[]{:S(2)}, u32[]{:S(2)}) collective-permute-start(bf16[256,1,128]{2,0,1:T(8,128)(2,1)} %copy.98), channel_id=1, source_target_pairs={{248,0},{0,8},{8,16},{16,24},{24,32},{32,40},{40,48},{48,56},{56,6... | collective-permute-start | bytes 196616 | tf_op jit(solution)/shard_map/while/body/eval_jaxpr/ppermute | solution.py:10
  356.9 31.8 %collective-permute-start = (bf16[256,1,128]{2,0,1:T(8,128)(2,1)}, bf16[256,1,128]{2,0,1:T(8,128)(2,1)}, u32[]{:S(2)}, u32[]{:S(2)}) collective-permute-start(bf16[256,1,128]{2,0,1:T(8,128)(2,1)} %copy.97), channel_id=1, source_target_pairs={{248,0},{0,8},{8,16},{16,24},{24,32},{32,40},{40,48},{48,56},{56,6... | collective-permute-start | bytes 196616 | tf_op jit(solution)/shard_map/while/body/eval_jaxpr/ppermute | solution.py:10
  358.7 29.9 %collective-permute-start.1 = (bf16[256,1,128]{2,0,1:T(8,128)(2,1)}, bf16[256,1,128]{2,0,1:T(8,128)(2,1)}, u32[]{:S(2)}, u32[]{:S(2)}) collective-permute-start(bf16[256,1,128]{2,0,1:T(8,128)(2,1)} %copy.98), channel_id=1, source_target_pairs={{248,0},{0,8},{8,16},{16,24},{24,32},{32,40},{40,48},{48,56},{56,6... | collective-permute-start | bytes 196616 | tf_op jit(solution)/shard_map/while/body/eval_jaxpr/ppermute | solution.py:10
  390.2 35.2 %collective-permute-start = (bf16[256,1,128]{2,0,1:T(8,128)(2,1)}, bf16[256,1,128]{2,0,1:T(8,128)(2,1)}, u32[]{:S(2)}, u32[]{:S(2)}) collective-permute-start(bf16[256,1,128]{2,0,1:T(8,128)(2,1)} %copy.97), channel_id=1, source_target_pairs={{248,0},{0,8},{8,16},{16,24},{24,32},{32,40},{40,48},{48,56},{56,6... | collective-permute-start | bytes 196616 | tf_op jit(solution)/shard_map/while/body/eval_jaxpr/ppermute | solution.py:10
  426.9 30.1 %collective-permute-start = (bf16[256,1,128]{2,0,1:T(8,128)(2,1)}, bf16[256,1,128]{2,0,1:T(8,128)(2,1)}, u32[]{:S(2)}, u32[]{:S(2)}) collective-permute-start(bf16[256,1,128]{2,0,1:T(8,128)(2,1)} %copy.97), channel_id=1, source_target_pairs={{248,0},{0,8},{8,16},{16,24},{24,32},{32,40},{40,48},{48,56},{56,6... | collective-permute-start | bytes 196616 | tf_op jit(solution)/shard_map/while/body/eval_jaxpr/ppermute | solution.py:10
  458.6 30.7 %collective-permute-start = (bf16[256,1,128]{2,0,1:T(8,128)(2,1)}, bf16[256,1,128]{2,0,1:T(8,128)(2,1)}, u32[]{:S(2)}, u32[]{:S(2)}) collective-permute-start(bf16[256,1,128]{2,0,1:T(8,128)(2,1)} %copy.97), channel_id=1, source_target_pairs={{248,0},{0,8},{8,16},{16,24},{24,32},{32,40},{40,48},{48,56},{56,6... | collective-permute-start | bytes 196616 | tf_op jit(solution)/shard_map/while/body/eval_jaxpr/ppermute | solution.py:10
  490.9 30.6 %collective-permute-start = (bf16[256,1,128]{2,0,1:T(8,128)(2,1)}, bf16[256,1,128]{2,0,1:T(8,128)(2,1)}, u32[]{:S(2)}, u32[]{:S(2)}) collective-permute-start(bf16[256,1,128]{2,0,1:T(8,128)(2,1)} %copy.97), channel_id=1, source_target_pairs={{248,0},{0,8},{8,16},{16,24},{24,32},{32,40},{40,48},{48,56},{56,6... | collective-permute-start | bytes 196616 | tf_op jit(solution)/shard_map/while/body/eval_jaxpr/ppermute | solution.py:10
  523.0 33.2 %collective-permute-start = (bf16[256,1,128]{2,0,1:T(8,128)(2,1)}, bf16[256,1,128]{2,0,1:T(8,128)(2,1)}, u32[]{:S(2)}, u32[]{:S(2)}) collective-permute-start(bf16[256,1,128]{2,0,1:T(8,128)(2,1)} %copy.97), channel_id=1, source_target_pairs={{248,0},{0,8},{8,16},{16,24},{24,32},{32,40},{40,48},{48,56},{56,6... | collective-permute-start | bytes 196616 | tf_op jit(solution)/shard_map/while/body/eval_jaxpr/ppermute | solution.py:10
  526.1 30.1 %collective-permute-start.1 = (bf16[256,1,128]{2,0,1:T(8,128)(2,1)}, bf16[256,1,128]{2,0,1:T(8,128)(2,1)}, u32[]{:S(2)}, u32[]{:S(2)}) collective-permute-start(bf16[256,1,128]{2,0,1:T(8,128)(2,1)} %copy.98), channel_id=1, source_target_pairs={{248,0},{0,8},{8,16},{16,24},{24,32},{32,40},{40,48},{48,56},{56,6... | collective-permute-start | bytes 196616 | tf_op jit(solution)/shard_map/while/body/eval_jaxpr/ppermute | solution.py:10
  557.8 35.2 %collective-permute-start = (bf16[256,1,128]{2,0,1:T(8,128)(2,1)}, bf16[256,1,128]{2,0,1:T(8,128)(2,1)}, u32[]{:S(2)}, u32[]{:S(2)}) collective-permute-start(bf16[256,1,128]{2,0,1:T(8,128)(2,1)} %copy.97), channel_id=1, source_target_pairs={{248,0},{0,8},{8,16},{16,24},{24,32},{32,40},{40,48},{48,56},{56,6... | collective-permute-start | bytes 196616 | tf_op jit(solution)/shard_map/while/body/eval_jaxpr/ppermute | solution.py:10
  559.4 33.6 %collective-permute-start.1 = (bf16[256,1,128]{2,0,1:T(8,128)(2,1)}, bf16[256,1,128]{2,0,1:T(8,128)(2,1)}, u32[]{:S(2)}, u32[]{:S(2)}) collective-permute-start(bf16[256,1,128]{2,0,1:T(8,128)(2,1)} %copy.98), channel_id=1, source_target_pairs={{248,0},{0,8},{8,16},{16,24},{24,32},{32,40},{40,48},{48,56},{56,6... | collective-permute-start | bytes 196616 | tf_op jit(solution)/shard_map/while/body/eval_jaxpr/ppermute | solution.py:10
  594.6 30.2 %collective-permute-start = (bf16[256,1,128]{2,0,1:T(8,128)(2,1)}, bf16[256,1,128]{2,0,1:T(8,128)(2,1)}, u32[]{:S(2)}, u32[]{:S(2)}) collective-permute-start(bf16[256,1,128]{2,0,1:T(8,128)(2,1)} %copy.97), channel_id=1, source_target_pairs={{248,0},{0,8},{8,16},{16,24},{24,32},{32,40},{40,48},{48,56},{56,6... | collective-permute-start | bytes 196616 | tf_op jit(solution)/shard_map/while/body/eval_jaxpr/ppermute | solution.py:10
  626.3 30.2 %collective-permute-start = (bf16[256,1,128]{2,0,1:T(8,128)(2,1)}, bf16[256,1,128]{2,0,1:T(8,128)(2,1)}, u32[]{:S(2)}, u32[]{:S(2)}) collective-permute-start(bf16[256,1,128]{2,0,1:T(8,128)(2,1)} %copy.97), channel_id=1, source_target_pairs={{248,0},{0,8},{8,16},{16,24},{24,32},{32,40},{40,48},{48,56},{56,6... | collective-permute-start | bytes 196616 | tf_op jit(solution)/shard_map/while/body/eval_jaxpr/ppermute | solution.py:10
  658.0 31.2 %collective-permute-start = (bf16[256,1,128]{2,0,1:T(8,128)(2,1)}, bf16[256,1,128]{2,0,1:T(8,128)(2,1)}, u32[]{:S(2)}, u32[]{:S(2)}) collective-permute-start(bf16[256,1,128]{2,0,1:T(8,128)(2,1)} %copy.97), channel_id=1, source_target_pairs={{248,0},{0,8},{8,16},{16,24},{24,32},{32,40},{40,48},{48,56},{56,6... | collective-permute-start | bytes 196616 | tf_op jit(solution)/shard_map/while/body/eval_jaxpr/ppermute | solution.py:10
  690.8 32.9 %collective-permute-start = (bf16[256,1,128]{2,0,1:T(8,128)(2,1)}, bf16[256,1,128]{2,0,1:T(8,128)(2,1)}, u32[]{:S(2)}, u32[]{:S(2)}) collective-permute-start(bf16[256,1,128]{2,0,1:T(8,128)(2,1)} %copy.97), channel_id=1, source_target_pairs={{248,0},{0,8},{8,16},{16,24},{24,32},{32,40},{40,48},{48,56},{56,6... | collective-permute-start | bytes 196616 | tf_op jit(solution)/shard_map/while/body/eval_jaxpr/ppermute | solution.py:10
  692.4 31.2 %collective-permute-start.1 = (bf16[256,1,128]{2,0,1:T(8,128)(2,1)}, bf16[256,1,128]{2,0,1:T(8,128)(2,1)}, u32[]{:S(2)}, u32[]{:S(2)}) collective-permute-start(bf16[256,1,128]{2,0,1:T(8,128)(2,1)} %copy.98), channel_id=1, source_target_pairs={{248,0},{0,8},{8,16},{16,24},{24,32},{32,40},{40,48},{48,56},{56,6... | collective-permute-start | bytes 196616 | tf_op jit(solution)/shard_map/while/body/eval_jaxpr/ppermute | solution.py:10
  725.2 36.2 %collective-permute-start = (bf16[256,1,128]{2,0,1:T(8,128)(2,1)}, bf16[256,1,128]{2,0,1:T(8,128)(2,1)}, u32[]{:S(2)}, u32[]{:S(2)}) collective-permute-start(bf16[256,1,128]{2,0,1:T(8,128)(2,1)} %copy.97), channel_id=1, source_target_pairs={{248,0},{0,8},{8,16},{16,24},{24,32},{32,40},{40,48},{48,56},{56,6... | collective-permute-start | bytes 196616 | tf_op jit(solution)/shard_map/while/body/eval_jaxpr/ppermute | solution.py:10
  728.0 33.4 %collective-permute-start.1 = (bf16[256,1,128]{2,0,1:T(8,128)(2,1)}, bf16[256,1,128]{2,0,1:T(8,128)(2,1)}, u32[]{:S(2)}, u32[]{:S(2)}) collective-permute-start(bf16[256,1,128]{2,0,1:T(8,128)(2,1)} %copy.98), channel_id=1, source_target_pairs={{248,0},{0,8},{8,16},{16,24},{24,32},{32,40},{40,48},{48,56},{56,6... | collective-permute-start | bytes 196616 | tf_op jit(solution)/shard_map/while/body/eval_jaxpr/ppermute | solution.py:10
  762.9 30.5 %collective-permute-start = (bf16[256,1,128]{2,0,1:T(8,128)(2,1)}, bf16[256,1,128]{2,0,1:T(8,128)(2,1)}, u32[]{:S(2)}, u32[]{:S(2)}) collective-permute-start(bf16[256,1,128]{2,0,1:T(8,128)(2,1)} %copy.97), channel_id=1, source_target_pairs={{248,0},{0,8},{8,16},{16,24},{24,32},{32,40},{40,48},{48,56},{56,6... | collective-permute-start | bytes 196616 | tf_op jit(solution)/shard_map/while/body/eval_jaxpr/ppermute | solution.py:10
  795.0 30.2 %collective-permute-start = (bf16[256,1,128]{2,0,1:T(8,128)(2,1)}, bf16[256,1,128]{2,0,1:T(8,128)(2,1)}, u32[]{:S(2)}, u32[]{:S(2)}) collective-permute-start(bf16[256,1,128]{2,0,1:T(8,128)(2,1)} %copy.97), channel_id=1, source_target_pairs={{248,0},{0,8},{8,16},{16,24},{24,32},{32,40},{40,48},{48,56},{56,6... | collective-permute-start | bytes 196616 | tf_op jit(solution)/shard_map/while/body/eval_jaxpr/ppermute | solution.py:10
  826.8 31.1 %collective-permute-start = (bf16[256,1,128]{2,0,1:T(8,128)(2,1)}, bf16[256,1,128]{2,0,1:T(8,128)(2,1)}, u32[]{:S(2)}, u32[]{:S(2)}) collective-permute-start(bf16[256,1,128]{2,0,1:T(8,128)(2,1)} %copy.97), channel_id=1, source_target_pairs={{248,0},{0,8},{8,16},{16,24},{24,32},{32,40},{40,48},{48,56},{56,6... | collective-permute-start | bytes 196616 | tf_op jit(solution)/shard_map/while/body/eval_jaxpr/ppermute | solution.py:10
  828.3 29.6 %collective-permute-start.1 = (bf16[256,1,128]{2,0,1:T(8,128)(2,1)}, bf16[256,1,128]{2,0,1:T(8,128)(2,1)}, u32[]{:S(2)}, u32[]{:S(2)}) collective-permute-start(bf16[256,1,128]{2,0,1:T(8,128)(2,1)} %copy.98), channel_id=1, source_target_pairs={{248,0},{0,8},{8,16},{16,24},{24,32},{32,40},{40,48},{48,56},{56,6... | collective-permute-start | bytes 196616 | tf_op jit(solution)/shard_map/while/body/eval_jaxpr/ppermute | solution.py:10
  859.4 31.6 %collective-permute-start = (bf16[256,1,128]{2,0,1:T(8,128)(2,1)}, bf16[256,1,128]{2,0,1:T(8,128)(2,1)}, u32[]{:S(2)}, u32[]{:S(2)}) collective-permute-start(bf16[256,1,128]{2,0,1:T(8,128)(2,1)} %copy.97), channel_id=1, source_target_pairs={{248,0},{0,8},{8,16},{16,24},{24,32},{32,40},{40,48},{48,56},{56,6... | collective-permute-start | bytes 196616 | tf_op jit(solution)/shard_map/while/body/eval_jaxpr/ppermute | solution.py:10
  860.9 30.1 %collective-permute-start.1 = (bf16[256,1,128]{2,0,1:T(8,128)(2,1)}, bf16[256,1,128]{2,0,1:T(8,128)(2,1)}, u32[]{:S(2)}, u32[]{:S(2)}) collective-permute-start(bf16[256,1,128]{2,0,1:T(8,128)(2,1)} %copy.98), channel_id=1, source_target_pairs={{248,0},{0,8},{8,16},{16,24},{24,32},{32,40},{40,48},{48,56},{56,6... | collective-permute-start | bytes 196616 | tf_op jit(solution)/shard_map/while/body/eval_jaxpr/ppermute | solution.py:10
  892.6 31.8 %collective-permute-start = (bf16[256,1,128]{2,0,1:T(8,128)(2,1)}, bf16[256,1,128]{2,0,1:T(8,128)(2,1)}, u32[]{:S(2)}, u32[]{:S(2)}) collective-permute-start(bf16[256,1,128]{2,0,1:T(8,128)(2,1)} %copy.97), channel_id=1, source_target_pairs={{248,0},{0,8},{8,16},{16,24},{24,32},{32,40},{40,48},{48,56},{56,6... | collective-permute-start | bytes 196616 | tf_op jit(solution)/shard_map/while/body/eval_jaxpr/ppermute | solution.py:10
  894.5 29.8 %collective-permute-start.1 = (bf16[256,1,128]{2,0,1:T(8,128)(2,1)}, bf16[256,1,128]{2,0,1:T(8,128)(2,1)}, u32[]{:S(2)}, u32[]{:S(2)}) collective-permute-start(bf16[256,1,128]{2,0,1:T(8,128)(2,1)} %copy.98), channel_id=1, source_target_pairs={{248,0},{0,8},{8,16},{16,24},{24,32},{32,40},{40,48},{48,56},{56,6... | collective-permute-start | bytes 196616 | tf_op jit(solution)/shard_map/while/body/eval_jaxpr/ppermute | solution.py:10
  925.9 35.3 %collective-permute-start = (bf16[256,1,128]{2,0,1:T(8,128)(2,1)}, bf16[256,1,128]{2,0,1:T(8,128)(2,1)}, u32[]{:S(2)}, u32[]{:S(2)}) collective-permute-start(bf16[256,1,128]{2,0,1:T(8,128)(2,1)} %copy.97), channel_id=1, source_target_pairs={{248,0},{0,8},{8,16},{16,24},{24,32},{32,40},{40,48},{48,56},{56,6... | collective-permute-start | bytes 196616 | tf_op jit(solution)/shard_map/while/body/eval_jaxpr/ppermute | solution.py:10
  962.8 30.1 %collective-permute-start = (bf16[256,1,128]{2,0,1:T(8,128)(2,1)}, bf16[256,1,128]{2,0,1:T(8,128)(2,1)}, u32[]{:S(2)}, u32[]{:S(2)}) collective-permute-start(bf16[256,1,128]{2,0,1:T(8,128)(2,1)} %copy.97), channel_id=1, source_target_pairs={{248,0},{0,8},{8,16},{16,24},{24,32},{32,40},{40,48},{48,56},{56,6... | collective-permute-start | bytes 196616 | tf_op jit(solution)/shard_map/while/body/eval_jaxpr/ppermute | solution.py:10
  994.4 30.8 %collective-permute-start = (bf16[256,1,128]{2,0,1:T(8,128)(2,1)}, bf16[256,1,128]{2,0,1:T(8,128)(2,1)}, u32[]{:S(2)}, u32[]{:S(2)}) collective-permute-start(bf16[256,1,128]{2,0,1:T(8,128)(2,1)} %copy.97), channel_id=1, source_target_pairs={{248,0},{0,8},{8,16},{16,24},{24,32},{32,40},{40,48},{48,56},{56,6... | collective-permute-start | bytes 196616 | tf_op jit(solution)/shard_map/while/body/eval_jaxpr/ppermute | solution.py:10
  1026.8 30.5 %collective-permute-start = (bf16[256,1,128]{2,0,1:T(8,128)(2,1)}, bf16[256,1,128]{2,0,1:T(8,128)(2,1)}, u32[]{:S(2)}, u32[]{:S(2)}) collective-permute-start(bf16[256,1,128]{2,0,1:T(8,128)(2,1)} %copy.97), channel_id=1, source_target_pairs={{248,0},{0,8},{8,16},{16,24},{24,32},{32,40},{40,48},{48,56},{56,6... | collective-permute-start | bytes 196616 | tf_op jit(solution)/shard_map/while/body/eval_jaxpr/ppermute | solution.py:10
  1058.8 34.1 %collective-permute-start = (bf16[256,1,128]{2,0,1:T(8,128)(2,1)}, bf16[256,1,128]{2,0,1:T(8,128)(2,1)}, u32[]{:S(2)}, u32[]{:S(2)}) collective-permute-start(bf16[256,1,128]{2,0,1:T(8,128)(2,1)} %copy.97), channel_id=1, source_target_pairs={{248,0},{0,8},{8,16},{16,24},{24,32},{32,40},{40,48},{48,56},{56,6... | collective-permute-start | bytes 196616 | tf_op jit(solution)/shard_map/while/body/eval_jaxpr/ppermute | solution.py:10
  1062.9 30.0 %collective-permute-start.1 = (bf16[256,1,128]{2,0,1:T(8,128)(2,1)}, bf16[256,1,128]{2,0,1:T(8,128)(2,1)}, u32[]{:S(2)}, u32[]{:S(2)}) collective-permute-start(bf16[256,1,128]{2,0,1:T(8,128)(2,1)} %copy.98), channel_id=1, source_target_pairs={{248,0},{0,8},{8,16},{16,24},{24,32},{32,40},{40,48},{48,56},{56,6... | collective-permute-start | bytes 196616 | tf_op jit(solution)/shard_map/while/body/eval_jaxpr/ppermute | solution.py:10
  1094.4 35.4 %collective-permute-start = (bf16[256,1,128]{2,0,1:T(8,128)(2,1)}, bf16[256,1,128]{2,0,1:T(8,128)(2,1)}, u32[]{:S(2)}, u32[]{:S(2)}) collective-permute-start(bf16[256,1,128]{2,0,1:T(8,128)(2,1)} %copy.97), channel_id=1, source_target_pairs={{248,0},{0,8},{8,16},{16,24},{24,32},{32,40},{40,48},{48,56},{56,6... | collective-permute-start | bytes 196616 | tf_op jit(solution)/shard_map/while/body/eval_jaxpr/ppermute | solution.py:10
  1096.0 33.8 %collective-permute-start.1 = (bf16[256,1,128]{2,0,1:T(8,128)(2,1)}, bf16[256,1,128]{2,0,1:T(8,128)(2,1)}, u32[]{:S(2)}, u32[]{:S(2)}) collective-permute-start(bf16[256,1,128]{2,0,1:T(8,128)(2,1)} %copy.98), channel_id=1, source_target_pairs={{248,0},{0,8},{8,16},{16,24},{24,32},{32,40},{40,48},{48,56},{56,6... | collective-permute-start | bytes 196616 | tf_op jit(solution)/shard_map/while/body/eval_jaxpr/ppermute | solution.py:10
  (569 other events, 3822.7 us)
Sparse Core Ops, SparseCore 0:
  1136.2 114.4 reduce-scatter.1
where the time goes:
time: 1280 us; the launch traced here: 1260 us
  other arithmetic  526 us (41%)
  local copies, waits for them, and re-layouts  247 us (19%)
  loops' own time  173 us (14%)
  waiting for transfers between devices  112 us (9%)
  matrix products  82.9 us (6%)
  starting transfers between devices  66.4 us (5%)
  blocking collectives  38.7 us (3%)
  between operations  14.1 us (1%)
    scatter-add x128, other arithmetic, visit_piece(): query_grad = query_grad.at[:, low:low + half_rows].add(query_term)  254 us
    another operation x1, loops' own time, on_device(): final_state = lax.fori_loop(0, members, advance, start_state)  169 us
    another operation x128, other arithmetic, visit_piece(): return (query_grad, jnp.stack([key_part, value_part], 1))  152 us
    reduce_scatter x1, waiting for transfers between devices, on_device(): lax.psum_scatter(term + jnp.einsum('cgd,tgd->ct', value_weight, value_gra...  111 us
    another operation x253, local copies, waits for them, and re-layouts  97.5 us
    while x1024, local copies, waits for them, and re-layouts  71.5 us
    ppermute x96, starting transfers between devices, shifted(): return lax.ppermute(block, axis, route)  66.3 us
    le x65, other arithmetic, compute(): allowed = key_pos[None, :] <= query_pos[:, None]  45.8 us
  transfers between devices with their start and end apart: 97, of which 1 were waited for; matrix products, arithmetic and copies ran while one was open for 57% of the time, Pallas kernels for 0%

commit v1 on v0

v1 whole, which is shorter than its diff:
```python
import functools
import math

import jax
import jax.numpy as jnp
from jax import lax
from jax.experimental import pallas as pl
from jax.experimental.pallas import tpu as pltpu
from jax.sharding import Mesh, PartitionSpec as P

F32, BF16 = jnp.float32, jnp.bfloat16
HD = 128
RUN = 128
BLK = 2 * RUN
PAY = BLK + 16
QPK = 4
SCALING = HD**-0.5
NT = (((1,), (1,)), ((), ()))
NN = (((1,), (0,)), ((), ()))
CTX = ("xl", "z", "core")
HEAD = ("xh", "y")
COST_A = 0.05


def visits_kernel(*refs, nb, m, q_in, q_raw, kv_in, kv_raw):
    refs = list(refs)

    def take(count):
        head = refs[:count]
        del refs[:count]
        return head

    qd_hbm, aux_hbm, kv_hbm = take(nb), take(nb), take(m)
    dqi_hbm, acci_hbm = take(len(q_in)), take(2 if kv_in else 0)
    dq_hbm = take(nb)
    dkv_hbm = take(2 if kv_raw else m)
    qds, auxs, kvs, dqs, dqo, dkvo, ks, vs, kts, acck, accv = take(11)
    order, krun, qrun_s, sem, osem = take(5)
    nr = 2 * m
    layers = qds.shape[2]
    rows = qds.shape[3] // 2
    c1 = SCALING * math.log2(math.e)

    copies = [(kv_hbm[j], kvs.at[j]) for j in range(m)]
    for b in range(nb):
        copies.append((aux_hbm[b], auxs.at[b]))
        copies.append((qd_hbm[b], qds.at[b]))
    if kv_in:
        copies.append((acci_hbm[0], acck))
        copies.append((acci_hbm[1], accv))
    for i, b in enumerate(q_in):
        copies.append((dqi_hbm[i], dqs.at[b]))
    copies = [pltpu.make_async_copy(s, d, sem.at[i]) for i, (s, d) in enumerate(copies)]
    for c in copies:
        c.start()
    for b in range(nb):
        if b not in q_in:
            dqs[b] = jnp.zeros(dqs.shape[1:], F32)
    if not kv_in:
        acck[...] = jnp.zeros_like(acck)
        accv[...] = jnp.zeros_like(accv)
    for c in copies:
        c.wait()

    for j in range(m):
        for i in range(2):
            tag = kvs[j, BLK + 8 * i : BLK + 8 * i + 8, 0:HD].astype(F32)
            krun[2 * j + i] = jnp.max(tag).astype(jnp.int32)
    for b in range(nb):
        for i in range(2):
            qrun_s[2 * b + i] = jnp.max(auxs[b, 4 + i : 5 + i, 0:HD]).astype(jnp.int32)
    for i in range(nr):
        mine = krun[i]
        rank = jnp.int32(0)
        for j in range(nr):
            if j != i:
                rank = rank + (krun[j] < mine).astype(jnp.int32)
        order[rank] = i

    def arrange(i, carry):
        s = order[i]
        at = pl.multiple_of((s % 2) * RUN, RUN)
        to = pl.multiple_of(i * RUN, RUN)
        k = kvs[s // 2, pl.ds(at, RUN), 0:HD]
        ks[pl.ds(to, RUN), :] = k
        vs[pl.ds(to, RUN), :] = kvs[s // 2, pl.ds(at, RUN), HD : 2 * HD]
        kts[i // 2, i % 2] = k.T
        return carry

    lax.fori_loop(0, nr, arrange, 0)

    def query_half(qi, carry):
        b = qi // 2
        half = qi % 2
        qrun = qrun_s[qi]
        reach = jnp.int32(0)
        for j in range(nr):
            reach = reach + (krun[j] <= qrun).astype(jnp.int32)
        off = pl.multiple_of(half * rows, rows)

        def visit(p, masked):
            at = pl.multiple_of(p * BLK, BLK)
            kp = ks[pl.ds(at, BLK), :]
            vp = vs[pl.ds(at, BLK), :]
            kt = jnp.concatenate([kts[p, 0], kts[p, 1]], axis=1)
            if masked:
                first = krun[order[2 * p]] * RUN
                second = krun[order[2 * p + 1]] * RUN
                ii = lax.broadcasted_iota(jnp.int32, (BLK, 1), 0)
                kpos = jnp.where(ii < RUN, ii + first, ii - RUN + second)
                jj = lax.broadcasted_iota(jnp.int32, (1, rows), 1)
                seen = kpos <= jj // QPK + qrun * RUN
            dk = acck[p]
            dv = accv[p]
            for l in range(layers):
                q = qds[b, 0, l, pl.ds(off, rows), :]
                do = qds[b, 1, l, pl.ds(off, rows), :]
                lse = auxs[b, l : l + 1, pl.ds(off, rows)]
                delta = auxs[b, 2 + l : 3 + l, pl.ds(off, rows)]
                scores = lax.dot_general(kp, q, NT, preferred_element_type=F32)
                probs = jnp.exp2(scores * c1 - lse)
                if masked:
                    probs = jnp.where(seen, probs, 0.0)
                dprobs = lax.dot_general(vp, do, NT, preferred_element_type=F32)
                dscore = (probs * (dprobs - delta)).astype(BF16)
                dv = dv + lax.dot_general(probs.astype(BF16), do, NN, preferred_element_type=F32)
                dk = dk + lax.dot_general(dscore, q, NN, preferred_element_type=F32)
                dqs[b, half, l] += lax.dot_general(kt, dscore, NN, preferred_element_type=F32)
            acck[p] = dk
            accv[p] = dv

        def step(p, inner):
            full = krun[order[2 * p + 1]] < qrun

            @pl.when(full)
            def _():
                visit(p, False)

            @pl.when(jnp.logical_not(full))
            def _():
                visit(p, True)

            return inner

        lax.fori_loop(0, (reach + 1) // 2, step, 0)
        return carry

    lax.fori_loop(0, 2 * nb, query_half, 0)

    outs = []
    if kv_raw:
        outs += [(acck, dkv_hbm[0]), (accv, dkv_hbm[1])]
    else:

        def settle(i, carry):
            s = order[i]
            at = pl.multiple_of((i % 2) * RUN, RUN)
            to = pl.multiple_of((s % 2) * RUN, RUN)
            k_sum = acck[i // 2, pl.ds(at, RUN), :] * SCALING
            v_sum = accv[i // 2, pl.ds(at, RUN), :]
            dkvo[s // 2, pl.ds(to, RUN), 0:HD] = k_sum.astype(BF16)
            dkvo[s // 2, pl.ds(to, RUN), HD : 2 * HD] = v_sum.astype(BF16)
            return carry

        lax.fori_loop(0, nr, settle, 0)
        outs += [(dkvo.at[j], dkv_hbm[j]) for j in range(m)]
    for b in range(nb):
        if b in q_raw:
            outs.append((dqs.at[b], dq_hbm[b]))
    outs = [pltpu.make_async_copy(s, d, osem.at[i]) for i, (s, d) in enumerate(outs)]
    for c in outs:
        c.start()
    late = []
    for b in range(nb):
        if b not in q_raw:
            for half in range(2):
                for l in range(layers):
                    dqo[b, l, half * rows : (half + 1) * rows, :] = (dqs[b, half, l] * SCALING).T.astype(BF16)
            c = pltpu.make_async_copy(dqo.at[b], dq_hbm[b], osem.at[len(outs) + len(late)])
            c.start()
            late.append(c)
    for c in outs + late:
        c.wait()


def visits(name, queries, keys, q_before=None, q_raw=(), kv_before=None, kv_raw=False, cost=1.0):
    nb, m = len(queries), len(keys)
    q_before = q_before or {}
    q_in = sorted(q_before)
    _, layers, rows, _ = queries[0][0].shape
    q_shape = (layers, rows, HD)
    aux_shape = queries[0][1].shape
    operands = (
        [q[0] for q in queries]
        + [q[1] for q in queries]
        + list(keys)
        + [q_before[b] for b in q_in]
        + list(kv_before or ())
    )
    units = nb * m * 2
    any_spec = pl.BlockSpec(memory_space=pl.ANY)
    raw_shape = (2, layers, HD, rows // 2)
    acc_shape = (m, BLK, HD)
    out_shape = [
        jax.ShapeDtypeStruct(raw_shape, F32) if b in q_raw else jax.ShapeDtypeStruct(q_shape, BF16)
        for b in range(nb)
    ]
    if kv_raw:
        out_shape += [jax.ShapeDtypeStruct(acc_shape, F32)] * 2
    else:
        out_shape += [jax.ShapeDtypeStruct((BLK, 2 * HD), BF16)] * m
    outs = pl.pallas_call(
        functools.partial(
            visits_kernel,
            nb=nb,
            m=m,
            q_in=tuple(q_in),
            q_raw=tuple(q_raw),
            kv_in=kv_before is not None,
            kv_raw=kv_raw,
        ),
        out_shape=out_shape,
        in_specs=[any_spec] * len(operands),
        out_specs=[any_spec] * len(out_shape),
        scratch_shapes=[
            pltpu.VMEM((nb, 2) + q_shape, BF16),
            pltpu.VMEM((nb,) + aux_shape, F32),
            pltpu.VMEM((m, PAY, 2 * HD), BF16),
            pltpu.VMEM((nb,) + raw_shape, F32),
            pltpu.VMEM((nb, layers, rows, HD), BF16),
            pltpu.VMEM((m, BLK, 2 * HD), BF16),
            pltpu.VMEM((2 * m * RUN, HD), BF16),
            pltpu.VMEM((2 * m * RUN, HD), BF16),
            pltpu.VMEM((m, 2, HD, RUN), BF16),
            pltpu.VMEM(acc_shape, F32),
            pltpu.VMEM(acc_shape, F32),
            pltpu.SMEM((2 * m,), jnp.int32),
            pltpu.SMEM((2 * m,), jnp.int32),
            pltpu.SMEM((2 * nb,), jnp.int32),
            pltpu.SemaphoreType.DMA((len(operands),)),
            pltpu.SemaphoreType.DMA((len(out_shape),)),
        ],
        compiler_params=pltpu.CompilerParams(vmem_limit_bytes=60 * 2**20),
        cost_estimate=pl.CostEstimate(
            flops=int(cost * units * 1024 * RUN * HD * 20),
            bytes_accessed=int(cost * nb * 3 * 2**20),
            transcendentals=int(cost * units * 1024 * RUN),
        ),
        name=name,
    )(*operands)
    return outs[:nb], outs[nb:]


def tail_kernel(first_ref, second_ref, grads_ref, out_ref):
    total = jnp.zeros(out_ref.shape, F32)
    for g in range(first_ref.shape[0]):
        w = jnp.concatenate([first_ref[g], second_ref[g]], axis=1)
        total = total + lax.dot_general(w, grads_ref[g], NT, preferred_element_type=F32)
    out_ref[...] = total.astype(out_ref.dtype)


def moved(value, axis, distance):
    size = lax.axis_size(axis)
    return lax.ppermute(value, axis, [(i, (i + distance) % size) for i in range(size)])


def on_device(
    queries, key_rows, value_rows, attn_out, out_grad, log_norm, positions, key_weight, value_weight
):
    layers, tokens, per_group, head_dim = queries.shape
    rows = tokens * per_group
    zn = lax.axis_size("z")
    runs = positions.reshape(2, RUN)[:, 0] // RUN
    tags = jnp.broadcast_to(runs.astype(BF16)[:, None, None], (2, 8, 2 * head_dim)).reshape(16, 2 * head_dim)
    block = jnp.concatenate([key_rows[:, 0], value_rows[:, 0]], axis=1)
    block = jnp.concatenate([block, tags], axis=0)
    keys = {0: block}
    keys[1], keys[zn - 1] = moved(block, "z", 1), moved(block, "z", -1)
    for t in (2, 3):
        keys[t], keys[zn - t] = moved(keys[t - 1], "z", 1), moved(keys[zn - t + 1], "z", -1)
    keys[4] = moved(keys[3], "z", 1)

    q = queries.reshape(layers, rows, head_dim)
    do = out_grad.reshape(layers, rows, head_dim)
    deltas = jnp.sum(out_grad.astype(F32) * attn_out.astype(F32), -1).reshape(layers, rows)
    lse = jnp.transpose(log_norm, (0, 2, 1)).reshape(layers, rows) * math.log2(math.e)
    run_rows = jnp.broadcast_to(runs.astype(F32)[:, None], (2, rows))
    aux = jnp.concatenate([lse, deltas, run_rows, jnp.zeros((2, rows), F32)], axis=0)
    own = (jnp.stack([q, do]), aux)
    over = tuple(moved(a, "core", 1) for a in own)
    both = moved(jnp.concatenate([aux, over[1]], axis=0), "xl", 1)
    far = (moved(own[0], "xl", 1), both[:8])

    near_t = (0, 1, 2, zn - 2, zn - 1)
    far_t = (3, 4, zn - 3)
    near_k = [keys[t] for t in near_t]
    far_k = [keys[t] for t in far_t]
    dq_a, acc_a = visits("near_near", [own, over], near_k, q_raw=(0, 1), kv_raw=True, cost=COST_A)
    held, _ = lax.optimization_barrier((far[0], acc_a[0]))
    far_over = (moved(held, "core", 1), both[8:])
    dq_b, dkv_b = visits(
        "all_far",
        [own, over, far, far_over],
        far_k,
        q_before={0: dq_a[0], 1: dq_a[1]},
        q_raw=(2, 3),
    )
    core = lax.axis_index("core")
    features = key_weight.shape[0]
    kw, vw, _ = lax.optimization_barrier((key_weight[:, 0], value_weight[:, 0], dkv_b[0]))
    mine = lax.all_to_all(jnp.where(core == 0, kw, vw), HEAD, 0, 0, tiled=True)
    mine = mine.reshape(8, features // 8, head_dim)
    other = moved(mine, "core", 1)

    dq_c, dkv_c = visits(
        "far_near", [far, far_over], near_k, q_before={0: dq_b[2], 1: dq_b[3]}, kv_before=acc_a
    )
    far_total = sum(moved(part, "z", -t).astype(F32) for t, part in zip(far_t, dkv_b))
    dkv_c, far_total = lax.optimization_barrier((dkv_c, far_total))
    total = far_total + dkv_c[0].astype(F32)
    for t, part in zip(near_t[1:], dkv_c[1:]):
        total = total + moved(part, "z", -t).astype(F32)
    grads = total.astype(BF16)

    got = moved(dq_b[1], "core", 1)
    far_sum = dq_c[0].astype(F32) + moved(dq_c[1], "core", 1).astype(F32)
    got_far = moved(far_sum.astype(BF16), "xl", 1)
    query_grad = (dq_b[0].astype(F32) + got.astype(F32) + got_far.astype(F32)).astype(BF16)
    query_grad = query_grad.reshape(queries.shape)

    swapped = jnp.concatenate([grads[:, head_dim:], grads[:, :head_dim]], axis=1)
    turned = jnp.where(core == 0, grads, swapped)
    every = lax.all_to_all(
        jnp.broadcast_to(turned[None], (8,) + grads.shape), HEAD, 0, 0, tiled=True
    )
    steps = 4
    tile = features // 8 // steps
    weight_spec = pl.BlockSpec((8, tile, head_dim), lambda i: (0, i, 0))
    input_grad = pl.pallas_call(
        tail_kernel,
        grid=(steps,),
        out_shape=jax.ShapeDtypeStruct((features // 8, tokens), BF16),
        in_specs=[
            weight_spec,
            weight_spec,
            pl.BlockSpec((8, tokens, 2 * head_dim), lambda i: (0, 0, 0)),
        ],
        out_specs=pl.BlockSpec((tile, tokens), lambda i: (i, 0)),
        compiler_params=pltpu.CompilerParams(vmem_limit_bytes=60 * 2**20),
        cost_estimate=pl.CostEstimate(
            flops=2 * features * tokens * 2 * head_dim, bytes_accessed=6 * 2**20, transcendentals=0
        ),
        name="input_grad",
    )(mine, other, every)
    return (
        query_grad,
        grads[:, None, :head_dim],
        grads[:, None, head_dim:],
        input_grad,
    )


def solution(mesh):
    fine = Mesh(mesh.devices.reshape(2, 8, 2, 2, 4), CTX + HEAD)
    placed = (
        P(None, CTX, HEAD, None),
        P(CTX, HEAD, None),
        P(CTX, HEAD, None),
        P(None, CTX, HEAD, None),
        P(None, CTX, HEAD, None),
        P(None, HEAD, CTX),
        P(CTX),
        P(None, HEAD, None),
        P(None, HEAD, None),
    )
    return jax.shard_map(
        on_device,
        mesh=fine,
        in_specs=placed,
        out_specs=(
            P(None, CTX, HEAD, None),
            P(CTX, HEAD, None),
            P(CTX, HEAD, None),
            P(HEAD, CTX),
        ),
        check_vma=False,
    )
```

time: 1280 us -> 163 us (0.13); the launches traced: 1260 us -> 161 us
  other arithmetic: 526 us -> 10.8 us
  local copies, waits for them, and re-layouts: 247 us -> 7.81 us
  loops' own time: 173 us -> 0 us
  matrix products: 82.9 us -> 0 us
  waiting for transfers between devices: 112 us -> 45.7 us
  Pallas kernels: 0 us -> 53.9 us
  blocking collectives: 38.7 us -> 0 us
  starting transfers between devices: 66.4 us -> 41.8 us
  between operations: 14.1 us -> 0.96 us
    scatter-add x128 -> x0, other arithmetic: 254 us -> none  [visit_piece(): query_grad = query_grad.at[:, low:low + half_rows].add(query_term)]
    another operation x129 -> x0, loops' own time: 173 us -> none  [the longest x1 169 us: on_device(): final_state = lax.fori_loop(0, members, advance, start_state)]
    another operation x128 -> x1, other arithmetic: 152 us -> 1.38 us  [on_device(): own = (jnp.stack([q, do]), aux)]
    reduce_scatter x1 -> x0, waiting for transfers between devices: 111 us -> none  [on_device(): lax.psum_scatter(term + jnp.einsum('cgd,tgd->ct', value_weight, value_gra...]
    another operation x253 -> x0, local copies, waits for them, and re-layouts: 97.5 us -> none
    dot_general x327 -> x0, matrix products: 82.9 us -> none  [the longest x65 16.6 us: compute(): jnp.einsum('lrgqd,kgd->lgqrk', query_tile, key_piece, preferred_element_t...]
    while x1024 -> x0, local copies, waits for them, and re-layouts: 71.5 us -> none
    slice x96 -> x3, local copies, waits for them, and re-layouts: 67.1 us -> 1.46 us  [the longest x1 0.69 us: on_device(): grads[:, None, head_dim:]]
  transfers between devices with their start and end apart: 97 -> 25, of which waited for: 1 -> 9; matrix products, arithmetic and copies ran while one was open for 57% -> 6% of each run, Pallas kernels for 0% -> 18%
where the time goes in v1:
time: 163 us; the launch traced here: 161 us
  Pallas kernels  53.9 us (33%)
  waiting for transfers between devices  45.7 us (28%)
  starting transfers between devices  41.8 us (26%)
  other arithmetic  10.8 us (7%)
  local copies, waits for them, and re-layouts  7.81 us (5%)
    pallas_call x3, Pallas kernels, visits(): pl.pallas_call(functools.partial(visits_kernel, nb=nb, m=m, q_in=tuple(q_...  48.9 us
    ppermute x23, waiting for transfers between devices, moved(): lax.ppermute(value, axis, [(i, (i + distance) % size) for i in range(size)])  41.3 us
    ppermute x23, starting transfers between devices, moved(): lax.ppermute(value, axis, [(i, (i + distance) % size) for i in range(size)])  30.3 us
    all_to_all x1, starting transfers between devices, on_device(): mine = lax.all_to_all(jnp.where(core == 0, kw, vw), HEAD, 0, 0, tiled=True)  6.48 us
    pallas_call x1, Pallas kernels, on_device(): pl.pallas_call(tail_kernel, grid=(steps,), out_shape=jax.ShapeDtypeStruct...  5.08 us
    all_to_all x1, starting transfers between devices, on_device(): lax.all_to_all(jnp.broadcast_to(turned[None], (8,) + grads.shape), HEAD,...  5 us
    all_to_all x1, waiting for transfers between devices, on_device(): mine = lax.all_to_all(jnp.where(core == 0, kw, vw), HEAD, 0, 0, tiled=True)  4.38 us
    unnamed x46, local copies, waits for them, and re-layouts  3.74 us
  transfers between devices with their start and end apart: 25, of which 9 were waited for; matrix products, arithmetic and copies ran while one was open for 6% of the time, Pallas kernels for 18%

profile of v1, /device:TPU:1, one launch (start us, length us, event | category | flops | bytes accessed | tf_op | source)
XLA Modules:
  0.0 161.0 jit_solution(14899196589001618347)
XLA Ops:
  0.7 1.4 pad_maximum_fusion.refs_0_
  2.1 3.3 %collective-permute-start = (bf16[2,2,1024,128]{3,2,1,0:T(8,128)(2,1)S(1)}, bf16[2,2,1024,128]{3,2,1,0:T(8,128)(2,1)S(1)}, u32[]{:S(2)}, u32[]{:S(2)}) collective-permute-start(bf16[2,2,1024,128]{3,2,1,0:T(8,128)(2,1)S(1)} %pad_maximum_fusion.refs_0_), channel_id=1, source_target_pairs={{0,8},{8,0},{1,9},{9,1},{2,10},{10,2},{3,11},{11,3},{4,12},{12,4},... | collective-permute-start | bytes 3145736 | tf_op jit(solution)/shard_map/ppermute | solution.py:264
  5.9 1.2 collective-permute-start.3
  7.1 4.0 %collective-permute-start.5 = (bf16[272,256]{1,0:T(8,128)(2,1)S(1)}, bf16[272,256]{1,0:T(8,128)(2,1)}, u32[]{:S(2)}, u32[]{:S(2)}) collective-permute-start(bf16[272,256]{1,0:T(8,128)(2,1)S(1)} %maximum_maximum_fusion.refs_4_), channel_id=1, source_target_pairs={{0,112},{16,0},{32,16},{48,32},{64,48},{80,64},{96,80},{112,96},{1... | collective-permute-start | bytes 417800 | tf_op jit(solution)/shard_map/ppermute | solution.py:264
  11.1 0.6 multiply_reduce_fusion
  11.8 0.1 copy.15
  11.9 0.2 mul.18
  12.1 0.2 reshape.56
  12.3 0.8 convert_reduce_fusion
  13.1 1.8 %collective-permute-done.3.refs_5_ = bf16[272,256]{1,0:T(8,128)(2,1)} collective-permute-done((bf16[272,256]{1,0:T(8,128)(2,1)S(1)}, bf16[272,256]{1,0:T(8,128)(2,1)}, u32[]{:S(2)}, u32[]{:S(2)}) %collective-permute-start.3) | collective-permute-done | bytes 139296 | tf_op jit(solution)/shard_map/ppermute | solution.py:264
  14.9 2.7 %collective-permute-start.6 = (bf16[272,256]{1,0:T(8,128)(2,1)}, bf16[272,256]{1,0:T(8,128)(2,1)S(1)}, u32[]{:S(2)}, u32[]{:S(2)}) collective-permute-start(bf16[272,256]{1,0:T(8,128)(2,1)} %collective-permute-done.5.refs_8_), channel_id=1, source_target_pairs={{0,112},{16,0},{32,16},{48,32},{64,48},{80,64},{96,80},{112,96},{1... | collective-permute-start | bytes 417800 | tf_op jit(solution)/shard_map/ppermute | solution.py:264
  17.7 1.5 collective-permute-start.2
  19.2 0.9 collective-permute-done.2.refs_3_.refs_5_
  20.0 0.6 collective-permute-done.4.refs_6_
  20.7 0.6 copy-done.8
  21.3 1.0 copy-done.5
  22.3 14.8 %near_near.1 = (f32[2,2,128,512]{3,2,1,0:T(8,128)}, f32[2,2,128,512]{3,2,1,0:T(8,128)}, f32[5,256,128]{2,1,0:T(8,128)}, f32[5,256,128]{2,1,0:T(8,128)}) custom-call(bf16[2,2,1024,128]{3,2,1,0:T(8,128)(2,1)} %copy-done.1, bf16[2,2,1024,128]{3,2,1,0:T(8,128)(2,1)} %copy-done.5, f32[8,1024]{1,0:T(8,128)} %copy-done.10, f32[8,1024]{1,0:T(8,128)} %copy-done.11, ...), custom_call_target="tpu_custom_call" | custom-call | flops 335544320 | bytes 314572 | tf_op jit(solution)/shard_map/near_near/pallas_call | solution.py:212
  37.1 1.9 %collective-permute-start.7 = (bf16[2,2,1024,128]{3,2,1,0:T(8,128)(2,1)}, bf16[2,2,1024,128]{3,2,1,0:T(8,128)(2,1)S(1)}, u32[]{:S(2)}, u32[]{:S(2)}) collective-permute-start(bf16[2,2,1024,128]{3,2,1,0:T(8,128)(2,1)} %collective-permute-done.1.refs_2_.refs_0_), channel_id=1, source_target_pairs={{0,8},{8,0},{1,9},{9,1},{2,10},{10,2},{3,11},{11,3},{4,12},{12,4},... | collective-permute-start | bytes 3145736 | tf_op jit(solution)/shard_map/ppermute | solution.py:264
  39.0 0.8 concatenate.19
  39.8 2.8 %collective-permute-start.11 = (bf16[272,256]{1,0:T(8,128)(2,1)}, bf16[272,256]{1,0:T(8,128)(2,1)S(1)}, u32[]{:S(2)}, u32[]{:S(2)}) collective-permute-start(bf16[272,256]{1,0:T(8,128)(2,1)} %copy-done.9), channel_id=1, source_target_pairs={{0,112},{16,0},{32,16},{48,32},{64,48},{80,64},{96,80},{112,96},{1... | collective-permute-start | bytes 417800 | tf_op jit(solution)/shard_map/ppermute | solution.py:264
  42.5 3.2 %collective-permute-done.9.refs_8_ = bf16[272,256]{1,0:T(8,128)(2,1)S(1)} collective-permute-done((bf16[272,256]{1,0:T(8,128)(2,1)}, bf16[272,256]{1,0:T(8,128)(2,1)S(1)}, u32[]{:S(2)}, u32[]{:S(2)}) %collective-permute-start.9) | collective-permute-done | bytes 139296 | tf_op jit(solution)/shard_map/ppermute | solution.py:264
  45.8 0.7 fusion.2
  46.5 5.0 %collective-permute-done.10.refs_9_ = bf16[272,256]{1,0:T(8,128)(2,1)S(1)} collective-permute-done((bf16[272,256]{1,0:T(8,128)(2,1)S(1)}, bf16[272,256]{1,0:T(8,128)(2,1)S(1)}, u32[]{:S(2)}, u32[]{:S(2)}) %collective-permute-start.10) | collective-permute-done | bytes 139296 | tf_op jit(solution)/shard_map/ppermute | solution.py:264
  51.4 0.6 copy-done.18
  52.1 0.4 copy-done.15
  52.5 19.4 %all_far.1 = (bf16[2,1024,128]{2,1,0:T(8,128)(2,1)}, bf16[2,1024,128]{2,1,0:T(8,128)(2,1)}, f32[2,2,128,512]{3,2,1,0:T(8,128)}, f32[2,2,128,512]{3,2,1,0:T(8,128...) custom-call(bf16[2,2,1024,128]{3,2,1,0:T(8,128)(2,1)} %copy-done.1, ...), custom_call_target="tpu_custom_call" | custom-call | flops 8053063680 | bytes 12582912 | tf_op jit(solution)/shard_map/all_far/pallas_call | solution.py:212
  71.9 3.2 %broadcast_select_fusion = bf16[8192,128]{1,0:T(8,128)(2,1)} fusion(bf16[8192,128]{1,0:T(8,128)(2,1)S(1)} %bitcast.15, bf16[8192,128]{1,0:T(8,128)(2,1)} %bitcast.16, pred[]{:T(512)S(6)} %eq.4), kind=kLoop, calls=%fused_computation | loop fusion | flops 1048576 | bytes 6291457 | tf_op jit(solution)/shard_map/jit(_where)/select_n | solution.py:311
  75.1 6.5 %all-to-all-start = ((bf16[8,1024,128]{2,1,0:T(8,128)(2,1)}), bf16[8,1024,128]{2,1,0:T(8,128)(2,1)S(1)}, u32[]{:S(2)}, u32[]{:S(2)}) async-start(bf16[8,1024,128]{2,1,0:T(8,128)(2,1)} %bitcast.11), calls=%async_computation | async-start | bytes 4194304 | tf_op jit(solution)/shard_map/all_to_all | solution.py:311
  81.6 0.4 collective-permute-start.15
  82.0 3.1 %collective-permute-start.16 = (bf16[256,256]{1,0:T(8,128)(2,1)S(1)}, bf16[256,256]{1,0:T(8,128)(2,1)S(1)}, u32[]{:S(2)}, u32[]{:S(2)}) collective-permute-start(bf16[256,256]{1,0:T(8,128)(2,1)S(1)} %copy-done.20), channel_id=1, source_target_pairs={{0,64},{16,80},{32,96},{48,112},{64,0},{80,16},{96,32},{112,48},{1... | collective-permute-start | bytes 393224 | tf_op jit(solution)/shard_map/ppermute | solution.py:264
  85.1 3.2 %collective-permute-start.17 = (bf16[256,256]{1,0:T(8,128)(2,1)S(1)}, bf16[256,256]{1,0:T(8,128)(2,1)S(1)}, u32[]{:S(2)}, u32[]{:S(2)}) collective-permute-start(bf16[256,256]{1,0:T(8,128)(2,1)S(1)} %copy-done.19), channel_id=1, source_target_pairs={{0,48},{16,64},{32,80},{48,96},{64,112},{80,0},{96,16},{112,32},{1... | collective-permute-start | bytes 393224 | tf_op jit(solution)/shard_map/ppermute | solution.py:264
  88.3 14.7 %far_near.1 = (bf16[2,1024,128]{2,1,0:T(8,128)(2,1)}, bf16[2,1024,128]{2,1,0:T(8,128)(2,1)}, bf16[256,256]{1,0:T(8,128)(2,1)}, bf16[256,256]{1,0:T(8,128)(2,1)},...) custom-call(bf16[2,2,1024,128]{3,2,1,0:T(8,128)(2,1)} %collective-permute-done.1.refs_2_.refs_0_, ...), custom_call_target="tpu_custom_call" | custom-call | flops 6710886400 | bytes 6291456 | tf_op jit(solution)/shard_map/far_near/pallas_call | solution.py:212
  102.9 4.4 %all-to-all-done.first_ref = bf16[8,1024,128]{2,1,0:T(8,128)(2,1)S(1)} async-done(((bf16[8,1024,128]{2,1,0:T(8,128)(2,1)}), bf16[8,1024,128]{2,1,0:T(8,128)(2,1)S(1)}, u32[]{:S(2)}, u32[]{:S(2)}) %all-to-all-start) | async-done | bytes 2097184 | tf_op jit(solution)/shard_map/all_to_all | solution.py:311
  107.5 0.2 collective-permute-start.19
  107.6 2.3 %collective-permute-start.20 = (bf16[256,256]{1,0:T(8,128)(2,1)}, bf16[256,256]{1,0:T(8,128)(2,1)S(1)}, u32[]{:S(2)}, u32[]{:S(2)}) collective-permute-start(bf16[256,256]{1,0:T(8,128)(2,1)} %get-tuple-element.54), channel_id=1, source_target_pairs={{0,32},{16,48},{32,64},{48,80},{64,96},{80,112},{96,0},{112,16},{1... | collective-permute-start | bytes 393224 | tf_op jit(solution)/shard_map/ppermute | solution.py:264
  109.9 1.4 collective-permute-start.21
  111.3 3.8 %collective-permute-done.18 = bf16[256,256]{1,0:T(8,128)(2,1)S(1)} collective-permute-done((bf16[256,256]{1,0:T(8,128)(2,1)}, bf16[256,256]{1,0:T(8,128)(2,1)S(1)}, u32[]{:S(2)}, u32[]{:S(2)}) %collective-permute-start.18) | collective-permute-done | bytes 131104 | tf_op jit(solution)/shard_map/ppermute | solution.py:264
  115.1 2.3 %collective-permute-start.13 = (bf16[2,1024,128]{2,1,0:T(8,128)(2,1)}, bf16[2,1024,128]{2,1,0:T(8,128)(2,1)}, u32[]{:S(2)}, u32[]{:S(2)}) collective-permute-start(bf16[2,1024,128]{2,1,0:T(8,128)(2,1)} %get-tuple-element.41), channel_id=1, source_target_pairs={{0,8},{8,0},{1,9},{9,1},{2,10},{10,2},{3,11},{11,3},{4,12},{12,4},... | collective-permute-start | bytes 1572872 | tf_op jit(solution)/shard_map/ppermute | solution.py:264
  117.3 5.3 %collective-permute-done.21 = bf16[256,256]{1,0:T(8,128)(2,1)S(1)} collective-permute-done((bf16[256,256]{1,0:T(8,128)(2,1)}, bf16[256,256]{1,0:T(8,128)(2,1)S(1)}, u32[]{:S(2)}, u32[]{:S(2)}) %collective-permute-start.21) | collective-permute-done | bytes 131104 | tf_op jit(solution)/shard_map/ppermute | solution.py:264
  122.6 1.0 add_convert_fusion.2
  123.6 0.7 fusion.1
  124.4 1.1 broadcast_in_dim.41
  125.4 5.0 %all-to-all-start.1 = ((bf16[8,256,256]{2,1,0:T(8,128)(2,1)}), bf16[8,256,256]{2,1,0:T(8,128)(2,1)S(1)}, u32[]{:S(2)}, u32[]{:S(2)}) async-start(bf16[8,256,256]{2,1,0:T(8,128)(2,1)} %broadcast_in_dim.41), calls=%async_computation.1 | async-start | bytes 2097152 | tf_op jit(solution)/shard_map/all_to_all | solution.py:333
  130.4 1.3 add_convert_fusion.1
  131.9 20.8 %collective-permute-done.14 = bf16[2,1024,128]{2,1,0:T(8,128)(2,1)S(1)} collective-permute-done((bf16[2,1024,128]{2,1,0:T(8,128)(2,1)S(1)}, bf16[2,1024,128]{2,1,0:T(8,128)(2,1)S(1)}, u32[]{:S(2)}, u32[]{:S(2)}) %collective-permute-start.14) | collective-permute-done | bytes 524320 | tf_op jit(solution)/shard_map/ppermute | solution.py:264
  152.7 2.2 %add_convert_fusion = bf16[2,1024,128]{2,1,0:T(8,128)(2,1)} fusion(bf16[2,1024,128]{2,1,0:T(8,128)(2,1)S(1)} %collective-permute-done.14, bf16[2,1024,128]{2,1,0:T(8,128)(2,1)} %collective-permute-done.12, bf16[2,1024,128]{2,1,0:T(8,128)(2,1)} %get-tuple-element.35), kind=kLoop, calls=%fused_computation.2 | loop fusion | flops 1572864 | bytes 2097152 | tf_op jit(solution)/shard_map/convert_element_type | solution.py:328
  154.9 1.0 copy-done.2
  155.9 5.1 %input_grad.1 = bf16[1024,256]{1,0:T(8,128)(2,1)} custom-call(bf16[8,1024,128]{2,1,0:T(8,128)(2,1)} %copy-done, bf16[8,1024,128]{2,1,0:T(8,128)(2,1)} %collective-permute-done.22.second_ref, bf16[8,256,256]{2,1,0:T(8,128)(2,1)} %copy-done.2), custom_call_target="tpu_custom_call" | custom-call | flops 1073741824 | bytes 6291456 | tf_op jit(solution)/shard_map/input_grad/pallas_call | solution.py:339
  (78 shorter events, 1.0 us)
Async XLA Ops:
  0.6 10.5 %copy-start.4 = (bf16[2,256,4,128]{3,2,1,0:T(4,128)(2,1)S(1)}, bf16[2,256,4,128]{3,2,1,0:T(4,128)(2,1)}, u32[]{:S(2)}) copy-start(bf16[2,256,4,128]{3,2,1,0:T(4,128)(2,1)} %param.13) | copy-start | bytes 1572868
  0.6 4.8 %copy-start.22 = (s32[256]{0:T(256)S(1)}, s32[256]{0:T(256)}, u32[]{:S(2)}) copy-start(s32[256]{0:T(256)} %param.15) | copy-start | bytes 3076
  0.7 5.1 %copy-start.13 = (bf16[256,1,128]{2,0,1:T(8,128)(2,1)S(1)}, bf16[256,1,128]{2,0,1:T(8,128)(2,1)}, u32[]{:S(2)}) copy-start(bf16[256,1,128]{2,0,1:T(8,128)(2,1)} %param.10) | copy-start | bytes 196612
  0.7 5.1 %copy-start.12 = (bf16[256,1,128]{2,0,1:T(8,128)(2,1)S(1)}, bf16[256,1,128]{2,0,1:T(8,128)(2,1)}, u32[]{:S(2)}) copy-start(bf16[256,1,128]{2,0,1:T(8,128)(2,1)} %param.11) | copy-start | bytes 196612
  0.7 10.4 %copy-start.14 = (f32[2,4,256]{2,1,0:T(4,128)S(1)}, f32[2,4,256]{2,1,0:T(4,128)}, u32[]{:S(2)}) copy-start(f32[2,4,256]{2,1,0:T(4,128)} %param.14) | copy-start | bytes 24580
  0.7 10.4 %copy-start.7 = (bf16[2,256,4,128]{3,2,1,0:T(4,128)(2,1)S(1)}, bf16[2,256,4,128]{3,2,1,0:T(4,128)(2,1)}, u32[]{:S(2)}) copy-start(bf16[2,256,4,128]{3,2,1,0:T(4,128)(2,1)} %param.12) | copy-start | bytes 1572868
  2.1 18.5 %copy-start.1 = (bf16[2,2,1024,128]{3,2,1,0:T(8,128)(2,1)}, bf16[2,2,1024,128]{3,2,1,0:T(8,128)(2,1)S(1)}, u32[]{:S(2)}) copy-start(bf16[2,2,1024,128]{3,2,1,0:T(8,128)(2,1)S(1)} %pad_maximum_fusion.refs_0_) | copy-start | bytes 3145732
  2.1 18.5 %collective-permute-start = (bf16[2,2,1024,128]{3,2,1,0:T(8,128)(2,1)S(1)}, bf16[2,2,1024,128]{3,2,1,0:T(8,128)(2,1)S(1)}, u32[]{:S(2)}, u32[]{:S(2)}) collective-permute-start(bf16[2,2,1024,128]{3,2,1,0:T(8,128)(2,1)S(1)} %pad_maximum_fusion.refs_0_), channel_id=1, source_target_pairs={{0,8},{8,0},{1,9},{9,1},{2,10},{10,2},{3,11},{11,3},{4,12},{12,4},... | collective-permute-start | bytes 3145736 | tf_op jit(solution)/shard_map/ppermute | solution.py:264
  5.4 31.7 %collective-permute-start.1 = (bf16[2,2,1024,128]{3,2,1,0:T(8,128)(2,1)S(1)}, bf16[2,2,1024,128]{3,2,1,0:T(8,128)(2,1)}, u32[]{:S(2)}, u32[]{:S(2)}) collective-permute-start(bf16[2,2,1024,128]{3,2,1,0:T(8,128)(2,1)S(1)} %pad_maximum_fusion.refs_0_), channel_id=1, source_target_pairs={{0,128},{128,0},{1,129},{129,1},{2,130},{130,2},{3,131},{131,3},{4... | collective-permute-start | bytes 3145736 | tf_op jit(solution)/shard_map/ppermute | solution.py:264
  5.8 14.8 %copy-start.6 = (bf16[272,256]{1,0:T(8,128)(2,1)}, bf16[272,256]{1,0:T(8,128)(2,1)S(1)}, u32[]{:S(2)}) copy-start(bf16[272,256]{1,0:T(8,128)(2,1)S(1)} %maximum_maximum_fusion.refs_4_) | copy-start | bytes 417796
  5.9 9.0 %collective-permute-start.3 = (bf16[272,256]{1,0:T(8,128)(2,1)S(1)}, bf16[272,256]{1,0:T(8,128)(2,1)}, u32[]{:S(2)}, u32[]{:S(2)}) collective-permute-start(bf16[272,256]{1,0:T(8,128)(2,1)S(1)} %maximum_maximum_fusion.refs_4_), channel_id=1, source_target_pairs={{0,16},{16,32},{32,48},{48,64},{64,80},{80,96},{96,112},{112,0},{1... | collective-permute-start | bytes 417800 | tf_op jit(solution)/shard_map/ppermute | solution.py:264
  7.1 7.8 %collective-permute-start.5 = (bf16[272,256]{1,0:T(8,128)(2,1)S(1)}, bf16[272,256]{1,0:T(8,128)(2,1)}, u32[]{:S(2)}, u32[]{:S(2)}) collective-permute-start(bf16[272,256]{1,0:T(8,128)(2,1)S(1)} %maximum_maximum_fusion.refs_4_), channel_id=1, source_target_pairs={{0,112},{16,0},{32,16},{48,32},{64,48},{80,64},{96,80},{112,96},{1... | collective-permute-start | bytes 417800 | tf_op jit(solution)/shard_map/ppermute | solution.py:264
  14.9 5.7 %collective-permute-start.4 = (bf16[272,256]{1,0:T(8,128)(2,1)}, bf16[272,256]{1,0:T(8,128)(2,1)S(1)}, u32[]{:S(2)}, u32[]{:S(2)}) collective-permute-start(bf16[272,256]{1,0:T(8,128)(2,1)} %collective-permute-done.3.refs_5_), channel_id=1, source_target_pairs={{0,16},{16,32},{32,48},{48,64},{64,80},{80,96},{96,112},{112,0},{1... | collective-permute-start | bytes 417800 | tf_op jit(solution)/shard_map/ppermute | solution.py:264
  14.9 5.7 %collective-permute-start.6 = (bf16[272,256]{1,0:T(8,128)(2,1)}, bf16[272,256]{1,0:T(8,128)(2,1)S(1)}, u32[]{:S(2)}, u32[]{:S(2)}) collective-permute-start(bf16[272,256]{1,0:T(8,128)(2,1)} %collective-permute-done.5.refs_8_), channel_id=1, source_target_pairs={{0,112},{16,0},{32,16},{48,32},{64,48},{80,64},{96,80},{112,96},{1... | collective-permute-start | bytes 417800 | tf_op jit(solution)/shard_map/ppermute | solution.py:264
  17.6 3.0 %copy-start.10 = (f32[8,1024]{1,0:T(8,128)}, f32[8,1024]{1,0:T(8,128)S(1)}, u32[]{:S(2)}) copy-start(f32[8,1024]{1,0:T(8,128)S(1)} %pad_maximum_fusion.1.refs_2_.refs_4_) | copy-start | bytes 98308
  17.7 2.4 %collective-permute-start.2 = (f32[8,1024]{1,0:T(8,128)S(1)}, f32[8,1024]{1,0:T(8,128)S(1)}, u32[]{:S(2)}, u32[]{:S(2)}) collective-permute-start(f32[8,1024]{1,0:T(8,128)S(1)} %pad_maximum_fusion.1.refs_2_.refs_4_), channel_id=1, source_target_pairs={{0,8},{8,0},{1,9},{9,1},{2,10},{10,2},{3,11},{11,3},{4,12},{12,4},... | collective-permute-start | bytes 98312 | tf_op jit(solution)/shard_map/ppermute | solution.py:264
  20.0 0.6 copy-start.11
  20.6 0.7 copy-start.8
  20.6 0.7 copy-start.9
  21.3 1.0 copy-start.5
  37.1 14.3 %collective-permute-start.7 = (bf16[2,2,1024,128]{3,2,1,0:T(8,128)(2,1)}, bf16[2,2,1024,128]{3,2,1,0:T(8,128)(2,1)S(1)}, u32[]{:S(2)}, u32[]{:S(2)}) collective-permute-start(bf16[2,2,1024,128]{3,2,1,0:T(8,128)(2,1)} %collective-permute-done.1.refs_2_.refs_0_), channel_id=1, source_target_pairs={{0,8},{8,0},{1,9},{9,1},{2,10},{10,2},{3,11},{11,3},{4,12},{12,4},... | collective-permute-start | bytes 3145736 | tf_op jit(solution)/shard_map/ppermute | solution.py:264
  39.0 6.8 %collective-permute-start.9 = (bf16[272,256]{1,0:T(8,128)(2,1)}, bf16[272,256]{1,0:T(8,128)(2,1)S(1)}, u32[]{:S(2)}, u32[]{:S(2)}) collective-permute-start(bf16[272,256]{1,0:T(8,128)(2,1)} %copy-done.8), channel_id=1, source_target_pairs={{0,16},{16,32},{32,48},{48,64},{64,80},{80,96},{96,112},{112,0},{1... | collective-permute-start | bytes 417800 | tf_op jit(solution)/shard_map/ppermute | solution.py:264
  39.8 6.0 %collective-permute-start.8 = (f32[16,1024]{1,0:T(8,128)S(1)}, f32[16,1024]{1,0:T(8,128)S(1)}, u32[]{:S(2)}, u32[]{:S(2)}) collective-permute-start(f32[16,1024]{1,0:T(8,128)S(1)} %concatenate.19), channel_id=1, source_target_pairs={{0,128},{128,0},{1,129},{129,1},{2,130},{130,2},{3,131},{131,3},{4... | collective-permute-start | bytes 196616 | tf_op jit(solution)/shard_map/ppermute | solution.py:264
  39.8 6.7 %collective-permute-start.11 = (bf16[272,256]{1,0:T(8,128)(2,1)}, bf16[272,256]{1,0:T(8,128)(2,1)S(1)}, u32[]{:S(2)}, u32[]{:S(2)}) collective-permute-start(bf16[272,256]{1,0:T(8,128)(2,1)} %copy-done.9), channel_id=1, source_target_pairs={{0,112},{16,0},{32,16},{48,32},{64,48},{80,64},{96,80},{112,96},{1... | collective-permute-start | bytes 417800 | tf_op jit(solution)/shard_map/ppermute | solution.py:264
  45.8 5.6 %copy-start.16 = (bf16[272,256]{1,0:T(8,128)(2,1)}, bf16[272,256]{1,0:T(8,128)(2,1)S(1)}, u32[]{:S(2)}) copy-start(bf16[272,256]{1,0:T(8,128)(2,1)S(1)} %collective-permute-done.9.refs_8_) | copy-start | bytes 417796
  45.8 5.6 %collective-permute-start.10 = (bf16[272,256]{1,0:T(8,128)(2,1)S(1)}, bf16[272,256]{1,0:T(8,128)(2,1)S(1)}, u32[]{:S(2)}, u32[]{:S(2)}) collective-permute-start(bf16[272,256]{1,0:T(8,128)(2,1)S(1)} %collective-permute-done.9.refs_8_), channel_id=1, source_target_pairs={{0,16},{16,32},{32,48},{48,64},{64,80},{80,96},{96,112},{112,0},{1... | collective-permute-start | bytes 417800 | tf_op jit(solution)/shard_map/ppermute | solution.py:264
  46.5 5.0 %copy-start.17 = (bf16[272,256]{1,0:T(8,128)(2,1)}, bf16[272,256]{1,0:T(8,128)(2,1)S(1)}, u32[]{:S(2)}) copy-start(bf16[272,256]{1,0:T(8,128)(2,1)S(1)} %collective-permute-done.11.refs_10_) | copy-start | bytes 417796
  51.4 0.7 copy-start.18
  51.4 1.0 copy-start.15
  52.5 19.4 %copy-start.3 = (bf16[8192,1,128]{2,0,1:T(8,128)(2,1)S(1)}, bf16[8192,1,128]{2,0,1:T(8,128)(2,1)}, u32[]{:S(2)}) copy-start(bf16[8192,1,128]{2,0,1:T(8,128)(2,1)} %param.16) | copy-start | bytes 6291460
  75.1 6.5 %copy-start.21 = (bf16[256,256]{1,0:T(8,128)(2,1)S(1)}, bf16[256,256]{1,0:T(8,128)(2,1)}, u32[]{:S(2)}) copy-start(bf16[256,256]{1,0:T(8,128)(2,1)} %get-tuple-element.47) | copy-start | bytes 393220
  75.1 6.9 %copy-start.20 = (bf16[256,256]{1,0:T(8,128)(2,1)S(1)}, bf16[256,256]{1,0:T(8,128)(2,1)}, u32[]{:S(2)}) copy-start(bf16[256,256]{1,0:T(8,128)(2,1)} %get-tuple-element.48) | copy-start | bytes 393220
  75.1 10.0 %copy-start.19 = (bf16[256,256]{1,0:T(8,128)(2,1)S(1)}, bf16[256,256]{1,0:T(8,128)(2,1)}, u32[]{:S(2)}) copy-start(bf16[256,256]{1,0:T(8,128)(2,1)} %get-tuple-element.49) | copy-start | bytes 393220
  75.1 32.2 %all-to-all-start = ((bf16[8,1024,128]{2,1,0:T(8,128)(2,1)}), bf16[8,1024,128]{2,1,0:T(8,128)(2,1)S(1)}, u32[]{:S(2)}, u32[]{:S(2)}) async-start(bf16[8,1024,128]{2,1,0:T(8,128)(2,1)} %bitcast.11), calls=%async_computation | async-start | bytes 4194304 | tf_op jit(solution)/shard_map/all_to_all | solution.py:311
  81.6 25.7 %collective-permute-start.15 = (bf16[256,256]{1,0:T(8,128)(2,1)S(1)}, bf16[256,256]{1,0:T(8,128)(2,1)S(1)}, u32[]{:S(2)}, u32[]{:S(2)}) collective-permute-start(bf16[256,256]{1,0:T(8,128)(2,1)S(1)} %copy-done.21), channel_id=1, source_target_pairs={{0,80},{16,96},{32,112},{48,0},{64,16},{80,32},{96,48},{112,64},{1... | collective-permute-start | bytes 393224 | tf_op jit(solution)/shard_map/ppermute | solution.py:264
  82.0 25.3 %collective-permute-start.16 = (bf16[256,256]{1,0:T(8,128)(2,1)S(1)}, bf16[256,256]{1,0:T(8,128)(2,1)S(1)}, u32[]{:S(2)}, u32[]{:S(2)}) collective-permute-start(bf16[256,256]{1,0:T(8,128)(2,1)S(1)} %copy-done.20), channel_id=1, source_target_pairs={{0,64},{16,80},{32,96},{48,112},{64,0},{80,16},{96,32},{112,48},{1... | collective-permute-start | bytes 393224 | tf_op jit(solution)/shard_map/ppermute | solution.py:264
  85.1 22.2 %collective-permute-start.17 = (bf16[256,256]{1,0:T(8,128)(2,1)S(1)}, bf16[256,256]{1,0:T(8,128)(2,1)S(1)}, u32[]{:S(2)}, u32[]{:S(2)}) collective-permute-start(bf16[256,256]{1,0:T(8,128)(2,1)S(1)} %copy-done.19), channel_id=1, source_target_pairs={{0,48},{16,64},{32,80},{48,96},{64,112},{80,0},{96,16},{112,32},{1... | collective-permute-start | bytes 393224 | tf_op jit(solution)/shard_map/ppermute | solution.py:264
  107.3 18.1 %copy-start = (bf16[8,1024,128]{2,1,0:T(8,128)(2,1)}, bf16[8,1024,128]{2,1,0:T(8,128)(2,1)S(1)}, u32[]{:S(2)}) copy-start(bf16[8,1024,128]{2,1,0:T(8,128)(2,1)S(1)} %all-to-all-done.first_ref) | copy-start | bytes 6291460
  107.3 47.6 %collective-permute-start.22 = (bf16[8,1024,128]{2,1,0:T(8,128)(2,1)S(1)}, bf16[8,1024,128]{2,1,0:T(8,128)(2,1)}, u32[]{:S(2)}, u32[]{:S(2)}) collective-permute-start(bf16[8,1024,128]{2,1,0:T(8,128)(2,1)S(1)} %all-to-all-done.first_ref), channel_id=1, source_target_pairs={{0,8},{8,0},{1,9},{9,1},{2,10},{10,2},{3,11},{11,3},{4,12},{12,4},... | collective-permute-start | bytes 6291464 | tf_op jit(solution)/shard_map/ppermute | solution.py:264
  107.4 7.7 %collective-permute-start.18 = (bf16[256,256]{1,0:T(8,128)(2,1)}, bf16[256,256]{1,0:T(8,128)(2,1)S(1)}, u32[]{:S(2)}, u32[]{:S(2)}) collective-permute-start(bf16[256,256]{1,0:T(8,128)(2,1)} %get-tuple-element.52), channel_id=1, source_target_pairs={{0,112},{16,0},{32,16},{48,32},{64,48},{80,64},{96,80},{112,96},{1... | collective-permute-start | bytes 393224 | tf_op jit(solution)/shard_map/ppermute | solution.py:264
  107.5 9.9 %collective-permute-start.19 = (bf16[256,256]{1,0:T(8,128)(2,1)}, bf16[256,256]{1,0:T(8,128)(2,1)S(1)}, u32[]{:S(2)}, u32[]{:S(2)}) collective-permute-start(bf16[256,256]{1,0:T(8,128)(2,1)} %get-tuple-element.53), channel_id=1, source_target_pairs={{0,96},{16,112},{32,0},{48,16},{64,32},{80,48},{96,64},{112,80},{1... | collective-permute-start | bytes 393224 | tf_op jit(solution)/shard_map/ppermute | solution.py:264
  107.6 9.7 %collective-permute-start.20 = (bf16[256,256]{1,0:T(8,128)(2,1)}, bf16[256,256]{1,0:T(8,128)(2,1)S(1)}, u32[]{:S(2)}, u32[]{:S(2)}) collective-permute-start(bf16[256,256]{1,0:T(8,128)(2,1)} %get-tuple-element.54), channel_id=1, source_target_pairs={{0,32},{16,48},{32,64},{48,80},{64,96},{80,112},{96,0},{112,16},{1... | collective-permute-start | bytes 393224 | tf_op jit(solution)/shard_map/ppermute | solution.py:264
  109.9 12.7 %collective-permute-start.21 = (bf16[256,256]{1,0:T(8,128)(2,1)}, bf16[256,256]{1,0:T(8,128)(2,1)S(1)}, u32[]{:S(2)}, u32[]{:S(2)}) collective-permute-start(bf16[256,256]{1,0:T(8,128)(2,1)} %get-tuple-element.55), channel_id=1, source_target_pairs={{0,16},{16,32},{32,48},{48,64},{64,80},{80,96},{96,112},{112,0},{1... | collective-permute-start | bytes 393224 | tf_op jit(solution)/shard_map/ppermute | solution.py:264
  115.1 15.4 %collective-permute-start.13 = (bf16[2,1024,128]{2,1,0:T(8,128)(2,1)}, bf16[2,1024,128]{2,1,0:T(8,128)(2,1)}, u32[]{:S(2)}, u32[]{:S(2)}) collective-permute-start(bf16[2,1024,128]{2,1,0:T(8,128)(2,1)} %get-tuple-element.41), channel_id=1, source_target_pairs={{0,8},{8,0},{1,9},{9,1},{2,10},{10,2},{3,11},{11,3},{4,12},{12,4},... | collective-permute-start | bytes 1572872 | tf_op jit(solution)/shard_map/ppermute | solution.py:264
  117.3 14.6 %collective-permute-start.12 = (bf16[2,1024,128]{2,1,0:T(8,128)(2,1)}, bf16[2,1024,128]{2,1,0:T(8,128)(2,1)}, u32[]{:S(2)}, u32[]{:S(2)}) collective-permute-start(bf16[2,1024,128]{2,1,0:T(8,128)(2,1)} %get-tuple-element.36), channel_id=1, source_target_pairs={{0,8},{8,0},{1,9},{9,1},{2,10},{10,2},{3,11},{11,3},{4,12},{12,4},... | collective-permute-start | bytes 1572872 | tf_op jit(solution)/shard_map/ppermute | solution.py:264
  125.4 29.5 %all-to-all-start.1 = ((bf16[8,256,256]{2,1,0:T(8,128)(2,1)}), bf16[8,256,256]{2,1,0:T(8,128)(2,1)S(1)}, u32[]{:S(2)}, u32[]{:S(2)}) async-start(bf16[8,256,256]{2,1,0:T(8,128)(2,1)} %broadcast_in_dim.41), calls=%async_computation.1 | async-start | bytes 2097152 | tf_op jit(solution)/shard_map/all_to_all | solution.py:333
  131.8 20.9 %collective-permute-start.14 = (bf16[2,1024,128]{2,1,0:T(8,128)(2,1)S(1)}, bf16[2,1024,128]{2,1,0:T(8,128)(2,1)S(1)}, u32[]{:S(2)}, u32[]{:S(2)}) collective-permute-start(bf16[2,1024,128]{2,1,0:T(8,128)(2,1)S(1)} %add_convert_fusion.1), channel_id=1, source_target_pairs={{0,128},{128,0},{1,129},{129,1},{2,130},{130,2},{3,131},{131,3},{4... | collective-permute-start | bytes 1572872 | tf_op jit(solution)/shard_map/ppermute | solution.py:264
  154.9 1.0 copy-start.2

commit v2 on v1

v2 whole, which is shorter than its diff:
```python
import functools
import math

import jax
import jax.numpy as jnp
from jax import lax
from jax.experimental import pallas as pl
from jax.experimental.pallas import tpu as pltpu
from jax.sharding import Mesh, PartitionSpec as P

F32, BF16 = jnp.float32, jnp.bfloat16
HD = 128
RUN = 128
BLK = 2 * RUN
PAY = BLK + 16
QPK = 4
SCALING = HD**-0.5
NT = (((1,), (1,)), ((), ()))
NN = (((1,), (0,)), ((), ()))
CTX = ("xl", "z", "core")
HEAD = ("xh", "y")


def visits_kernel(*refs, nb, m):
    refs = list(refs)

    def take(count):
        head = refs[:count]
        del refs[:count]
        return head

    (z_ref,) = take(1)
    qd_hbm, aux_hbm, kv_hbm = take(nb), take(nb - 1), take(m)
    dq_hbm, (dkv_hbm,) = take(nb), take(1)
    qds, auxs, kvs, dqt, dqo, dkvo, ks, vs, kts, acck, accv = take(11)
    order, krun, qrun_s, sem, osem = take(5)
    nr = 2 * m
    layers = qds.shape[2]
    rows = qds.shape[3] // 2
    c1 = SCALING * math.log2(math.e)

    z = z_ref[0]
    small = [
        pltpu.make_async_copy(kv_hbm[t], kvs.at[lax.rem(z - t + m, m)], sem.at[t]) for t in range(m)
    ]
    aux_hbm = aux_hbm[: nb - 2] + [aux_hbm[-1].at[0:8], aux_hbm[-1].at[8:16]]
    small += [pltpu.make_async_copy(aux_hbm[b], auxs.at[b], sem.at[m + b]) for b in range(nb)]
    large = [pltpu.make_async_copy(qd_hbm[b], qds.at[b], sem.at[m + nb + b]) for b in range(nb)]
    for c in small + large:
        c.start()
    acck[...] = jnp.zeros_like(acck)
    accv[...] = jnp.zeros_like(accv)
    for c in small:
        c.wait()

    for j in range(m):
        for i in range(2):
            tag = kvs[j, BLK + 8 * i : BLK + 8 * i + 8, 0:HD].astype(F32)
            krun[2 * j + i] = jnp.max(tag).astype(jnp.int32)
    for b in range(nb):
        for i in range(2):
            qrun_s[2 * b + i] = jnp.max(auxs[b, 4 + i : 5 + i, 0:HD]).astype(jnp.int32)
    for i in range(nr):
        mine = krun[i]
        rank = jnp.int32(0)
        for j in range(nr):
            if j != i:
                rank = rank + (krun[j] < mine).astype(jnp.int32)
        order[rank] = i

    def arrange(i, carry):
        s = order[i]
        at = pl.multiple_of((s % 2) * RUN, RUN)
        to = pl.multiple_of(i * RUN, RUN)
        k = kvs[s // 2, pl.ds(at, RUN), 0:HD]
        ks[pl.ds(to, RUN), :] = k
        vs[pl.ds(to, RUN), :] = kvs[s // 2, pl.ds(at, RUN), HD : 2 * HD]
        kts[i // 2, i % 2] = k.T
        return carry

    lax.fori_loop(0, nr, arrange, 0)
    for c in large:
        c.wait()

    def query_half(qi, carry):
        b = qi // 2
        qrun = qrun_s[qi]
        reach = jnp.int32(0)
        for j in range(nr):
            reach = reach + (krun[j] <= qrun).astype(jnp.int32)
        off = pl.multiple_of((qi % 2) * rows, rows)
        dqt[...] = jnp.zeros_like(dqt)

        def visit(p, masked):
            at = pl.multiple_of(p * BLK, BLK)
            kp = ks[pl.ds(at, BLK), :]
            vp = vs[pl.ds(at, BLK), :]
            kt = jnp.concatenate([kts[p, 0], kts[p, 1]], axis=1)
            if masked:
                first = krun[order[2 * p]] * RUN
                second = krun[order[2 * p + 1]] * RUN
                ii = lax.broadcasted_iota(jnp.int32, (BLK, 1), 0)
                kpos = jnp.where(ii < RUN, ii + first, ii - RUN + second)
                jj = lax.broadcasted_iota(jnp.int32, (1, rows), 1)
                seen = kpos <= jj // QPK + qrun * RUN
            dk = acck[p]
            dv = accv[p]
            for l in range(layers):
                q = qds[b, 0, l, pl.ds(off, rows), :]
                do = qds[b, 1, l, pl.ds(off, rows), :]
                lse = auxs[b, l : l + 1, pl.ds(off, rows)]
                delta = auxs[b, 2 + l : 3 + l, pl.ds(off, rows)]
                scores = lax.dot_general(kp, q, NT, preferred_element_type=F32)
                probs = jnp.exp2(scores * c1 - lse)
                if masked:
                    probs = jnp.where(seen, probs, 0.0)
                dprobs = lax.dot_general(vp, do, NT, preferred_element_type=F32)
                dscore = (probs * (dprobs - delta)).astype(BF16)
                dv = dv + lax.dot_general(probs.astype(BF16), do, NN, preferred_element_type=F32)
                dk = dk + lax.dot_general(dscore, q, NN, preferred_element_type=F32)
                dqt[l] += lax.dot_general(kt, dscore, NN, preferred_element_type=F32)
            acck[p] = dk
            accv[p] = dv

        def step(p, inner):
            full = krun[order[2 * p + 1]] < qrun

            @pl.when(full)
            def _():
                visit(p, False)

            @pl.when(jnp.logical_not(full))
            def _():
                visit(p, True)

            return inner

        lax.fori_loop(0, (reach + 1) // 2, step, 0)
        for l in range(layers):
            dqo[b, l, pl.ds(off, rows), :] = (dqt[l] * SCALING).T.astype(BF16)
        return carry

    lax.fori_loop(0, 2 * nb, query_half, 0)

    def settle(i, carry):
        s = order[i]
        at = pl.multiple_of((i % 2) * RUN, RUN)
        to = pl.multiple_of((s % 2) * RUN, RUN)
        k_sum = acck[i // 2, pl.ds(at, RUN), :] * SCALING
        v_sum = accv[i // 2, pl.ds(at, RUN), :]
        dkvo[s // 2, pl.ds(to, RUN), 0:HD] = k_sum.astype(BF16)
        dkvo[s // 2, pl.ds(to, RUN), HD : 2 * HD] = v_sum.astype(BF16)
        return carry

    outs = [pltpu.make_async_copy(dqo.at[b], dq_hbm[b], osem.at[b]) for b in range(nb)]
    for c in outs:
        c.start()
    lax.fori_loop(0, nr, settle, 0)
    outs.append(pltpu.make_async_copy(dkvo, dkv_hbm, osem.at[nb]))
    outs[-1].start()
    for c in outs:
        c.wait()


def visits(z, queries, auxes, keys):
    nb, m = len(queries), len(keys)
    _, layers, rows, _ = queries[0].shape
    q_shape = (layers, rows, HD)
    aux_shape = auxes[0].shape
    operands = list(queries) + list(auxes) + list(keys)
    units = nb * m * 2
    any_spec = pl.BlockSpec(memory_space=pl.ANY)
    acc_shape = (m, BLK, HD)
    out_shape = [jax.ShapeDtypeStruct(q_shape, BF16)] * nb
    out_shape += [jax.ShapeDtypeStruct((m, BLK, 2 * HD), BF16)]
    outs = pl.pallas_call(
        functools.partial(visits_kernel, nb=nb, m=m),
        out_shape=out_shape,
        in_specs=[pl.BlockSpec(memory_space=pltpu.SMEM)] + [any_spec] * len(operands),
        out_specs=[any_spec] * len(out_shape),
        scratch_shapes=[
            pltpu.VMEM((nb, 2) + q_shape, BF16),
            pltpu.VMEM((nb,) + aux_shape, F32),
            pltpu.VMEM((m, PAY, 2 * HD), BF16),
            pltpu.VMEM((layers, HD, rows // 2), F32),
            pltpu.VMEM((nb,) + q_shape, BF16),
            pltpu.VMEM((m, BLK, 2 * HD), BF16),
            pltpu.VMEM((2 * m * RUN, HD), BF16),
            pltpu.VMEM((2 * m * RUN, HD), BF16),
            pltpu.VMEM((m, 2, HD, RUN), BF16),
            pltpu.VMEM(acc_shape, F32),
            pltpu.VMEM(acc_shape, F32),
            pltpu.SMEM((2 * m,), jnp.int32),
            pltpu.SMEM((2 * m,), jnp.int32),
            pltpu.SMEM((2 * nb,), jnp.int32),
            pltpu.SemaphoreType.DMA((m + 2 * nb,)),
            pltpu.SemaphoreType.DMA((len(out_shape),)),
        ],
        compiler_params=pltpu.CompilerParams(vmem_limit_bytes=60 * 2**20),
        cost_estimate=pl.CostEstimate(
            flops=units * 1024 * RUN * HD * 20,
            bytes_accessed=nb * 3 * 2**20,
            transcendentals=units * 1024 * RUN,
        ),
        name="visits",
    )(z.reshape(1), *operands)
    return outs


def tail_kernel(core_ref, mine_hbm, other_hbm, grads_hbm, out_ref, w, grads, sem):
    core = core_ref[0]
    heads = mine_hbm.shape[0]
    copies = []
    for g in range(heads):
        first = pl.multiple_of((2 * g + core) * HD, HD)
        second = pl.multiple_of((2 * g + 1 - core) * HD, HD)
        both = slice(2 * g * HD, 2 * (g + 1) * HD)
        copies.append(pltpu.make_async_copy(mine_hbm.at[g], w.at[:, pl.ds(first, HD)], sem.at[0, g]))
        copies.append(pltpu.make_async_copy(other_hbm.at[g], w.at[:, pl.ds(second, HD)], sem.at[1, g]))
        copies.append(pltpu.make_async_copy(grads_hbm.at[g], grads.at[:, both], sem.at[2, g]))
    for c in copies:
        c.start()
    for c in copies:
        c.wait()
    out_ref[...] = lax.dot_general(w[...], grads[...], NT, preferred_element_type=F32).astype(out_ref.dtype)


def tail(core, mine, other, grads):
    heads, features, _ = mine.shape
    tokens = grads.shape[1]
    any_spec = pl.BlockSpec(memory_space=pl.ANY)
    return pl.pallas_call(
        tail_kernel,
        out_shape=jax.ShapeDtypeStruct((features, tokens), BF16),
        in_specs=[pl.BlockSpec(memory_space=pltpu.SMEM), any_spec, any_spec, any_spec],
        out_specs=pl.BlockSpec(memory_space=pltpu.VMEM),
        scratch_shapes=[
            pltpu.VMEM((features, 2 * heads * HD), BF16),
            pltpu.VMEM((tokens, 2 * heads * HD), BF16),
            pltpu.SemaphoreType.DMA((3, heads)),
        ],
        compiler_params=pltpu.CompilerParams(vmem_limit_bytes=60 * 2**20),
        cost_estimate=pl.CostEstimate(
            flops=4 * features * tokens * heads * HD, bytes_accessed=6 * 2**20, transcendentals=0
        ),
        name="input_grad",
    )(core.reshape(1), mine, other, grads)


def moved(value, axis, distance):
    size = lax.axis_size(axis)
    return lax.ppermute(value, axis, [(i, (i + distance) % size) for i in range(size)])


def on_device(
    queries, key_rows, value_rows, attn_out, out_grad, log_norm, positions, key_weight, value_weight
):
    layers, tokens, per_group, head_dim = queries.shape
    rows = tokens * per_group
    zn = lax.axis_size("z")
    runs = positions.reshape(2, RUN)[:, 0] // RUN
    tags = jnp.broadcast_to(runs.astype(BF16)[:, None, None], (2, 8, 2 * head_dim)).reshape(16, 2 * head_dim)
    block = jnp.concatenate([key_rows[:, 0], value_rows[:, 0]], axis=1)
    block = jnp.concatenate([block, tags], axis=0)
    keys = {0: block}
    keys[1], keys[zn - 1] = moved(block, "z", 1), moved(block, "z", -1)
    for t in (2, 3):
        keys[t], keys[zn - t] = moved(keys[t - 1], "z", 1), moved(keys[zn - t + 1], "z", -1)
    keys[4] = moved(keys[3], "z", 1)

    q = queries.reshape(layers, rows, head_dim)
    do = out_grad.reshape(layers, rows, head_dim)
    deltas = jnp.sum(out_grad.astype(F32) * attn_out.astype(F32), -1).reshape(layers, rows)
    lse = jnp.transpose(log_norm, (0, 2, 1)).reshape(layers, rows) * math.log2(math.e)
    run_rows = jnp.broadcast_to(runs.astype(F32)[:, None], (2, rows))
    aux = jnp.concatenate([lse, deltas, run_rows, jnp.zeros((2, rows), F32)], axis=0)
    own = (jnp.stack([q, do]), aux)
    over = tuple(moved(a, "core", 1) for a in own)
    both = moved(jnp.concatenate([aux, over[1]], axis=0), "xl", 1)
    far = moved(own[0], "xl", 1)
    far_over = moved(far, "core", 1)

    core = lax.axis_index("core")
    features = key_weight.shape[0]
    kw, vw, _ = lax.optimization_barrier(
        (key_weight[:, 0], value_weight[:, 0], (keys[3], keys[zn - 3]))
    )
    mine = lax.all_to_all(jnp.where(core == 0, kw, vw), HEAD, 0, 0, tiled=True)
    mine = mine.reshape(8, features // 8, head_dim)
    other = moved(mine, "core", 1)

    *dq, dkv = visits(
        lax.axis_index("z"),
        [own[0], over[0], far, far_over],
        [own[1], over[1], both],
        [keys[t] for t in range(zn)],
    )
    back = lax.all_to_all(dkv, "z", 0, 0, tiled=True)
    grads = jnp.sum(back.astype(F32), axis=0).astype(BF16)

    got = moved(dq[1], "core", 1)
    far_sum = (dq[2].astype(F32) + moved(dq[3], "core", 1).astype(F32)).astype(BF16)
    got_far = moved(far_sum, "xl", 1)
    grads, got_far, got = lax.optimization_barrier((grads, got_far, got))
    query_grad = (dq[0].astype(F32) + got.astype(F32) + got_far.astype(F32)).astype(BF16)
    query_grad = query_grad.reshape(queries.shape)

    every = lax.all_to_all(
        jnp.broadcast_to(grads[None], (8,) + grads.shape), HEAD, 0, 0, tiled=True
    )
    input_grad = tail(core, mine, other, every)
    return (
        query_grad,
        grads[:, None, :head_dim],
        grads[:, None, head_dim:],
        input_grad,
    )


def solution(mesh):
    fine = Mesh(mesh.devices.reshape(2, 8, 2, 2, 4), CTX + HEAD)
    placed = (
        P(None, CTX, HEAD, None),
        P(CTX, HEAD, None),
        P(CTX, HEAD, None),
        P(None, CTX, HEAD, None),
        P(None, CTX, HEAD, None),
        P(None, HEAD, CTX),
        P(CTX),
        P(None, HEAD, None),
        P(None, HEAD, None),
    )
    return jax.shard_map(
        on_device,
        mesh=fine,
        in_specs=placed,
        out_specs=(
            P(None, CTX, HEAD, None),
            P(CTX, HEAD, None),
            P(CTX, HEAD, None),
            P(HEAD, CTX),
        ),
        check_vma=False,
    )
```

time: 163 us -> 142 us (0.87)
  Pallas kernels: 53.9 us -> 39.2 us
  waiting for transfers between devices: 45.7 us -> 41.9 us
  local copies, waits for them, and re-layouts: 7.81 us -> 5.19 us
    all_to_all x1 -> x2, waiting for transfers between devices: 0.01 us -> 35.7 us  [the longest x1 24.3 us: on_device(): back = lax.all_to_all(dkv, 'z', 0, 0, tiled=True)]
    ppermute x23 -> x16, waiting for transfers between devices: 41.3 us -> 6.18 us  [moved(): lax.ppermute(value, axis, [(i, (i + distance) % size) for i in range(size)])]
    pallas_call x4 -> x2, Pallas kernels: 53.9 us -> 39.2 us  [the longest x1 34.5 us: visits(): pl.pallas_call(functools.partial(visits_kernel, nb=nb, m=m), out_shape=ou...]
    all_to_all x1 -> x2, starting transfers between devices: 5 us -> 15.9 us  [the longest x1 8.91 us: on_device(): back = lax.all_to_all(dkv, 'z', 0, 0, tiled=True)]
    ppermute x23 -> x16, starting transfers between devices: 30.3 us -> 19.8 us  [moved(): lax.ppermute(value, axis, [(i, (i + distance) % size) for i in range(size)])]
    all_to_all x1, waiting for transfers between devices: 4.38 us -> 0.01 us  [on_device(): mine = lax.all_to_all(jnp.where(core == 0, kw, vw), HEAD, 0, 0, tiled=True)]
    unnamed x46 -> x30, local copies, waits for them, and re-layouts: 3.74 us -> 2.57 us
    convert_element_type x3 -> x2, other arithmetic: 4.54 us -> 4.34 us  [the longest x1 2.35 us: on_device(): (dq[0].astype(F32) + got.astype(F32) + got_far.astype(F32)).astype(BF16)]
  transfers between devices with their start and end apart: 25 -> 19, of which waited for: 9 -> 6; matrix products, arithmetic and copies ran while one was open for 6% -> 8% of each run, Pallas kernels for 18% -> 24%
where the time goes in v2:
time: 142 us; the launch traced here: 141 us
  starting transfers between devices  42.4 us (30%)
  waiting for transfers between devices  41.9 us (30%)
  Pallas kernels  39.2 us (28%)
  other arithmetic  11.7 us (8%)
  local copies, waits for them, and re-layouts  5.19 us (4%)
    pallas_call x1, Pallas kernels, visits(): pl.pallas_call(functools.partial(visits_kernel, nb=nb, m=m), out_shape=ou...  34.5 us
    all_to_all x1, waiting for transfers between devices, on_device(): back = lax.all_to_all(dkv, 'z', 0, 0, tiled=True)  24.3 us
    ppermute x16, starting transfers between devices, moved(): lax.ppermute(value, axis, [(i, (i + distance) % size) for i in range(size)])  19.8 us
    all_to_all x1, waiting for transfers between devices, on_device(): lax.all_to_all(jnp.broadcast_to(grads[None], (8,) + grads.shape), HEAD, 0...  11.5 us
    all_to_all x1, starting transfers between devices, on_device(): back = lax.all_to_all(dkv, 'z', 0, 0, tiled=True)  8.91 us
    all_to_all x1, starting transfers between devices, on_device(): lax.all_to_all(jnp.broadcast_to(grads[None], (8,) + grads.shape), HEAD, 0...  6.99 us
    all_to_all x1, starting transfers between devices, on_device(): mine = lax.all_to_all(jnp.where(core == 0, kw, vw), HEAD, 0, 0, tiled=True)  6.69 us
    ppermute x16, waiting for transfers between devices, moved(): lax.ppermute(value, axis, [(i, (i + distance) % size) for i in range(size)])  6.18 us
  transfers between devices with their start and end apart: 19, of which 6 were waited for; matrix products, arithmetic and copies ran while one was open for 8% of the time, Pallas kernels for 24%

profile of v2, /device:TPU:1, one launch (start us, length us, event | category | flops | bytes accessed | tf_op | source)
XLA Modules:
  0.0 141.4 jit_solution(11504273365758763136)
XLA Ops:
  0.6 0.0 copy-start.14
  0.7 2.4 %pad_maximum_fusion.refs_1_ = bf16[2,2,1024,128]{3,2,1,0:T(8,128)(2,1)} fusion(bf16[1,2,1024,128]{3,2,1,0:T(8,128)(2,1)} %bitcast.20, bf16[1,2,1024,128]{3,2,1,0:T(8,128)(2,1)} %bitcast.21), kind=kLoop, calls=%fused_computation.1 | loop fusion | flops 524288 | bytes 2097152 | tf_op jit(solution)/shard_map/stack | solution.py:277
  3.1 2.0 %collective-permute-start.1 = (bf16[2,2,1024,128]{3,2,1,0:T(8,128)(2,1)}, bf16[2,2,1024,128]{3,2,1,0:T(8,128)(2,1)}, u32[]{:S(2)}, u32[]{:S(2)}) collective-permute-start(bf16[2,2,1024,128]{3,2,1,0:T(8,128)(2,1)} %pad_maximum_fusion.refs_1_), channel_id=1, source_target_pairs={{0,128},{128,0},{1,129},{129,1},{2,130},{130,2},{3,131},{131,3},{4... | collective-permute-start | bytes 3145736 | tf_op jit(solution)/shard_map/ppermute | solution.py:252
  5.2 0.1 slice_reduce_fusion
  5.3 0.1 broadcast_in_dim.36
  5.4 0.1 reshape.69
  5.5 0.1 maximum_maximum_fusion.refs_8_
  5.6 1.7 %collective-permute-start.5 = (bf16[272,256]{1,0:T(8,128)(2,1)S(1)}, bf16[272,256]{1,0:T(8,128)(2,1)}, u32[]{:S(2)}, u32[]{:S(2)}) collective-permute-start(bf16[272,256]{1,0:T(8,128)(2,1)S(1)} %maximum_maximum_fusion.refs_8_), channel_id=1, source_target_pairs={{0,16},{16,32},{32,48},{48,64},{64,80},{80,96},{96,112},{112,0},{1... | collective-permute-start | bytes 417800 | tf_op jit(solution)/shard_map/ppermute | solution.py:252
  7.3 4.0 %collective-permute-start.9 = (bf16[272,256]{1,0:T(8,128)(2,1)S(1)}, bf16[272,256]{1,0:T(8,128)(2,1)}, u32[]{:S(2)}, u32[]{:S(2)}) collective-permute-start(bf16[272,256]{1,0:T(8,128)(2,1)S(1)} %maximum_maximum_fusion.refs_8_), channel_id=1, source_target_pairs={{0,112},{16,0},{32,16},{48,32},{64,48},{80,64},{96,80},{112,96},{1... | collective-permute-start | bytes 417800 | tf_op jit(solution)/shard_map/ppermute | solution.py:252
  11.4 3.1 %collective-permute-done.5.refs_9_ = bf16[272,256]{1,0:T(8,128)(2,1)} collective-permute-done((bf16[272,256]{1,0:T(8,128)(2,1)S(1)}, bf16[272,256]{1,0:T(8,128)(2,1)}, u32[]{:S(2)}, u32[]{:S(2)}) %collective-permute-start.5) | collective-permute-done | bytes 139296 | tf_op jit(solution)/shard_map/ppermute | solution.py:252
  14.5 2.7 %collective-permute-start.10 = (bf16[272,256]{1,0:T(8,128)(2,1)}, bf16[272,256]{1,0:T(8,128)(2,1)}, u32[]{:S(2)}, u32[]{:S(2)}) collective-permute-start(bf16[272,256]{1,0:T(8,128)(2,1)} %collective-permute-done.9.refs_15_), channel_id=1, source_target_pairs={{0,112},{16,0},{32,16},{48,32},{64,48},{80,64},{96,80},{112,96},{1... | collective-permute-start | bytes 417800 | tf_op jit(solution)/shard_map/ppermute | solution.py:252
  17.2 0.6 multiply_reduce_fusion
  17.8 0.1 copy.15
  18.0 0.2 mul.18
  18.1 0.2 reshape.63
  18.3 0.8 convert_reduce_fusion
  19.1 0.8 collective-permute-done.6.refs_10_
  19.9 2.7 %collective-permute-start.11 = (bf16[272,256]{1,0:T(8,128)(2,1)}, bf16[272,256]{1,0:T(8,128)(2,1)S(1)}, u32[]{:S(2)}, u32[]{:S(2)}) collective-permute-start(bf16[272,256]{1,0:T(8,128)(2,1)} %collective-permute-done.10.refs_14_), channel_id=1, source_target_pairs={{0,112},{16,0},{32,16},{48,32},{64,48},{80,64},{96,80},{112,96},{1... | collective-permute-start | bytes 417800 | tf_op jit(solution)/shard_map/ppermute | solution.py:252
  22.6 0.1 broadcast_in_dim.34
  22.7 0.0 copy-start.8
  22.7 3.3 %collective-permute-start.3 = (f32[8,1024]{1,0:T(8,128)S(1)}, f32[8,1024]{1,0:T(8,128)S(1)}, u32[]{:S(2)}, u32[]{:S(2)}) collective-permute-start(f32[8,1024]{1,0:T(8,128)S(1)} %pad_maximum_fusion.1.refs_5_), channel_id=1, source_target_pairs={{0,8},{8,0},{1,9},{9,1},{2,10},{10,2},{3,11},{11,3},{4,12},{12,4},... | collective-permute-start | bytes 98312 | tf_op jit(solution)/shard_map/ppermute | solution.py:252
  26.0 0.1 collective-permute-start
  26.1 0.8 collective-permute-done.3.refs_6_
  26.9 0.3 collective-permute-start.4
  27.3 0.1 collective-permute-start.8
  27.4 0.6 copy-done.12
  27.9 1.9 %collective-permute-start.2 = (bf16[2,2,1024,128]{3,2,1,0:T(8,128)(2,1)}, bf16[2,2,1024,128]{3,2,1,0:T(8,128)(2,1)S(1)}, u32[]{:S(2)}, u32[]{:S(2)}) collective-permute-start(bf16[2,2,1024,128]{3,2,1,0:T(8,128)(2,1)} %collective-permute-done.1.refs_3_), channel_id=1, source_target_pairs={{0,8},{8,0},{1,9},{9,1},{2,10},{10,2},{3,11},{11,3},{4,12},{12,4},... | collective-permute-start | bytes 3145736 | tf_op jit(solution)/shard_map/ppermute | solution.py:252
  29.8 3.1 %broadcast_select_fusion = bf16[8192,128]{1,0:T(8,128)(2,1)} fusion(bf16[8192,128]{1,0:T(8,128)(2,1)S(1)} %bitcast.18, bf16[8192,128]{1,0:T(8,128)(2,1)} %bitcast.19, pred[]{:T(512)S(6)} %eq.3), kind=kLoop, calls=%fused_computation | loop fusion | flops 1048576 | bytes 6291457 | tf_op jit(solution)/shard_map/jit(_where)/select_n | solution.py:288
  33.0 6.7 %all-to-all-start.1 = ((bf16[8,1024,128]{2,1,0:T(8,128)(2,1)}), bf16[8,1024,128]{2,1,0:T(8,128)(2,1)S(1)}, u32[]{:S(2)}, u32[]{:S(2)}) async-start(bf16[8,1024,128]{2,1,0:T(8,128)(2,1)} %bitcast.17), calls=%async_computation.1 | async-start | bytes 4194304 | tf_op jit(solution)/shard_map/all_to_all | solution.py:288
  39.7 0.0 copy-start.13
  39.7 0.6 copy-done.13
  40.3 0.4 copy-done.11
  40.7 34.5 %visits.1 = (bf16[2,1024,128]{2,1,0:T(8,128)(2,1)}, bf16[2,1024,128]{2,1,0:T(8,128)(2,1)}, bf16[2,1024,128]{2,1,0:T(8,128)(2,1)}, bf16[2,1024,128]{2,1,0:T(8,128)(2,1)}, bf16[8,256,256]{2,1,0:T(8,128)(2,1)}) custom-call(s32[1]{0:T(128)} %bitcast.refs_0_, bf16[2,2,1024,128]{3,2,1,0:T(8,128)(2,1)} %pad_maximum_fusion.refs_1_, ...), custom_call_target="tpu_custom_call" | custom-call | flops 21474836480 | bytes 12582912 | tf_op jit(solution)/shard_map/visits/pallas_call | solution.py:176
  75.2 8.9 %all-to-all-start = ((bf16[8,256,256]{2,1,0:T(8,128)(2,1)}), bf16[8,256,256]{2,1,0:T(8,128)(2,1)S(1)}, u32[]{:S(2)}, u32[]{:S(2)}) async-start(bf16[8,256,256]{2,1,0:T(8,128)(2,1)} %get-tuple-element.15), calls=%async_computation | async-start | bytes 2097152 | tf_op jit(solution)/shard_map/all_to_all | solution.py:298
  84.1 0.5 collective-permute-start.15
  84.6 0.1 collective-permute-start.14
  84.7 1.5 %collective-permute-done.12 = bf16[2,1024,128]{2,1,0:T(8,128)(2,1)S(1)} collective-permute-done((bf16[2,1024,128]{2,1,0:T(8,128)(2,1)}, bf16[2,1024,128]{2,1,0:T(8,128)(2,1)S(1)}, u32[]{:S(2)}, u32[]{:S(2)}) %collective-permute-start.12) | collective-permute-done | bytes 524320 | tf_op jit(solution)/shard_map/ppermute | solution.py:252
  86.3 2.0 %add_convert_fusion.1 = bf16[2,1024,128]{2,1,0:T(8,128)(2,1)} fusion(bf16[2,1024,128]{2,1,0:T(8,128)(2,1)S(1)} %collective-permute-done.12, bf16[2,1024,128]{2,1,0:T(8,128)(2,1)} %get-tuple-element.16), kind=kLoop, calls=%fused_computation.3 | loop fusion | flops 1048576 | bytes 1572864 | tf_op jit(solution)/shard_map/convert_element_type | solution.py:302
  88.2 0.3 collective-permute-start.13
  88.5 24.3 %all-to-all-done = bf16[8,256,256]{2,1,0:T(8,128)(2,1)S(1)} async-done(((bf16[8,256,256]{2,1,0:T(8,128)(2,1)}), bf16[8,256,256]{2,1,0:T(8,128)(2,1)S(1)}, u32[]{:S(2)}, u32[]{:S(2)}) %all-to-all-start) | async-done | bytes 1048608 | tf_op jit(solution)/shard_map/all_to_all | solution.py:298
  112.8 0.1 reduce_sum.22
  113.0 1.1 broadcast_in_dim.41
  114.1 7.0 %all-to-all-start.2 = ((bf16[8,256,256]{2,1,0:T(8,128)(2,1)}), bf16[8,256,256]{2,1,0:T(8,128)(2,1)S(1)}, u32[]{:S(2)}, u32[]{:S(2)}) async-start(bf16[8,256,256]{2,1,0:T(8,128)(2,1)} %broadcast_in_dim.41), calls=%async_computation.2 | async-start | bytes 2097152 | tf_op jit(solution)/shard_map/all_to_all | solution.py:308
  121.0 0.7 slice_bitcast_fusion
  121.7 2.4 %add_convert_fusion = bf16[2,1024,128]{2,1,0:T(8,128)(2,1)} fusion(bf16[2,1024,128]{2,1,0:T(8,128)(2,1)} %collective-permute-done.13, bf16[2,1024,128]{2,1,0:T(8,128)(2,1)} %collective-permute-done.14, bf16[2,1024,128]{2,1,0:T(8,128)(2,1)} %get-tuple-element.14), kind=kLoop, calls=%fused_computation.2 | loop fusion | flops 1572864 | bytes 2097152 | tf_op jit(solution)/shard_map/convert_element_type | solution.py:305
  124.1 11.5 %all-to-all-done.2.grads_hbm = bf16[8,256,256]{2,1,0:T(8,128)(2,1)S(1)} async-done(((bf16[8,256,256]{2,1,0:T(8,128)(2,1)}), bf16[8,256,256]{2,1,0:T(8,128)(2,1)S(1)}, u32[]{:S(2)}, u32[]{:S(2)}) %all-to-all-start.2) | async-done | bytes 1048608 | tf_op jit(solution)/shard_map/all_to_all | solution.py:308
  135.5 1.0 copy-done.1
  136.5 4.7 %input_grad.1 = bf16[1024,256]{1,0:T(8,128)(2,1)} custom-call(s32[1]{0:T(128)} %bitcast.10.core_ref, bf16[8,1024,128]{2,1,0:T(8,128)(2,1)} %copy-done, bf16[8,1024,128]{2,1,0:T(8,128)(2,1)} %collective-permute-done.15.other_hbm, bf16[8,256,256]{2,1,0:T(8,128)(2,1)} %copy-done.1), custom_call_target="tpu_custom_call" | custom-call | flops 1073741824 | bytes 6291456 | tf_op jit(solution)/shard_map/input_grad/pallas_call | solution.py:232
  (45 shorter events, 0.2 us)
Async XLA Ops:
  0.6 16.5 %copy-start.3 = (bf16[2,256,4,128]{3,2,1,0:T(4,128)(2,1)S(1)}, bf16[2,256,4,128]{3,2,1,0:T(4,128)(2,1)}, u32[]{:S(2)}) copy-start(bf16[2,256,4,128]{3,2,1,0:T(4,128)(2,1)} %param.13) | copy-start | bytes 1572868
  0.6 4.5 %copy-start.14 = (s32[256]{0:T(256)S(1)}, s32[256]{0:T(256)}, u32[]{:S(2)}) copy-start(s32[256]{0:T(256)} %param.15) | copy-start | bytes 3076
  0.7 4.8 %copy-start.7 = (bf16[256,1,128]{2,0,1:T(8,128)(2,1)S(1)}, bf16[256,1,128]{2,0,1:T(8,128)(2,1)}, u32[]{:S(2)}) copy-start(bf16[256,1,128]{2,0,1:T(8,128)(2,1)} %param.10) | copy-start | bytes 196612
  0.7 4.8 %copy-start.6 = (bf16[256,1,128]{2,0,1:T(8,128)(2,1)S(1)}, bf16[256,1,128]{2,0,1:T(8,128)(2,1)}, u32[]{:S(2)}) copy-start(bf16[256,1,128]{2,0,1:T(8,128)(2,1)} %param.11) | copy-start | bytes 196612
  0.7 10.7 %copy-start.10 = (f32[2,4,256]{2,1,0:T(4,128)S(1)}, f32[2,4,256]{2,1,0:T(4,128)}, u32[]{:S(2)}) copy-start(f32[2,4,256]{2,1,0:T(4,128)} %param.14) | copy-start | bytes 24580
  0.7 16.5 %copy-start.4 = (bf16[2,256,4,128]{3,2,1,0:T(4,128)(2,1)S(1)}, bf16[2,256,4,128]{3,2,1,0:T(4,128)(2,1)}, u32[]{:S(2)}) copy-start(bf16[2,256,4,128]{3,2,1,0:T(4,128)(2,1)} %param.12) | copy-start | bytes 1572868
  0.7 29.1 %copy-start.2 = (bf16[8192,1,128]{2,0,1:T(8,128)(2,1)S(1)}, bf16[8192,1,128]{2,0,1:T(8,128)(2,1)}, u32[]{:S(2)}) copy-start(bf16[8192,1,128]{2,0,1:T(8,128)(2,1)} %param.16) | copy-start | bytes 6291460
  3.1 24.8 %collective-permute-start.1 = (bf16[2,2,1024,128]{3,2,1,0:T(8,128)(2,1)}, bf16[2,2,1024,128]{3,2,1,0:T(8,128)(2,1)}, u32[]{:S(2)}, u32[]{:S(2)}) collective-permute-start(bf16[2,2,1024,128]{3,2,1,0:T(8,128)(2,1)} %pad_maximum_fusion.refs_1_), channel_id=1, source_target_pairs={{0,128},{128,0},{1,129},{129,1},{2,130},{130,2},{3,131},{131,3},{4... | collective-permute-start | bytes 3145736 | tf_op jit(solution)/shard_map/ppermute | solution.py:252
  5.6 27.4 %copy-start.5 = (bf16[272,256]{1,0:T(8,128)(2,1)}, bf16[272,256]{1,0:T(8,128)(2,1)S(1)}, u32[]{:S(2)}) copy-start(bf16[272,256]{1,0:T(8,128)(2,1)S(1)} %maximum_maximum_fusion.refs_8_) | copy-start | bytes 417796
  5.6 8.8 %collective-permute-start.5 = (bf16[272,256]{1,0:T(8,128)(2,1)S(1)}, bf16[272,256]{1,0:T(8,128)(2,1)}, u32[]{:S(2)}, u32[]{:S(2)}) collective-permute-start(bf16[272,256]{1,0:T(8,128)(2,1)S(1)} %maximum_maximum_fusion.refs_8_), channel_id=1, source_target_pairs={{0,16},{16,32},{32,48},{48,64},{64,80},{80,96},{96,112},{112,0},{1... | collective-permute-start | bytes 417800 | tf_op jit(solution)/shard_map/ppermute | solution.py:252
  7.3 7.1 %collective-permute-start.9 = (bf16[272,256]{1,0:T(8,128)(2,1)S(1)}, bf16[272,256]{1,0:T(8,128)(2,1)}, u32[]{:S(2)}, u32[]{:S(2)}) collective-permute-start(bf16[272,256]{1,0:T(8,128)(2,1)S(1)} %maximum_maximum_fusion.refs_8_), channel_id=1, source_target_pairs={{0,112},{16,0},{32,16},{48,32},{64,48},{80,64},{96,80},{112,96},{1... | collective-permute-start | bytes 417800 | tf_op jit(solution)/shard_map/ppermute | solution.py:252
  14.5 5.4 %collective-permute-start.6 = (bf16[272,256]{1,0:T(8,128)(2,1)}, bf16[272,256]{1,0:T(8,128)(2,1)}, u32[]{:S(2)}, u32[]{:S(2)}) collective-permute-start(bf16[272,256]{1,0:T(8,128)(2,1)} %collective-permute-done.5.refs_9_), channel_id=1, source_target_pairs={{0,16},{16,32},{32,48},{48,64},{64,80},{80,96},{96,112},{112,0},{1... | collective-permute-start | bytes 417800 | tf_op jit(solution)/shard_map/ppermute | solution.py:252
  14.5 5.4 %collective-permute-start.10 = (bf16[272,256]{1,0:T(8,128)(2,1)}, bf16[272,256]{1,0:T(8,128)(2,1)}, u32[]{:S(2)}, u32[]{:S(2)}) collective-permute-start(bf16[272,256]{1,0:T(8,128)(2,1)} %collective-permute-done.9.refs_15_), channel_id=1, source_target_pairs={{0,112},{16,0},{32,16},{48,32},{64,48},{80,64},{96,80},{112,96},{1... | collective-permute-start | bytes 417800 | tf_op jit(solution)/shard_map/ppermute | solution.py:252
  19.9 7.4 %collective-permute-start.7 = (bf16[272,256]{1,0:T(8,128)(2,1)}, bf16[272,256]{1,0:T(8,128)(2,1)}, u32[]{:S(2)}, u32[]{:S(2)}) collective-permute-start(bf16[272,256]{1,0:T(8,128)(2,1)} %collective-permute-done.6.refs_10_), channel_id=1, source_target_pairs={{0,16},{16,32},{32,48},{48,64},{64,80},{80,96},{96,112},{112,0},{1... | collective-permute-start | bytes 417800 | tf_op jit(solution)/shard_map/ppermute | solution.py:252
  19.9 7.4 %collective-permute-start.11 = (bf16[272,256]{1,0:T(8,128)(2,1)}, bf16[272,256]{1,0:T(8,128)(2,1)S(1)}, u32[]{:S(2)}, u32[]{:S(2)}) collective-permute-start(bf16[272,256]{1,0:T(8,128)(2,1)} %collective-permute-done.10.refs_14_), channel_id=1, source_target_pairs={{0,112},{16,0},{32,16},{48,32},{64,48},{80,64},{96,80},{112,96},{1... | collective-permute-start | bytes 417800 | tf_op jit(solution)/shard_map/ppermute | solution.py:252
  22.7 10.3 %copy-start.8 = (f32[8,1024]{1,0:T(8,128)}, f32[8,1024]{1,0:T(8,128)S(1)}, u32[]{:S(2)}) copy-start(f32[8,1024]{1,0:T(8,128)S(1)} %pad_maximum_fusion.1.refs_5_) | copy-start | bytes 98308
  22.7 4.2 %collective-permute-start.3 = (f32[8,1024]{1,0:T(8,128)S(1)}, f32[8,1024]{1,0:T(8,128)S(1)}, u32[]{:S(2)}, u32[]{:S(2)}) collective-permute-start(f32[8,1024]{1,0:T(8,128)S(1)} %pad_maximum_fusion.1.refs_5_), channel_id=1, source_target_pairs={{0,8},{8,0},{1,9},{9,1},{2,10},{10,2},{3,11},{11,3},{4,12},{12,4},... | collective-permute-start | bytes 98312 | tf_op jit(solution)/shard_map/ppermute | solution.py:252
  26.0 13.7 %collective-permute-start = (bf16[2,2,1024,128]{3,2,1,0:T(8,128)(2,1)}, bf16[2,2,1024,128]{3,2,1,0:T(8,128)(2,1)}, u32[]{:S(2)}, u32[]{:S(2)}) collective-permute-start(bf16[2,2,1024,128]{3,2,1,0:T(8,128)(2,1)} %pad_maximum_fusion.refs_1_), channel_id=1, source_target_pairs={{0,8},{8,0},{1,9},{9,1},{2,10},{10,2},{3,11},{11,3},{4,12},{12,4},... | collective-permute-start | bytes 3145736 | tf_op jit(solution)/shard_map/ppermute | solution.py:252
  26.9 6.1 %copy-start.9 = (f32[8,1024]{1,0:T(8,128)}, f32[8,1024]{1,0:T(8,128)S(1)}, u32[]{:S(2)}) copy-start(f32[8,1024]{1,0:T(8,128)S(1)} %collective-permute-done.3.refs_6_) | copy-start | bytes 98308
  26.9 12.8 %collective-permute-start.4 = (f32[16,1024]{1,0:T(8,128)S(1)}, f32[16,1024]{1,0:T(8,128)S(1)}, u32[]{:S(2)}, u32[]{:S(2)}) collective-permute-start(f32[16,1024]{1,0:T(8,128)S(1)} %concatenate.14), channel_id=1, source_target_pairs={{0,128},{128,0},{1,129},{129,1},{2,130},{130,2},{3,131},{131,3},{4... | collective-permute-start | bytes 196616 | tf_op jit(solution)/shard_map/ppermute | solution.py:252
  27.3 0.7 copy-start.12
  27.3 12.4 %collective-permute-start.8 = (bf16[272,256]{1,0:T(8,128)(2,1)}, bf16[272,256]{1,0:T(8,128)(2,1)}, u32[]{:S(2)}, u32[]{:S(2)}) collective-permute-start(bf16[272,256]{1,0:T(8,128)(2,1)} %collective-permute-done.7.refs_11_), channel_id=1, source_target_pairs={{0,16},{16,32},{32,48},{48,64},{64,80},{80,96},{96,112},{112,0},{1... | collective-permute-start | bytes 417800 | tf_op jit(solution)/shard_map/ppermute | solution.py:252
  27.9 11.8 %collective-permute-start.2 = (bf16[2,2,1024,128]{3,2,1,0:T(8,128)(2,1)}, bf16[2,2,1024,128]{3,2,1,0:T(8,128)(2,1)S(1)}, u32[]{:S(2)}, u32[]{:S(2)}) collective-permute-start(bf16[2,2,1024,128]{3,2,1,0:T(8,128)(2,1)} %collective-permute-done.1.refs_3_), channel_id=1, source_target_pairs={{0,8},{8,0},{1,9},{9,1},{2,10},{10,2},{3,11},{11,3},{4,12},{12,4},... | collective-permute-start | bytes 3145736 | tf_op jit(solution)/shard_map/ppermute | solution.py:252
  33.0 42.2 %all-to-all-start.1 = ((bf16[8,1024,128]{2,1,0:T(8,128)(2,1)}), bf16[8,1024,128]{2,1,0:T(8,128)(2,1)S(1)}, u32[]{:S(2)}, u32[]{:S(2)}) async-start(bf16[8,1024,128]{2,1,0:T(8,128)(2,1)} %bitcast.17), calls=%async_computation.1 | async-start | bytes 4194304 | tf_op jit(solution)/shard_map/all_to_all | solution.py:288
  39.7 0.6 copy-start.13
  39.7 1.0 copy-start.11
  75.2 37.7 %copy-start = (bf16[8,1024,128]{2,1,0:T(8,128)(2,1)}, bf16[8,1024,128]{2,1,0:T(8,128)(2,1)S(1)}, u32[]{:S(2)}) copy-start(bf16[8,1024,128]{2,1,0:T(8,128)(2,1)S(1)} %all-to-all-done.1.mine_hbm) | copy-start | bytes 6291460
  75.2 37.6 %all-to-all-start = ((bf16[8,256,256]{2,1,0:T(8,128)(2,1)}), bf16[8,256,256]{2,1,0:T(8,128)(2,1)S(1)}, u32[]{:S(2)}, u32[]{:S(2)}) async-start(bf16[8,256,256]{2,1,0:T(8,128)(2,1)} %get-tuple-element.15), calls=%async_computation | async-start | bytes 2097152 | tf_op jit(solution)/shard_map/all_to_all | solution.py:298
  84.1 2.1 %collective-permute-start.12 = (bf16[2,1024,128]{2,1,0:T(8,128)(2,1)}, bf16[2,1024,128]{2,1,0:T(8,128)(2,1)S(1)}, u32[]{:S(2)}, u32[]{:S(2)}) collective-permute-start(bf16[2,1024,128]{2,1,0:T(8,128)(2,1)} %get-tuple-element.17), channel_id=1, source_target_pairs={{0,8},{8,0},{1,9},{9,1},{2,10},{10,2},{3,11},{11,3},{4,12},{12,4},... | collective-permute-start | bytes 1572872 | tf_op jit(solution)/shard_map/ppermute | solution.py:252
  84.1 39.9 %collective-permute-start.15 = (bf16[8,1024,128]{2,1,0:T(8,128)(2,1)S(1)}, bf16[8,1024,128]{2,1,0:T(8,128)(2,1)}, u32[]{:S(2)}, u32[]{:S(2)}) collective-permute-start(bf16[8,1024,128]{2,1,0:T(8,128)(2,1)S(1)} %all-to-all-done.1.mine_hbm), channel_id=1, source_target_pairs={{0,8},{8,0},{1,9},{9,1},{2,10},{10,2},{3,11},{11,3},{4,12},{12,4},... | collective-permute-start | bytes 6291464 | tf_op jit(solution)/shard_map/ppermute | solution.py:252
  84.6 28.3 %collective-permute-start.14 = (bf16[2,1024,128]{2,1,0:T(8,128)(2,1)}, bf16[2,1024,128]{2,1,0:T(8,128)(2,1)}, u32[]{:S(2)}, u32[]{:S(2)}) collective-permute-start(bf16[2,1024,128]{2,1,0:T(8,128)(2,1)} %get-tuple-element.18), channel_id=1, source_target_pairs={{0,8},{8,0},{1,9},{9,1},{2,10},{10,2},{3,11},{11,3},{4,12},{12,4},... | collective-permute-start | bytes 1572872 | tf_op jit(solution)/shard_map/ppermute | solution.py:252
  88.2 24.7 %collective-permute-start.13 = (bf16[2,1024,128]{2,1,0:T(8,128)(2,1)}, bf16[2,1024,128]{2,1,0:T(8,128)(2,1)}, u32[]{:S(2)}, u32[]{:S(2)}) collective-permute-start(bf16[2,1024,128]{2,1,0:T(8,128)(2,1)} %add_convert_fusion.1), channel_id=1, source_target_pairs={{0,128},{128,0},{1,129},{129,1},{2,130},{130,2},{3,131},{131,3},{4... | collective-permute-start | bytes 1572872 | tf_op jit(solution)/shard_map/ppermute | solution.py:252
  114.1 21.5 %all-to-all-start.2 = ((bf16[8,256,256]{2,1,0:T(8,128)(2,1)}), bf16[8,256,256]{2,1,0:T(8,128)(2,1)S(1)}, u32[]{:S(2)}, u32[]{:S(2)}) async-start(bf16[8,256,256]{2,1,0:T(8,128)(2,1)} %broadcast_in_dim.41), calls=%async_computation.2 | async-start | bytes 2097152 | tf_op jit(solution)/shard_map/all_to_all | solution.py:308
  135.5 1.0 copy-start.1

commit v3 on v2

--- a/solution.py
+++ b/solution.py
@@ -14,6 +14,7 @@
 BLK = 2 * RUN
 PAY = BLK + 16
 QPK = 4
+WIDE = 4
 SCALING = HD**-0.5
 NT = (((1,), (1,)), ((), ()))
 NN = (((1,), (0,)), ((), ()))
@@ -60,12 +61,12 @@
     for b in range(nb):
         for i in range(2):
             qrun_s[2 * b + i] = jnp.max(auxs[b, 4 + i : 5 + i, 0:HD]).astype(jnp.int32)
+    held = [krun[j] for j in range(nr)]
     for i in range(nr):
-        mine = krun[i]
         rank = jnp.int32(0)
         for j in range(nr):
             if j != i:
-                rank = rank + (krun[j] < mine).astype(jnp.int32)
+                rank = rank + (held[j] < held[i]).astype(jnp.int32)
         order[rank] = i
 
     def arrange(i, carry):
@@ -79,23 +80,30 @@
         return carry
 
     lax.fori_loop(0, nr, arrange, 0)
-    for c in large:
-        c.wait()
+    outs = [pltpu.make_async_copy(dqo.at[b], dq_hbm[b], osem.at[b]) for b in range(nb)]
 
     def query_half(qi, carry):
         b = qi // 2
+        for i in range(nb):
+
+            @pl.when(qi == 2 * i)
+            def _():
+                large[i].wait()
+
         qrun = qrun_s[qi]
         reach = jnp.int32(0)
+        before = jnp.int32(0)
         for j in range(nr):
             reach = reach + (krun[j] <= qrun).astype(jnp.int32)
+            before = before + (krun[j] < qrun).astype(jnp.int32)
         off = pl.multiple_of((qi % 2) * rows, rows)
         dqt[...] = jnp.zeros_like(dqt)
 
-        def visit(p, masked):
-            at = pl.multiple_of(p * BLK, BLK)
-            kp = ks[pl.ds(at, BLK), :]
-            vp = vs[pl.ds(at, BLK), :]
-            kt = jnp.concatenate([kts[p, 0], kts[p, 1]], axis=1)
+        def visit(p, masked, runs=2):
+            keys = pl.ds(pl.multiple_of(p * BLK, BLK), runs * RUN)
+            kp = ks[keys, :]
+            vp = vs[keys, :]
+            kt = jnp.concatenate([kts[p + i // 2, i % 2] for i in range(runs)], axis=1)
             if masked:
                 first = krun[order[2 * p]] * RUN
                 second = krun[order[2 * p + 1]] * RUN
@@ -103,8 +111,8 @@
                 kpos = jnp.where(ii < RUN, ii + first, ii - RUN + second)
                 jj = lax.broadcasted_iota(jnp.int32, (1, rows), 1)
                 seen = kpos <= jj // QPK + qrun * RUN
-            dk = acck[p]
-            dv = accv[p]
+            dk = acck[keys, :]
+            dv = accv[keys, :]
             for l in range(layers):
                 q = qds[b, 0, l, pl.ds(off, rows), :]
                 do = qds[b, 1, l, pl.ds(off, rows), :]
@@ -115,12 +123,12 @@
                 if masked:
                     probs = jnp.where(seen, probs, 0.0)
                 dprobs = lax.dot_general(vp, do, NT, preferred_element_type=F32)
-                dscore = (probs * (dprobs - delta)).astype(BF16)
+                dscore = ((probs * SCALING) * (dprobs - delta)).astype(BF16)
                 dv = dv + lax.dot_general(probs.astype(BF16), do, NN, preferred_element_type=F32)
                 dk = dk + lax.dot_general(dscore, q, NN, preferred_element_type=F32)
                 dqt[l] += lax.dot_general(kt, dscore, NN, preferred_element_type=F32)
-            acck[p] = dk
-            accv[p] = dv
+            acck[keys, :] = dk
+            accv[keys, :] = dv
 
         def step(p, inner):
             full = krun[order[2 * p + 1]] < qrun
@@ -135,26 +143,35 @@
 
             return inner
 
-        lax.fori_loop(0, (reach + 1) // 2, step, 0)
+        def wide_step(p, inner):
+            visit(p * (WIDE // 2), False, WIDE)
+            return inner
+
+        wide = before // WIDE
+        lax.fori_loop(0, wide, wide_step, 0)
+        lax.fori_loop(wide * (WIDE // 2), (reach + 1) // 2, step, 0)
         for l in range(layers):
-            dqo[b, l, pl.ds(off, rows), :] = (dqt[l] * SCALING).T.astype(BF16)
+            dqo[b, l, pl.ds(off, rows), :] = dqt[l].T.astype(BF16)
+        for i in range(nb):
+
+            @pl.when(qi == 2 * i + 1)
+            def _():
+                outs[i].start()
+
         return carry
 
     lax.fori_loop(0, 2 * nb, query_half, 0)
 
     def settle(i, carry):
         s = order[i]
-        at = pl.multiple_of((i % 2) * RUN, RUN)
+        at = pl.multiple_of(i * RUN, RUN)
         to = pl.multiple_of((s % 2) * RUN, RUN)
-        k_sum = acck[i // 2, pl.ds(at, RUN), :] * SCALING
-        v_sum = accv[i // 2, pl.ds(at, RUN), :]
+        k_sum = acck[pl.ds(at, RUN), :]
+        v_sum = accv[pl.ds(at, RUN), :]
         dkvo[s // 2, pl.ds(to, RUN), 0:HD] = k_sum.astype(BF16)
         dkvo[s // 2, pl.ds(to, RUN), HD : 2 * HD] = v_sum.astype(BF16)
         return carry
 
-    outs = [pltpu.make_async_copy(dqo.at[b], dq_hbm[b], osem.at[b]) for b in range(nb)]
-    for c in outs:
-        c.start()
     lax.fori_loop(0, nr, settle, 0)
     outs.append(pltpu.make_async_copy(dkvo, dkv_hbm, osem.at[nb]))
     outs[-1].start()
@@ -170,7 +187,7 @@
     operands = list(queries) + list(auxes) + list(keys)
     units = nb * m * 2
     any_spec = pl.BlockSpec(memory_space=pl.ANY)
-    acc_shape = (m, BLK, HD)
+    acc_shape = (m * BLK, HD)
     out_shape = [jax.ShapeDtypeStruct(q_shape, BF16)] * nb
     out_shape += [jax.ShapeDtypeStruct((m, BLK, 2 * HD), BF16)]
     outs = pl.pallas_call(
@@ -207,39 +224,28 @@
     return outs
 
 
-def tail_kernel(core_ref, mine_hbm, other_hbm, grads_hbm, out_ref, w, grads, sem):
-    core = core_ref[0]
-    heads = mine_hbm.shape[0]
-    copies = []
-    for g in range(heads):
-        first = pl.multiple_of((2 * g + core) * HD, HD)
-        second = pl.multiple_of((2 * g + 1 - core) * HD, HD)
-        both = slice(2 * g * HD, 2 * (g + 1) * HD)
-        copies.append(pltpu.make_async_copy(mine_hbm.at[g], w.at[:, pl.ds(first, HD)], sem.at[0, g]))
-        copies.append(pltpu.make_async_copy(other_hbm.at[g], w.at[:, pl.ds(second, HD)], sem.at[1, g]))
-        copies.append(pltpu.make_async_copy(grads_hbm.at[g], grads.at[:, both], sem.at[2, g]))
-    for c in copies:
-        c.start()
-    for c in copies:
-        c.wait()
-    out_ref[...] = lax.dot_general(w[...], grads[...], NT, preferred_element_type=F32).astype(out_ref.dtype)
+def tail_kernel(core_ref, mine_ref, other_ref, grads_ref, out_ref):
+    first = core_ref[0] == 0
+    total = jnp.zeros(out_ref.shape, F32)
+    for g in range(mine_ref.shape[0]):
+        w = jnp.concatenate([mine_ref[g], other_ref[g]], axis=1)
+        key, value = grads_ref[g, :, :HD], grads_ref[g, :, HD:]
+        mine, other = jnp.where(first, key, value), jnp.where(first, value, key)
+        grads = jnp.concatenate([mine, other], axis=1)
+        total = total + lax.dot_general(w, grads, NT, preferred_element_type=F32)
+    out_ref[...] = total.astype(out_ref.dtype)
 
 
 def tail(core, mine, other, grads):
     heads, features, _ = mine.shape
     tokens = grads.shape[1]
-    any_spec = pl.BlockSpec(memory_space=pl.ANY)
+    vm = pl.BlockSpec(memory_space=pltpu.VMEM)
     return pl.pallas_call(
         tail_kernel,
         out_shape=jax.ShapeDtypeStruct((features, tokens), BF16),
-        in_specs=[pl.BlockSpec(memory_space=pltpu.SMEM), any_spec, any_spec, any_spec],
-        out_specs=pl.BlockSpec(memory_space=pltpu.VMEM),
-        scratch_shapes=[
-            pltpu.VMEM((features, 2 * heads * HD), BF16),
-            pltpu.VMEM((tokens, 2 * heads * HD), BF16),
-            pltpu.SemaphoreType.DMA((3, heads)),
-        ],
-        compiler_params=pltpu.CompilerParams(vmem_limit_bytes=60 * 2**20),
+        in_specs=[pl.BlockSpec(memory_space=pltpu.SMEM), vm, vm, vm],
+        out_specs=vm,
+        compiler_params=pltpu.CompilerParams(vmem_limit_bytes=24 * 2**20),
         cost_estimate=pl.CostEstimate(
             flops=4 * features * tokens * heads * HD, bytes_accessed=6 * 2**20, transcendentals=0
         ),

time: 142 us -> 136 us (0.958)
  Pallas kernels: 39.2 us -> 35 us
  waiting for transfers between devices: 41.9 us -> 40.2 us
    pallas_call x1, Pallas kernels: 34.5 us -> 31.4 us  [visits(): pl.pallas_call(functools.partial(visits_kernel, nb=nb, m=m), out_shape=ou...]
    ppermute x16, starting transfers between devices: 19.8 us -> 22 us  [moved(): lax.ppermute(value, axis, [(i, (i + distance) % size) for i in range(size)])]
  transfers between devices with their start and end apart: 19 -> 19, of which waited for: 6 -> 6; matrix products, arithmetic and copies ran while one was open for 8% -> 9% of each run, Pallas kernels for 24% -> 23%
where the time goes in v3:
time: 136 us; the launch traced here: 135 us
  starting transfers between devices  42.9 us (32%)
  waiting for transfers between devices  40.2 us (30%)
  Pallas kernels  35 us (26%)
  other arithmetic  11.6 us (9%)
  local copies, waits for them, and re-layouts  4.19 us (3%)
    pallas_call x1, Pallas kernels, visits(): pl.pallas_call(functools.partial(visits_kernel, nb=nb, m=m), out_shape=ou...  31.4 us
    all_to_all x1, waiting for transfers between devices, on_device(): back = lax.all_to_all(dkv, 'z', 0, 0, tiled=True)  22.9 us
    ppermute x16, starting transfers between devices, moved(): lax.ppermute(value, axis, [(i, (i + distance) % size) for i in range(size)])  22 us
    all_to_all x1, waiting for transfers between devices, on_device(): lax.all_to_all(jnp.broadcast_to(grads[None], (8,) + grads.shape), HEAD, 0...  11.4 us
    all_to_all x1, starting transfers between devices, on_device(): back = lax.all_to_all(dkv, 'z', 0, 0, tiled=True)  7.66 us
    all_to_all x1, starting transfers between devices, on_device(): mine = lax.all_to_all(jnp.where(core == 0, kw, vw), HEAD, 0, 0, tiled=True)  6.68 us
    all_to_all x1, starting transfers between devices, on_device(): lax.all_to_all(jnp.broadcast_to(grads[None], (8,) + grads.shape), HEAD, 0...  6.59 us
    ppermute x16, waiting for transfers between devices, moved(): lax.ppermute(value, axis, [(i, (i + distance) % size) for i in range(size)])  5.9 us
  transfers between devices with their start and end apart: 19, of which 6 were waited for; matrix products, arithmetic and copies ran while one was open for 9% of the time, Pallas kernels for 23%

profile of v3, /device:TPU:1, one launch (start us, length us, event | category | flops | bytes accessed | tf_op | source)
XLA Modules:
  0.0 134.9 jit_solution(10076457701371129950)
XLA Ops:
  0.6 0.0 copy-start.12
  0.7 2.4 %pad_maximum_fusion.refs_1_ = bf16[2,2,1024,128]{3,2,1,0:T(8,128)(2,1)} fusion(bf16[1,2,1024,128]{3,2,1,0:T(8,128)(2,1)} %bitcast.20, bf16[1,2,1024,128]{3,2,1,0:T(8,128)(2,1)} %bitcast.21), kind=kLoop, calls=%fused_computation.1 | loop fusion | flops 524288 | bytes 2097152 | tf_op jit(solution)/shard_map/stack | solution.py:283
  3.1 2.0 %collective-permute-start.1 = (bf16[2,2,1024,128]{3,2,1,0:T(8,128)(2,1)}, bf16[2,2,1024,128]{3,2,1,0:T(8,128)(2,1)}, u32[]{:S(2)}, u32[]{:S(2)}) collective-permute-start(bf16[2,2,1024,128]{3,2,1,0:T(8,128)(2,1)} %pad_maximum_fusion.refs_1_), channel_id=1, source_target_pairs={{0,128},{128,0},{1,129},{129,1},{2,130},{130,2},{3,131},{131,3},{4... | collective-permute-start | bytes 3145736 | tf_op jit(solution)/shard_map/ppermute | solution.py:258
  5.2 0.1 slice_reduce_fusion
  5.3 0.1 broadcast_in_dim.36
  5.4 0.1 reshape.69
  5.5 0.1 maximum_maximum_fusion.refs_8_
  5.6 1.7 %collective-permute-start.5 = (bf16[272,256]{1,0:T(8,128)(2,1)S(1)}, bf16[272,256]{1,0:T(8,128)(2,1)}, u32[]{:S(2)}, u32[]{:S(2)}) collective-permute-start(bf16[272,256]{1,0:T(8,128)(2,1)S(1)} %maximum_maximum_fusion.refs_8_), channel_id=1, source_target_pairs={{0,16},{16,32},{32,48},{48,64},{64,80},{80,96},{96,112},{112,0},{1... | collective-permute-start | bytes 417800 | tf_op jit(solution)/shard_map/ppermute | solution.py:258
  7.3 4.0 %collective-permute-start.9 = (bf16[272,256]{1,0:T(8,128)(2,1)S(1)}, bf16[272,256]{1,0:T(8,128)(2,1)}, u32[]{:S(2)}, u32[]{:S(2)}) collective-permute-start(bf16[272,256]{1,0:T(8,128)(2,1)S(1)} %maximum_maximum_fusion.refs_8_), channel_id=1, source_target_pairs={{0,112},{16,0},{32,16},{48,32},{64,48},{80,64},{96,80},{112,96},{1... | collective-permute-start | bytes 417800 | tf_op jit(solution)/shard_map/ppermute | solution.py:258
  11.3 3.1 %collective-permute-done.5.refs_9_ = bf16[272,256]{1,0:T(8,128)(2,1)} collective-permute-done((bf16[272,256]{1,0:T(8,128)(2,1)S(1)}, bf16[272,256]{1,0:T(8,128)(2,1)}, u32[]{:S(2)}, u32[]{:S(2)}) %collective-permute-start.5) | collective-permute-done | bytes 139296 | tf_op jit(solution)/shard_map/ppermute | solution.py:258
  14.4 2.7 %collective-permute-start.10 = (bf16[272,256]{1,0:T(8,128)(2,1)}, bf16[272,256]{1,0:T(8,128)(2,1)}, u32[]{:S(2)}, u32[]{:S(2)}) collective-permute-start(bf16[272,256]{1,0:T(8,128)(2,1)} %collective-permute-done.9.refs_15_), channel_id=1, source_target_pairs={{0,112},{16,0},{32,16},{48,32},{64,48},{80,64},{96,80},{112,96},{1... | collective-permute-start | bytes 417800 | tf_op jit(solution)/shard_map/ppermute | solution.py:258
  17.1 0.6 multiply_reduce_fusion
  17.8 0.1 copy.15
  17.9 0.2 mul.18
  18.1 0.2 reshape.63
  18.3 0.8 convert_reduce_fusion
  19.1 0.8 collective-permute-done.6.refs_10_
  19.9 2.7 %collective-permute-start.11 = (bf16[272,256]{1,0:T(8,128)(2,1)}, bf16[272,256]{1,0:T(8,128)(2,1)S(1)}, u32[]{:S(2)}, u32[]{:S(2)}) collective-permute-start(bf16[272,256]{1,0:T(8,128)(2,1)} %collective-permute-done.10.refs_14_), channel_id=1, source_target_pairs={{0,112},{16,0},{32,16},{48,32},{64,48},{80,64},{96,80},{112,96},{1... | collective-permute-start | bytes 417800 | tf_op jit(solution)/shard_map/ppermute | solution.py:258
  22.6 0.1 broadcast_in_dim.34
  22.6 0.0 copy-start.6
  22.7 3.3 %collective-permute-start.3 = (f32[8,1024]{1,0:T(8,128)S(1)}, f32[8,1024]{1,0:T(8,128)S(1)}, u32[]{:S(2)}, u32[]{:S(2)}) collective-permute-start(f32[8,1024]{1,0:T(8,128)S(1)} %pad_maximum_fusion.1.refs_5_), channel_id=1, source_target_pairs={{0,8},{8,0},{1,9},{9,1},{2,10},{10,2},{3,11},{11,3},{4,12},{12,4},... | collective-permute-start | bytes 98312 | tf_op jit(solution)/shard_map/ppermute | solution.py:258
  26.0 0.1 collective-permute-start
  26.1 0.8 collective-permute-done.3.refs_6_
  26.9 0.3 collective-permute-start.4
  27.3 0.1 collective-permute-start.8
  27.3 0.6 copy-done.10
  27.9 1.9 %collective-permute-start.2 = (bf16[2,2,1024,128]{3,2,1,0:T(8,128)(2,1)}, bf16[2,2,1024,128]{3,2,1,0:T(8,128)(2,1)S(1)}, u32[]{:S(2)}, u32[]{:S(2)}) collective-permute-start(bf16[2,2,1024,128]{3,2,1,0:T(8,128)(2,1)} %collective-permute-done.1.refs_3_), channel_id=1, source_target_pairs={{0,8},{8,0},{1,9},{9,1},{2,10},{10,2},{3,11},{11,3},{4,12},{12,4},... | collective-permute-start | bytes 3145736 | tf_op jit(solution)/shard_map/ppermute | solution.py:258
  29.8 3.1 %broadcast_select_fusion = bf16[8192,128]{1,0:T(8,128)(2,1)} fusion(bf16[8192,128]{1,0:T(8,128)(2,1)S(1)} %bitcast.18, bf16[8192,128]{1,0:T(8,128)(2,1)} %bitcast.19, pred[]{:T(512)S(6)} %eq.3), kind=kLoop, calls=%fused_computation | loop fusion | flops 1048576 | bytes 6291457 | tf_op jit(solution)/shard_map/jit(_where)/select_n | solution.py:294
  33.0 6.7 %all-to-all-start.1 = ((bf16[8,1024,128]{2,1,0:T(8,128)(2,1)}), bf16[8,1024,128]{2,1,0:T(8,128)(2,1)S(1)}, u32[]{:S(2)}, u32[]{:S(2)}) async-start(bf16[8,1024,128]{2,1,0:T(8,128)(2,1)} %bitcast.17), calls=%async_computation.1 | async-start | bytes 4194304 | tf_op jit(solution)/shard_map/all_to_all | solution.py:294
  39.7 0.0 copy-start.11
  39.7 0.6 copy-done.11
  40.3 0.4 copy-done.9
  40.7 31.4 %visits.1 = (bf16[2,1024,128]{2,1,0:T(8,128)(2,1)}, bf16[2,1024,128]{2,1,0:T(8,128)(2,1)}, bf16[2,1024,128]{2,1,0:T(8,128)(2,1)}, bf16[2,1024,128]{2,1,0:T(8,128)(2,1)}, bf16[8,256,256]{2,1,0:T(8,128)(2,1)}) custom-call(s32[1]{0:T(128)} %bitcast.refs_0_, bf16[2,2,1024,128]{3,2,1,0:T(8,128)(2,1)} %pad_maximum_fusion.refs_1_, ...), custom_call_target="tpu_custom_call" | custom-call | flops 21474836480 | bytes 12582912 | tf_op jit(solution)/shard_map/visits/pallas_call | solution.py:193
  72.1 7.7 %all-to-all-start = ((bf16[8,256,256]{2,1,0:T(8,128)(2,1)}), bf16[8,256,256]{2,1,0:T(8,128)(2,1)S(1)}, u32[]{:S(2)}, u32[]{:S(2)}) async-start(bf16[8,256,256]{2,1,0:T(8,128)(2,1)} %get-tuple-element.15), calls=%async_computation | async-start | bytes 2097152 | tf_op jit(solution)/shard_map/all_to_all | solution.py:304
  79.7 0.7 collective-permute-start.12
  80.4 0.1 collective-permute-start.15
  80.5 0.4 collective-permute-start.14
  80.9 1.2 collective-permute-done.12
  82.2 2.0 %add_convert_fusion.1 = bf16[2,1024,128]{2,1,0:T(8,128)(2,1)} fusion(bf16[2,1024,128]{2,1,0:T(8,128)(2,1)S(1)} %collective-permute-done.12, bf16[2,1024,128]{2,1,0:T(8,128)(2,1)} %get-tuple-element.16), kind=kLoop, calls=%fused_computation.3 | loop fusion | flops 1048576 | bytes 1572864 | tf_op jit(solution)/shard_map/convert_element_type | solution.py:308
  84.2 1.9 %collective-permute-start.13 = (bf16[2,1024,128]{2,1,0:T(8,128)(2,1)}, bf16[2,1024,128]{2,1,0:T(8,128)(2,1)}, u32[]{:S(2)}, u32[]{:S(2)}) collective-permute-start(bf16[2,1024,128]{2,1,0:T(8,128)(2,1)} %add_convert_fusion.1), channel_id=1, source_target_pairs={{0,128},{128,0},{1,129},{129,1},{2,130},{130,2},{3,131},{131,3},{4... | collective-permute-start | bytes 1572872 | tf_op jit(solution)/shard_map/ppermute | solution.py:258
  86.0 22.9 %all-to-all-done = bf16[8,256,256]{2,1,0:T(8,128)(2,1)S(1)} async-done(((bf16[8,256,256]{2,1,0:T(8,128)(2,1)}), bf16[8,256,256]{2,1,0:T(8,128)(2,1)S(1)}, u32[]{:S(2)}, u32[]{:S(2)}) %all-to-all-start) | async-done | bytes 1048608 | tf_op jit(solution)/shard_map/all_to_all | solution.py:304
  109.0 0.1 reduce_sum.22
  109.2 1.1 broadcast_in_dim.41
  110.2 6.6 %all-to-all-start.2 = ((bf16[8,256,256]{2,1,0:T(8,128)(2,1)}), bf16[8,256,256]{2,1,0:T(8,128)(2,1)S(1)}, u32[]{:S(2)}, u32[]{:S(2)}) async-start(bf16[8,256,256]{2,1,0:T(8,128)(2,1)} %broadcast_in_dim.41), calls=%async_computation.2 | async-start | bytes 2097152 | tf_op jit(solution)/shard_map/all_to_all | solution.py:314
  116.8 0.7 slice_bitcast_fusion
  117.5 2.4 %add_convert_fusion = bf16[2,1024,128]{2,1,0:T(8,128)(2,1)} fusion(bf16[2,1024,128]{2,1,0:T(8,128)(2,1)} %collective-permute-done.13, bf16[2,1024,128]{2,1,0:T(8,128)(2,1)} %collective-permute-done.14, bf16[2,1024,128]{2,1,0:T(8,128)(2,1)} %get-tuple-element.14), kind=kLoop, calls=%fused_computation.2 | loop fusion | flops 1572864 | bytes 2097152 | tf_op jit(solution)/shard_map/convert_element_type | solution.py:311
  119.8 11.4 %all-to-all-done.2.grads_ref = bf16[8,256,256]{2,1,0:T(8,128)(2,1)S(1)} async-done(((bf16[8,256,256]{2,1,0:T(8,128)(2,1)}), bf16[8,256,256]{2,1,0:T(8,128)(2,1)S(1)}, u32[]{:S(2)}, u32[]{:S(2)}) %all-to-all-start.2) | async-done | bytes 1048608 | tf_op jit(solution)/shard_map/all_to_all | solution.py:314
  131.2 3.7 %input_grad.1 = bf16[1024,256]{1,0:T(8,128)(2,1)} custom-call(s32[1]{0:T(128)} %bitcast.10.core_ref, bf16[8,1024,128]{2,1,0:T(8,128)(2,1)S(1)} %all-to-all-done.1.mine_ref, bf16[8,1024,128]{2,1,0:T(8,128)(2,1)} %collective-permute-done.15.other_ref, bf16[8,256,256]{2,1,0:T(8,128)(2,1)S(1)} %all-to-all-done.2.grads_ref), custom_call_target="tpu_custom_call" | custom-call | flops 1073741824 | bytes 6291456 | tf_op jit(solution)/shard_map/input_grad/pallas_call | solution.py:243
  (41 shorter events, 0.2 us)
Async XLA Ops:
  0.6 16.5 %copy-start.1 = (bf16[2,256,4,128]{3,2,1,0:T(4,128)(2,1)S(1)}, bf16[2,256,4,128]{3,2,1,0:T(4,128)(2,1)}, u32[]{:S(2)}) copy-start(bf16[2,256,4,128]{3,2,1,0:T(4,128)(2,1)} %param.13) | copy-start | bytes 1572868
  0.6 4.5 %copy-start.12 = (s32[256]{0:T(256)S(1)}, s32[256]{0:T(256)}, u32[]{:S(2)}) copy-start(s32[256]{0:T(256)} %param.15) | copy-start | bytes 3076
  0.7 4.8 %copy-start.5 = (bf16[256,1,128]{2,0,1:T(8,128)(2,1)S(1)}, bf16[256,1,128]{2,0,1:T(8,128)(2,1)}, u32[]{:S(2)}) copy-start(bf16[256,1,128]{2,0,1:T(8,128)(2,1)} %param.10) | copy-start | bytes 196612
  0.7 4.8 %copy-start.4 = (bf16[256,1,128]{2,0,1:T(8,128)(2,1)S(1)}, bf16[256,1,128]{2,0,1:T(8,128)(2,1)}, u32[]{:S(2)}) copy-start(bf16[256,1,128]{2,0,1:T(8,128)(2,1)} %param.11) | copy-start | bytes 196612
  0.7 10.7 %copy-start.8 = (f32[2,4,256]{2,1,0:T(4,128)S(1)}, f32[2,4,256]{2,1,0:T(4,128)}, u32[]{:S(2)}) copy-start(f32[2,4,256]{2,1,0:T(4,128)} %param.14) | copy-start | bytes 24580
  0.7 16.4 %copy-start.2 = (bf16[2,256,4,128]{3,2,1,0:T(4,128)(2,1)S(1)}, bf16[2,256,4,128]{3,2,1,0:T(4,128)(2,1)}, u32[]{:S(2)}) copy-start(bf16[2,256,4,128]{3,2,1,0:T(4,128)(2,1)} %param.12) | copy-start | bytes 1572868
  0.7 29.1 %copy-start = (bf16[8192,1,128]{2,0,1:T(8,128)(2,1)S(1)}, bf16[8192,1,128]{2,0,1:T(8,128)(2,1)}, u32[]{:S(2)}) copy-start(bf16[8192,1,128]{2,0,1:T(8,128)(2,1)} %param.16) | copy-start | bytes 6291460
  3.1 24.8 %collective-permute-start.1 = (bf16[2,2,1024,128]{3,2,1,0:T(8,128)(2,1)}, bf16[2,2,1024,128]{3,2,1,0:T(8,128)(2,1)}, u32[]{:S(2)}, u32[]{:S(2)}) collective-permute-start(bf16[2,2,1024,128]{3,2,1,0:T(8,128)(2,1)} %pad_maximum_fusion.refs_1_), channel_id=1, source_target_pairs={{0,128},{128,0},{1,129},{129,1},{2,130},{130,2},{3,131},{131,3},{4... | collective-permute-start | bytes 3145736 | tf_op jit(solution)/shard_map/ppermute | solution.py:258
  5.6 27.4 %copy-start.3 = (bf16[272,256]{1,0:T(8,128)(2,1)}, bf16[272,256]{1,0:T(8,128)(2,1)S(1)}, u32[]{:S(2)}) copy-start(bf16[272,256]{1,0:T(8,128)(2,1)S(1)} %maximum_maximum_fusion.refs_8_) | copy-start | bytes 417796
  5.6 8.8 %collective-permute-start.5 = (bf16[272,256]{1,0:T(8,128)(2,1)S(1)}, bf16[272,256]{1,0:T(8,128)(2,1)}, u32[]{:S(2)}, u32[]{:S(2)}) collective-permute-start(bf16[272,256]{1,0:T(8,128)(2,1)S(1)} %maximum_maximum_fusion.refs_8_), channel_id=1, source_target_pairs={{0,16},{16,32},{32,48},{48,64},{64,80},{80,96},{96,112},{112,0},{1... | collective-permute-start | bytes 417800 | tf_op jit(solution)/shard_map/ppermute | solution.py:258
  7.3 7.1 %collective-permute-start.9 = (bf16[272,256]{1,0:T(8,128)(2,1)S(1)}, bf16[272,256]{1,0:T(8,128)(2,1)}, u32[]{:S(2)}, u32[]{:S(2)}) collective-permute-start(bf16[272,256]{1,0:T(8,128)(2,1)S(1)} %maximum_maximum_fusion.refs_8_), channel_id=1, source_target_pairs={{0,112},{16,0},{32,16},{48,32},{64,48},{80,64},{96,80},{112,96},{1... | collective-permute-start | bytes 417800 | tf_op jit(solution)/shard_map/ppermute | solution.py:258
  14.4 5.4 %collective-permute-start.6 = (bf16[272,256]{1,0:T(8,128)(2,1)}, bf16[272,256]{1,0:T(8,128)(2,1)}, u32[]{:S(2)}, u32[]{:S(2)}) collective-permute-start(bf16[272,256]{1,0:T(8,128)(2,1)} %collective-permute-done.5.refs_9_), channel_id=1, source_target_pairs={{0,16},{16,32},{32,48},{48,64},{64,80},{80,96},{96,112},{112,0},{1... | collective-permute-start | bytes 417800 | tf_op jit(solution)/shard_map/ppermute | solution.py:258
  14.4 5.4 %collective-permute-start.10 = (bf16[272,256]{1,0:T(8,128)(2,1)}, bf16[272,256]{1,0:T(8,128)(2,1)}, u32[]{:S(2)}, u32[]{:S(2)}) collective-permute-start(bf16[272,256]{1,0:T(8,128)(2,1)} %collective-permute-done.9.refs_15_), channel_id=1, source_target_pairs={{0,112},{16,0},{32,16},{48,32},{64,48},{80,64},{96,80},{112,96},{1... | collective-permute-start | bytes 417800 | tf_op jit(solution)/shard_map/ppermute | solution.py:258
  19.9 7.4 %collective-permute-start.7 = (bf16[272,256]{1,0:T(8,128)(2,1)}, bf16[272,256]{1,0:T(8,128)(2,1)}, u32[]{:S(2)}, u32[]{:S(2)}) collective-permute-start(bf16[272,256]{1,0:T(8,128)(2,1)} %collective-permute-done.6.refs_10_), channel_id=1, source_target_pairs={{0,16},{16,32},{32,48},{48,64},{64,80},{80,96},{96,112},{112,0},{1... | collective-permute-start | bytes 417800 | tf_op jit(solution)/shard_map/ppermute | solution.py:258
  19.9 7.4 %collective-permute-start.11 = (bf16[272,256]{1,0:T(8,128)(2,1)}, bf16[272,256]{1,0:T(8,128)(2,1)S(1)}, u32[]{:S(2)}, u32[]{:S(2)}) collective-permute-start(bf16[272,256]{1,0:T(8,128)(2,1)} %collective-permute-done.10.refs_14_), channel_id=1, source_target_pairs={{0,112},{16,0},{32,16},{48,32},{64,48},{80,64},{96,80},{112,96},{1... | collective-permute-start | bytes 417800 | tf_op jit(solution)/shard_map/ppermute | solution.py:258
  22.6 10.3 %copy-start.6 = (f32[8,1024]{1,0:T(8,128)}, f32[8,1024]{1,0:T(8,128)S(1)}, u32[]{:S(2)}) copy-start(f32[8,1024]{1,0:T(8,128)S(1)} %pad_maximum_fusion.1.refs_5_) | copy-start | bytes 98308
  22.7 4.2 %collective-permute-start.3 = (f32[8,1024]{1,0:T(8,128)S(1)}, f32[8,1024]{1,0:T(8,128)S(1)}, u32[]{:S(2)}, u32[]{:S(2)}) collective-permute-start(f32[8,1024]{1,0:T(8,128)S(1)} %pad_maximum_fusion.1.refs_5_), channel_id=1, source_target_pairs={{0,8},{8,0},{1,9},{9,1},{2,10},{10,2},{3,11},{11,3},{4,12},{12,4},... | collective-permute-start | bytes 98312 | tf_op jit(solution)/shard_map/ppermute | solution.py:258
  26.0 13.7 %collective-permute-start = (bf16[2,2,1024,128]{3,2,1,0:T(8,128)(2,1)}, bf16[2,2,1024,128]{3,2,1,0:T(8,128)(2,1)}, u32[]{:S(2)}, u32[]{:S(2)}) collective-permute-start(bf16[2,2,1024,128]{3,2,1,0:T(8,128)(2,1)} %pad_maximum_fusion.refs_1_), channel_id=1, source_target_pairs={{0,8},{8,0},{1,9},{9,1},{2,10},{10,2},{3,11},{11,3},{4,12},{12,4},... | collective-permute-start | bytes 3145736 | tf_op jit(solution)/shard_map/ppermute | solution.py:258
  26.9 6.1 %copy-start.7 = (f32[8,1024]{1,0:T(8,128)}, f32[8,1024]{1,0:T(8,128)S(1)}, u32[]{:S(2)}) copy-start(f32[8,1024]{1,0:T(8,128)S(1)} %collective-permute-done.3.refs_6_) | copy-start | bytes 98308
  26.9 12.8 %collective-permute-start.4 = (f32[16,1024]{1,0:T(8,128)S(1)}, f32[16,1024]{1,0:T(8,128)S(1)}, u32[]{:S(2)}, u32[]{:S(2)}) collective-permute-start(f32[16,1024]{1,0:T(8,128)S(1)} %concatenate.14), channel_id=1, source_target_pairs={{0,128},{128,0},{1,129},{129,1},{2,130},{130,2},{3,131},{131,3},{4... | collective-permute-start | bytes 196616 | tf_op jit(solution)/shard_map/ppermute | solution.py:258
  27.3 0.7 copy-start.10
  27.3 12.4 %collective-permute-start.8 = (bf16[272,256]{1,0:T(8,128)(2,1)}, bf16[272,256]{1,0:T(8,128)(2,1)}, u32[]{:S(2)}, u32[]{:S(2)}) collective-permute-start(bf16[272,256]{1,0:T(8,128)(2,1)} %collective-permute-done.7.refs_11_), channel_id=1, source_target_pairs={{0,16},{16,32},{32,48},{48,64},{64,80},{80,96},{96,112},{112,0},{1... | collective-permute-start | bytes 417800 | tf_op jit(solution)/shard_map/ppermute | solution.py:258
  27.9 11.8 %collective-permute-start.2 = (bf16[2,2,1024,128]{3,2,1,0:T(8,128)(2,1)}, bf16[2,2,1024,128]{3,2,1,0:T(8,128)(2,1)S(1)}, u32[]{:S(2)}, u32[]{:S(2)}) collective-permute-start(bf16[2,2,1024,128]{3,2,1,0:T(8,128)(2,1)} %collective-permute-done.1.refs_3_), channel_id=1, source_target_pairs={{0,8},{8,0},{1,9},{9,1},{2,10},{10,2},{3,11},{11,3},{4,12},{12,4},... | collective-permute-start | bytes 3145736 | tf_op jit(solution)/shard_map/ppermute | solution.py:258
  33.0 39.1 %all-to-all-start.1 = ((bf16[8,1024,128]{2,1,0:T(8,128)(2,1)}), bf16[8,1024,128]{2,1,0:T(8,128)(2,1)S(1)}, u32[]{:S(2)}, u32[]{:S(2)}) async-start(bf16[8,1024,128]{2,1,0:T(8,128)(2,1)} %bitcast.17), calls=%async_computation.1 | async-start | bytes 4194304 | tf_op jit(solution)/shard_map/all_to_all | solution.py:294
  39.7 0.6 copy-start.11
  39.7 1.0 copy-start.9
  72.1 36.9 %all-to-all-start = ((bf16[8,256,256]{2,1,0:T(8,128)(2,1)}), bf16[8,256,256]{2,1,0:T(8,128)(2,1)S(1)}, u32[]{:S(2)}, u32[]{:S(2)}) async-start(bf16[8,256,256]{2,1,0:T(8,128)(2,1)} %get-tuple-element.15), calls=%async_computation | async-start | bytes 2097152 | tf_op jit(solution)/shard_map/all_to_all | solution.py:304
  79.7 2.4 %collective-permute-start.12 = (bf16[2,1024,128]{2,1,0:T(8,128)(2,1)}, bf16[2,1024,128]{2,1,0:T(8,128)(2,1)S(1)}, u32[]{:S(2)}, u32[]{:S(2)}) collective-permute-start(bf16[2,1024,128]{2,1,0:T(8,128)(2,1)} %get-tuple-element.17), channel_id=1, source_target_pairs={{0,8},{8,0},{1,9},{9,1},{2,10},{10,2},{3,11},{11,3},{4,12},{12,4},... | collective-permute-start | bytes 1572872 | tf_op jit(solution)/shard_map/ppermute | solution.py:258
  80.4 39.4 %collective-permute-start.15 = (bf16[8,1024,128]{2,1,0:T(8,128)(2,1)S(1)}, bf16[8,1024,128]{2,1,0:T(8,128)(2,1)}, u32[]{:S(2)}, u32[]{:S(2)}) collective-permute-start(bf16[8,1024,128]{2,1,0:T(8,128)(2,1)S(1)} %all-to-all-done.1.mine_ref), channel_id=1, source_target_pairs={{0,8},{8,0},{1,9},{9,1},{2,10},{10,2},{3,11},{11,3},{4,12},{12,4},... | collective-permute-start | bytes 6291464 | tf_op jit(solution)/shard_map/ppermute | solution.py:258
  80.5 28.6 %collective-permute-start.14 = (bf16[2,1024,128]{2,1,0:T(8,128)(2,1)}, bf16[2,1024,128]{2,1,0:T(8,128)(2,1)}, u32[]{:S(2)}, u32[]{:S(2)}) collective-permute-start(bf16[2,1024,128]{2,1,0:T(8,128)(2,1)} %get-tuple-element.18), channel_id=1, source_target_pairs={{0,8},{8,0},{1,9},{9,1},{2,10},{10,2},{3,11},{11,3},{4,12},{12,4},... | collective-permute-start | bytes 1572872 | tf_op jit(solution)/shard_map/ppermute | solution.py:258
  84.2 25.0 %collective-permute-start.13 = (bf16[2,1024,128]{2,1,0:T(8,128)(2,1)}, bf16[2,1024,128]{2,1,0:T(8,128)(2,1)}, u32[]{:S(2)}, u32[]{:S(2)}) collective-permute-start(bf16[2,1024,128]{2,1,0:T(8,128)(2,1)} %add_convert_fusion.1), channel_id=1, source_target_pairs={{0,128},{128,0},{1,129},{129,1},{2,130},{130,2},{3,131},{131,3},{4... | collective-permute-start | bytes 1572872 | tf_op jit(solution)/shard_map/ppermute | solution.py:258
  110.2 21.0 %all-to-all-start.2 = ((bf16[8,256,256]{2,1,0:T(8,128)(2,1)}), bf16[8,256,256]{2,1,0:T(8,128)(2,1)S(1)}, u32[]{:S(2)}, u32[]{:S(2)}) async-start(bf16[8,256,256]{2,1,0:T(8,128)(2,1)} %broadcast_in_dim.41), calls=%async_computation.2 | async-start | bytes 2097152 | tf_op jit(solution)/shard_map/all_to_all | solution.py:314

commit v4 on v3

--- a/solution.py
+++ b/solution.py
@@ -288,10 +288,12 @@
 
     core = lax.axis_index("core")
     features = key_weight.shape[0]
-    kw, vw, _ = lax.optimization_barrier(
-        (key_weight[:, 0], value_weight[:, 0], (keys[3], keys[zn - 3]))
-    )
-    mine = lax.all_to_all(jnp.where(core == 0, kw, vw), HEAD, 0, 0, tiled=True)
+    picked = jnp.where(core == 0, key_weight[:, 0], value_weight[:, 0])
+    picked, third, third_back = lax.optimization_barrier(
+        (picked, keys[3], keys[zn - 3])
+    )
+    keys[3], keys[zn - 3] = third, third_back
+    mine = lax.all_to_all(picked, HEAD, 0, 0, tiled=True)
     mine = mine.reshape(8, features // 8, head_dim)
     other = moved(mine, "core", 1)
 

time: 136 us -> 137 us (level)
  waiting for transfers between devices: 40.2 us -> 44.6 us
    ppermute x16, waiting for transfers between devices: 5.9 us -> 8.23 us  [moved(): lax.ppermute(value, axis, [(i, (i + distance) % size) for i in range(size)])]
    all_to_all x1, waiting for transfers between devices: 22.9 us -> 24.9 us  [on_device(): back = lax.all_to_all(dkv, 'z', 0, 0, tiled=True)]
    ppermute x16, starting transfers between devices: 22 us -> 20.5 us  [moved(): lax.ppermute(value, axis, [(i, (i + distance) % size) for i in range(size)])]
  transfers between devices with their start and end apart: 19 -> 19, of which waited for: 6 -> 6; matrix products, arithmetic and copies ran while one was open for 9% -> 9% of each run, Pallas kernels for 23% -> 22%
where the time goes in v4:
time: 137 us; the launch traced here: 136 us
  waiting for transfers between devices  44.6 us (33%)
  starting transfers between devices  41.8 us (31%)
  Pallas kernels  33.8 us (25%)
  other arithmetic  11.6 us (8%)
  local copies, waits for them, and re-layouts  3.62 us (3%)
    pallas_call x1, Pallas kernels, visits(): pl.pallas_call(functools.partial(visits_kernel, nb=nb, m=m), out_shape=ou...  30.2 us
    all_to_all x1, waiting for transfers between devices, on_device(): back = lax.all_to_all(dkv, 'z', 0, 0, tiled=True)  24.9 us
    ppermute x16, starting transfers between devices, moved(): lax.ppermute(value, axis, [(i, (i + distance) % size) for i in range(size)])  20.5 us
    all_to_all x1, waiting for transfers between devices, on_device(): lax.all_to_all(jnp.broadcast_to(grads[None], (8,) + grads.shape), HEAD, 0...  11.4 us
    all_to_all x1, starting transfers between devices, on_device(): back = lax.all_to_all(dkv, 'z', 0, 0, tiled=True)  8.26 us
    ppermute x16, waiting for transfers between devices, moved(): lax.ppermute(value, axis, [(i, (i + distance) % size) for i in range(size)])  8.23 us
    all_to_all x1, starting transfers between devices, on_device(): lax.all_to_all(jnp.broadcast_to(grads[None], (8,) + grads.shape), HEAD, 0...  6.65 us
    all_to_all x1, starting transfers between devices, on_device(): mine = lax.all_to_all(picked, HEAD, 0, 0, tiled=True)  6.37 us
  transfers between devices with their start and end apart: 19, of which 6 were waited for; matrix products, arithmetic and copies ran while one was open for 9% of the time, Pallas kernels for 22%

profile of v4, /device:TPU:1, one launch (start us, length us, event | category | flops | bytes accessed | tf_op | source)
XLA Modules:
  0.0 136.3 jit_solution(5268886830949482220)
XLA Ops:
  0.6 0.0 copy-start.11
  0.7 2.4 %pad_maximum_fusion.refs_1_ = bf16[2,2,1024,128]{3,2,1,0:T(8,128)(2,1)} fusion(bf16[1,2,1024,128]{3,2,1,0:T(8,128)(2,1)} %bitcast.18, bf16[1,2,1024,128]{3,2,1,0:T(8,128)(2,1)} %bitcast.19), kind=kLoop, calls=%fused_computation.1 | loop fusion | flops 524288 | bytes 2097152 | tf_op jit(solution)/shard_map/stack | solution.py:283
  3.1 2.0 %collective-permute-start.1 = (bf16[2,2,1024,128]{3,2,1,0:T(8,128)(2,1)}, bf16[2,2,1024,128]{3,2,1,0:T(8,128)(2,1)}, u32[]{:S(2)}, u32[]{:S(2)}) collective-permute-start(bf16[2,2,1024,128]{3,2,1,0:T(8,128)(2,1)} %pad_maximum_fusion.refs_1_), channel_id=1, source_target_pairs={{0,128},{128,0},{1,129},{129,1},{2,130},{130,2},{3,131},{131,3},{4... | collective-permute-start | bytes 3145736 | tf_op jit(solution)/shard_map/ppermute | solution.py:258
  5.2 0.1 slice_reduce_fusion
  5.3 0.1 broadcast_in_dim.36
  5.4 0.1 reshape.71
  5.5 0.1 maximum_maximum_fusion.refs_8_
  5.6 5.7 %collective-permute-start.8 = (bf16[272,256]{1,0:T(8,128)(2,1)S(1)}, bf16[272,256]{1,0:T(8,128)(2,1)}, u32[]{:S(2)}, u32[]{:S(2)}) collective-permute-start(bf16[272,256]{1,0:T(8,128)(2,1)S(1)} %maximum_maximum_fusion.refs_8_), channel_id=1, source_target_pairs={{0,112},{16,0},{32,16},{48,32},{64,48},{80,64},{96,80},{112,96},{1... | collective-permute-start | bytes 417800 | tf_op jit(solution)/shard_map/ppermute | solution.py:258
  11.3 5.2 %collective-permute-done.5.refs_9_ = bf16[272,256]{1,0:T(8,128)(2,1)} collective-permute-done((bf16[272,256]{1,0:T(8,128)(2,1)S(1)}, bf16[272,256]{1,0:T(8,128)(2,1)}, u32[]{:S(2)}, u32[]{:S(2)}) %collective-permute-start.5) | collective-permute-done | bytes 139296 | tf_op jit(solution)/shard_map/ppermute | solution.py:258
  16.5 0.0 collective-permute-start.6
  16.5 0.6 multiply_reduce_fusion
  17.1 0.1 copy.15
  17.3 0.2 mul.18
  17.5 0.2 reshape.65
  17.7 0.8 convert_reduce_fusion
  18.5 0.0 collective-permute-done.8.refs_15_
  18.5 2.7 %collective-permute-start.9 = (bf16[272,256]{1,0:T(8,128)(2,1)}, bf16[272,256]{1,0:T(8,128)(2,1)}, u32[]{:S(2)}, u32[]{:S(2)}) collective-permute-start(bf16[272,256]{1,0:T(8,128)(2,1)} %collective-permute-done.8.refs_15_), channel_id=1, source_target_pairs={{0,112},{16,0},{32,16},{48,32},{64,48},{80,64},{96,80},{112,96},{1... | collective-permute-start | bytes 417800 | tf_op jit(solution)/shard_map/ppermute | solution.py:258
  21.2 0.7 collective-permute-done.6.refs_10_
  21.9 0.0 collective-permute-start.7
  21.9 0.1 broadcast_in_dim.34
  22.0 0.0 copy-start.6
  22.0 3.6 %collective-permute-start.3 = (f32[8,1024]{1,0:T(8,128)S(1)}, f32[8,1024]{1,0:T(8,128)S(1)}, u32[]{:S(2)}, u32[]{:S(2)}) collective-permute-start(f32[8,1024]{1,0:T(8,128)S(1)} %pad_maximum_fusion.1.refs_5_), channel_id=1, source_target_pairs={{0,8},{8,0},{1,9},{9,1},{2,10},{10,2},{3,11},{11,3},{4,12},{12,4},... | collective-permute-start | bytes 98312 | tf_op jit(solution)/shard_map/ppermute | solution.py:258
  25.6 0.1 collective-permute-start
  25.7 0.8 collective-permute-done.3.refs_6_
  26.5 0.3 collective-permute-start.4
  26.9 3.0 %collective-permute-start.10 = (bf16[272,256]{1,0:T(8,128)(2,1)}, bf16[272,256]{1,0:T(8,128)(2,1)}, u32[]{:S(2)}, u32[]{:S(2)}) collective-permute-start(bf16[272,256]{1,0:T(8,128)(2,1)} %collective-permute-done.9.refs_14_), channel_id=1, source_target_pairs={{0,112},{16,0},{32,16},{48,32},{64,48},{80,64},{96,80},{112,96},{1... | collective-permute-start | bytes 417800 | tf_op jit(solution)/shard_map/ppermute | solution.py:258
  29.9 2.2 %collective-permute-start.2 = (bf16[2,2,1024,128]{3,2,1,0:T(8,128)(2,1)}, bf16[2,2,1024,128]{3,2,1,0:T(8,128)(2,1)S(1)}, u32[]{:S(2)}, u32[]{:S(2)}) collective-permute-start(bf16[2,2,1024,128]{3,2,1,0:T(8,128)(2,1)} %collective-permute-done.1.refs_3_), channel_id=1, source_target_pairs={{0,8},{8,0},{1,9},{9,1},{2,10},{10,2},{3,11},{11,3},{4,12},{12,4},... | collective-permute-start | bytes 3145736 | tf_op jit(solution)/shard_map/ppermute | solution.py:258
  32.0 3.1 %select_bitcast_fusion = bf16[8192,128]{1,0:T(8,128)(2,1)} fusion(bf16[8192,1,128]{2,0,1:T(8,128)(2,1)S(1)} %copy-done, bf16[8192,1,128]{2,0,1:T(8,128)(2,1)} %param.17, pred[]{:T(512)S(6)} %eq.3), kind=kLoop, calls=%fused_computation | loop fusion | flops 1048576 | bytes 6291457 | tf_op jit(solution)/shard_map/jit(_where)/select_n | solution.py:291
  35.2 6.4 %all-to-all-start.1 = ((bf16[8,1024,128]{2,1,0:T(8,128)(2,1)}), bf16[8,1024,128]{2,1,0:T(8,128)(2,1)S(1)}, u32[]{:S(2)}, u32[]{:S(2)}) async-start(bf16[8,1024,128]{2,1,0:T(8,128)(2,1)} %bitcast.17), calls=%async_computation.1 | async-start | bytes 4194304 | tf_op jit(solution)/shard_map/all_to_all | solution.py:296
  41.6 0.0 copy-start.10
  41.6 0.6 copy-done.10
  42.2 0.4 copy-done.9
  42.6 30.2 %visits.1 = (bf16[2,1024,128]{2,1,0:T(8,128)(2,1)}, bf16[2,1024,128]{2,1,0:T(8,128)(2,1)}, bf16[2,1024,128]{2,1,0:T(8,128)(2,1)}, bf16[2,1024,128]{2,1,0:T(8,128)(2,1)}, bf16[8,256,256]{2,1,0:T(8,128)(2,1)}) custom-call(s32[1]{0:T(128)} %bitcast.refs_0_, bf16[2,2,1024,128]{3,2,1,0:T(8,128)(2,1)} %pad_maximum_fusion.refs_1_, ...), custom_call_target="tpu_custom_call" | custom-call | flops 21474836480 | bytes 12582912 | tf_op jit(solution)/shard_map/visits/pallas_call | solution.py:193
  72.8 8.3 %all-to-all-start = ((bf16[8,256,256]{2,1,0:T(8,128)(2,1)}), bf16[8,256,256]{2,1,0:T(8,128)(2,1)S(1)}, u32[]{:S(2)}, u32[]{:S(2)}) async-start(bf16[8,256,256]{2,1,0:T(8,128)(2,1)} %get-tuple-element.18), calls=%async_computation | async-start | bytes 2097152 | tf_op jit(solution)/shard_map/all_to_all | solution.py:306
  81.1 0.0 collective-permute-start.12
  81.1 0.5 collective-permute-start.15
  81.6 0.1 collective-permute-start.14
  81.7 1.5 %collective-permute-done.12 = bf16[2,1024,128]{2,1,0:T(8,128)(2,1)S(1)} collective-permute-done((bf16[2,1024,128]{2,1,0:T(8,128)(2,1)}, bf16[2,1024,128]{2,1,0:T(8,128)(2,1)S(1)}, u32[]{:S(2)}, u32[]{:S(2)}) %collective-permute-start.12) | collective-permute-done | bytes 524320 | tf_op jit(solution)/shard_map/ppermute | solution.py:258
  83.2 2.0 %add_convert_fusion.1 = bf16[2,1024,128]{2,1,0:T(8,128)(2,1)} fusion(bf16[2,1024,128]{2,1,0:T(8,128)(2,1)S(1)} %collective-permute-done.12, bf16[2,1024,128]{2,1,0:T(8,128)(2,1)} %get-tuple-element.19), kind=kLoop, calls=%fused_computation.3 | loop fusion | flops 1048576 | bytes 1572864 | tf_op jit(solution)/shard_map/convert_element_type | solution.py:310
  85.2 0.3 collective-permute-start.13
  85.4 24.9 %all-to-all-done = bf16[8,256,256]{2,1,0:T(8,128)(2,1)S(1)} async-done(((bf16[8,256,256]{2,1,0:T(8,128)(2,1)}), bf16[8,256,256]{2,1,0:T(8,128)(2,1)S(1)}, u32[]{:S(2)}, u32[]{:S(2)}) %all-to-all-start) | async-done | bytes 1048608 | tf_op jit(solution)/shard_map/all_to_all | solution.py:306
  110.3 0.1 reduce_sum.22
  110.5 1.1 broadcast_in_dim.41
  111.6 6.6 %all-to-all-start.2 = ((bf16[8,256,256]{2,1,0:T(8,128)(2,1)}), bf16[8,256,256]{2,1,0:T(8,128)(2,1)S(1)}, u32[]{:S(2)}, u32[]{:S(2)}) async-start(bf16[8,256,256]{2,1,0:T(8,128)(2,1)} %broadcast_in_dim.41), calls=%async_computation.2 | async-start | bytes 2097152 | tf_op jit(solution)/shard_map/all_to_all | solution.py:316
  118.2 0.7 slice_bitcast_fusion
  118.9 2.4 %add_convert_fusion = bf16[2,1024,128]{2,1,0:T(8,128)(2,1)} fusion(bf16[2,1024,128]{2,1,0:T(8,128)(2,1)} %collective-permute-done.13, bf16[2,1024,128]{2,1,0:T(8,128)(2,1)} %collective-permute-done.14, bf16[2,1024,128]{2,1,0:T(8,128)(2,1)} %get-tuple-element.17), kind=kLoop, calls=%fused_computation.2 | loop fusion | flops 1572864 | bytes 2097152 | tf_op jit(solution)/shard_map/convert_element_type | solution.py:313
  121.2 11.4 %all-to-all-done.2.grads_ref = bf16[8,256,256]{2,1,0:T(8,128)(2,1)S(1)} async-done(((bf16[8,256,256]{2,1,0:T(8,128)(2,1)}), bf16[8,256,256]{2,1,0:T(8,128)(2,1)S(1)}, u32[]{:S(2)}, u32[]{:S(2)}) %all-to-all-start.2) | async-done | bytes 1048608 | tf_op jit(solution)/shard_map/all_to_all | solution.py:316
  132.6 3.7 %input_grad.1 = bf16[1024,256]{1,0:T(8,128)(2,1)} custom-call(s32[1]{0:T(128)} %bitcast.11.core_ref, bf16[8,1024,128]{2,1,0:T(8,128)(2,1)S(1)} %all-to-all-done.1.mine_ref, bf16[8,1024,128]{2,1,0:T(8,128)(2,1)} %collective-permute-done.15.other_ref, bf16[8,256,256]{2,1,0:T(8,128)(2,1)S(1)} %all-to-all-done.2.grads_ref), custom_call_target="tpu_custom_call" | custom-call | flops 1073741824 | bytes 6291456 | tf_op jit(solution)/shard_map/input_grad/pallas_call | solution.py:243
  (39 shorter events, 0.2 us)
Async XLA Ops:
  0.6 15.9 %copy-start.1 = (bf16[2,256,4,128]{3,2,1,0:T(4,128)(2,1)S(1)}, bf16[2,256,4,128]{3,2,1,0:T(4,128)(2,1)}, u32[]{:S(2)}) copy-start(bf16[2,256,4,128]{3,2,1,0:T(4,128)(2,1)} %param.13) | copy-start | bytes 1572868
  0.6 4.5 %copy-start.11 = (s32[256]{0:T(256)S(1)}, s32[256]{0:T(256)}, u32[]{:S(2)}) copy-start(s32[256]{0:T(256)} %param.15) | copy-start | bytes 3076
  0.7 4.8 %copy-start.4 = (bf16[256,1,128]{2,0,1:T(8,128)(2,1)S(1)}, bf16[256,1,128]{2,0,1:T(8,128)(2,1)}, u32[]{:S(2)}) copy-start(bf16[256,1,128]{2,0,1:T(8,128)(2,1)} %param.11) | copy-start | bytes 196612
  0.7 4.8 %copy-start.5 = (bf16[256,1,128]{2,0,1:T(8,128)(2,1)S(1)}, bf16[256,1,128]{2,0,1:T(8,128)(2,1)}, u32[]{:S(2)}) copy-start(bf16[256,1,128]{2,0,1:T(8,128)(2,1)} %param.10) | copy-start | bytes 196612
  0.7 10.6 %copy-start.8 = (f32[2,4,256]{2,1,0:T(4,128)S(1)}, f32[2,4,256]{2,1,0:T(4,128)}, u32[]{:S(2)}) copy-start(f32[2,4,256]{2,1,0:T(4,128)} %param.14) | copy-start | bytes 24580
  0.7 15.8 %copy-start.2 = (bf16[2,256,4,128]{3,2,1,0:T(4,128)(2,1)S(1)}, bf16[2,256,4,128]{3,2,1,0:T(4,128)(2,1)}, u32[]{:S(2)}) copy-start(bf16[2,256,4,128]{3,2,1,0:T(4,128)(2,1)} %param.12) | copy-start | bytes 1572868
  0.7 31.3 %copy-start = (bf16[8192,1,128]{2,0,1:T(8,128)(2,1)S(1)}, bf16[8192,1,128]{2,0,1:T(8,128)(2,1)}, u32[]{:S(2)}) copy-start(bf16[8192,1,128]{2,0,1:T(8,128)(2,1)} %param.16) | copy-start | bytes 6291460
  3.1 26.7 %collective-permute-start.1 = (bf16[2,2,1024,128]{3,2,1,0:T(8,128)(2,1)}, bf16[2,2,1024,128]{3,2,1,0:T(8,128)(2,1)}, u32[]{:S(2)}, u32[]{:S(2)}) collective-permute-start(bf16[2,2,1024,128]{3,2,1,0:T(8,128)(2,1)} %pad_maximum_fusion.refs_1_), channel_id=1, source_target_pairs={{0,128},{128,0},{1,129},{129,1},{2,130},{130,2},{3,131},{131,3},{4... | collective-permute-start | bytes 3145736 | tf_op jit(solution)/shard_map/ppermute | solution.py:258
  5.6 29.6 %copy-start.3 = (bf16[272,256]{1,0:T(8,128)(2,1)}, bf16[272,256]{1,0:T(8,128)(2,1)S(1)}, u32[]{:S(2)}) copy-start(bf16[272,256]{1,0:T(8,128)(2,1)S(1)} %maximum_maximum_fusion.refs_8_) | copy-start | bytes 417796
  5.6 12.9 %collective-permute-start.8 = (bf16[272,256]{1,0:T(8,128)(2,1)S(1)}, bf16[272,256]{1,0:T(8,128)(2,1)}, u32[]{:S(2)}, u32[]{:S(2)}) collective-permute-start(bf16[272,256]{1,0:T(8,128)(2,1)S(1)} %maximum_maximum_fusion.refs_8_), channel_id=1, source_target_pairs={{0,112},{16,0},{32,16},{48,32},{64,48},{80,64},{96,80},{112,96},{1... | collective-permute-start | bytes 417800 | tf_op jit(solution)/shard_map/ppermute | solution.py:258
  11.3 5.2 %collective-permute-start.5 = (bf16[272,256]{1,0:T(8,128)(2,1)S(1)}, bf16[272,256]{1,0:T(8,128)(2,1)}, u32[]{:S(2)}, u32[]{:S(2)}) collective-permute-start(bf16[272,256]{1,0:T(8,128)(2,1)S(1)} %maximum_maximum_fusion.refs_8_), channel_id=1, source_target_pairs={{0,16},{16,32},{32,48},{48,64},{64,80},{80,96},{96,112},{112,0},{1... | collective-permute-start | bytes 417800 | tf_op jit(solution)/shard_map/ppermute | solution.py:258
  16.5 5.4 %collective-permute-start.6 = (bf16[272,256]{1,0:T(8,128)(2,1)}, bf16[272,256]{1,0:T(8,128)(2,1)}, u32[]{:S(2)}, u32[]{:S(2)}) collective-permute-start(bf16[272,256]{1,0:T(8,128)(2,1)} %collective-permute-done.5.refs_9_), channel_id=1, source_target_pairs={{0,16},{16,32},{32,48},{48,64},{64,80},{80,96},{96,112},{112,0},{1... | collective-permute-start | bytes 417800 | tf_op jit(solution)/shard_map/ppermute | solution.py:258
  18.5 8.4 %collective-permute-start.9 = (bf16[272,256]{1,0:T(8,128)(2,1)}, bf16[272,256]{1,0:T(8,128)(2,1)}, u32[]{:S(2)}, u32[]{:S(2)}) collective-permute-start(bf16[272,256]{1,0:T(8,128)(2,1)} %collective-permute-done.8.refs_15_), channel_id=1, source_target_pairs={{0,112},{16,0},{32,16},{48,32},{64,48},{80,64},{96,80},{112,96},{1... | collective-permute-start | bytes 417800 | tf_op jit(solution)/shard_map/ppermute | solution.py:258
  21.9 7.9 %collective-permute-start.7 = (bf16[272,256]{1,0:T(8,128)(2,1)}, bf16[272,256]{1,0:T(8,128)(2,1)}, u32[]{:S(2)}, u32[]{:S(2)}) collective-permute-start(bf16[272,256]{1,0:T(8,128)(2,1)} %collective-permute-done.6.refs_10_), channel_id=1, source_target_pairs={{0,16},{16,32},{32,48},{48,64},{64,80},{80,96},{96,112},{112,0},{1... | collective-permute-start | bytes 417800 | tf_op jit(solution)/shard_map/ppermute | solution.py:258
  22.0 13.2 %copy-start.6 = (f32[8,1024]{1,0:T(8,128)}, f32[8,1024]{1,0:T(8,128)S(1)}, u32[]{:S(2)}) copy-start(f32[8,1024]{1,0:T(8,128)S(1)} %pad_maximum_fusion.1.refs_5_) | copy-start | bytes 98308
  22.0 4.5 %collective-permute-start.3 = (f32[8,1024]{1,0:T(8,128)S(1)}, f32[8,1024]{1,0:T(8,128)S(1)}, u32[]{:S(2)}, u32[]{:S(2)}) collective-permute-start(f32[8,1024]{1,0:T(8,128)S(1)} %pad_maximum_fusion.1.refs_5_), channel_id=1, source_target_pairs={{0,8},{8,0},{1,9},{9,1},{2,10},{10,2},{3,11},{11,3},{4,12},{12,4},... | collective-permute-start | bytes 98312 | tf_op jit(solution)/shard_map/ppermute | solution.py:258
  25.6 16.0 %collective-permute-start = (bf16[2,2,1024,128]{3,2,1,0:T(8,128)(2,1)}, bf16[2,2,1024,128]{3,2,1,0:T(8,128)(2,1)}, u32[]{:S(2)}, u32[]{:S(2)}) collective-permute-start(bf16[2,2,1024,128]{3,2,1,0:T(8,128)(2,1)} %pad_maximum_fusion.refs_1_), channel_id=1, source_target_pairs={{0,8},{8,0},{1,9},{9,1},{2,10},{10,2},{3,11},{11,3},{4,12},{12,4},... | collective-permute-start | bytes 3145736 | tf_op jit(solution)/shard_map/ppermute | solution.py:258
  26.5 8.7 %copy-start.7 = (f32[8,1024]{1,0:T(8,128)}, f32[8,1024]{1,0:T(8,128)S(1)}, u32[]{:S(2)}) copy-start(f32[8,1024]{1,0:T(8,128)S(1)} %collective-permute-done.3.refs_6_) | copy-start | bytes 98308
  26.5 15.0 %collective-permute-start.4 = (f32[16,1024]{1,0:T(8,128)S(1)}, f32[16,1024]{1,0:T(8,128)S(1)}, u32[]{:S(2)}, u32[]{:S(2)}) collective-permute-start(f32[16,1024]{1,0:T(8,128)S(1)} %concatenate.14), channel_id=1, source_target_pairs={{0,128},{128,0},{1,129},{129,1},{2,130},{130,2},{3,131},{131,3},{4... | collective-permute-start | bytes 196616 | tf_op jit(solution)/shard_map/ppermute | solution.py:258
  26.9 8.3 %collective-permute-start.10 = (bf16[272,256]{1,0:T(8,128)(2,1)}, bf16[272,256]{1,0:T(8,128)(2,1)}, u32[]{:S(2)}, u32[]{:S(2)}) collective-permute-start(bf16[272,256]{1,0:T(8,128)(2,1)} %collective-permute-done.9.refs_14_), channel_id=1, source_target_pairs={{0,112},{16,0},{32,16},{48,32},{64,48},{80,64},{96,80},{112,96},{1... | collective-permute-start | bytes 417800 | tf_op jit(solution)/shard_map/ppermute | solution.py:258
  29.8 11.8 %collective-permute-start.11 = (bf16[272,256]{1,0:T(8,128)(2,1)}, bf16[272,256]{1,0:T(8,128)(2,1)}, u32[]{:S(2)}, u32[]{:S(2)}) collective-permute-start(bf16[272,256]{1,0:T(8,128)(2,1)} %collective-permute-done.7.refs_11_), channel_id=1, source_target_pairs={{0,16},{16,32},{32,48},{48,64},{64,80},{80,96},{96,112},{112,0},{1... | collective-permute-start | bytes 417800 | tf_op jit(solution)/shard_map/ppermute | solution.py:258
  29.9 11.8 %collective-permute-start.2 = (bf16[2,2,1024,128]{3,2,1,0:T(8,128)(2,1)}, bf16[2,2,1024,128]{3,2,1,0:T(8,128)(2,1)S(1)}, u32[]{:S(2)}, u32[]{:S(2)}) collective-permute-start(bf16[2,2,1024,128]{3,2,1,0:T(8,128)(2,1)} %collective-permute-done.1.refs_3_), channel_id=1, source_target_pairs={{0,8},{8,0},{1,9},{9,1},{2,10},{10,2},{3,11},{11,3},{4,12},{12,4},... | collective-permute-start | bytes 3145736 | tf_op jit(solution)/shard_map/ppermute | solution.py:258
  35.2 37.6 %all-to-all-start.1 = ((bf16[8,1024,128]{2,1,0:T(8,128)(2,1)}), bf16[8,1024,128]{2,1,0:T(8,128)(2,1)S(1)}, u32[]{:S(2)}, u32[]{:S(2)}) async-start(bf16[8,1024,128]{2,1,0:T(8,128)(2,1)} %bitcast.17), calls=%async_computation.1 | async-start | bytes 4194304 | tf_op jit(solution)/shard_map/all_to_all | solution.py:296
  41.6 0.6 copy-start.10
  41.6 1.0 copy-start.9
  72.8 37.6 %all-to-all-start = ((bf16[8,256,256]{2,1,0:T(8,128)(2,1)}), bf16[8,256,256]{2,1,0:T(8,128)(2,1)S(1)}, u32[]{:S(2)}, u32[]{:S(2)}) async-start(bf16[8,256,256]{2,1,0:T(8,128)(2,1)} %get-tuple-element.18), calls=%async_computation | async-start | bytes 2097152 | tf_op jit(solution)/shard_map/all_to_all | solution.py:306
  81.1 2.1 %collective-permute-start.12 = (bf16[2,1024,128]{2,1,0:T(8,128)(2,1)}, bf16[2,1024,128]{2,1,0:T(8,128)(2,1)S(1)}, u32[]{:S(2)}, u32[]{:S(2)}) collective-permute-start(bf16[2,1024,128]{2,1,0:T(8,128)(2,1)} %get-tuple-element.20), channel_id=1, source_target_pairs={{0,8},{8,0},{1,9},{9,1},{2,10},{10,2},{3,11},{11,3},{4,12},{12,4},... | collective-permute-start | bytes 1572872 | tf_op jit(solution)/shard_map/ppermute | solution.py:258
  81.1 40.2 %collective-permute-start.15 = (bf16[8,1024,128]{2,1,0:T(8,128)(2,1)S(1)}, bf16[8,1024,128]{2,1,0:T(8,128)(2,1)}, u32[]{:S(2)}, u32[]{:S(2)}) collective-permute-start(bf16[8,1024,128]{2,1,0:T(8,128)(2,1)S(1)} %all-to-all-done.1.mine_ref), channel_id=1, source_target_pairs={{0,8},{8,0},{1,9},{9,1},{2,10},{10,2},{3,11},{11,3},{4,12},{12,4},... | collective-permute-start | bytes 6291464 | tf_op jit(solution)/shard_map/ppermute | solution.py:258
  81.6 28.9 %collective-permute-start.14 = (bf16[2,1024,128]{2,1,0:T(8,128)(2,1)}, bf16[2,1024,128]{2,1,0:T(8,128)(2,1)}, u32[]{:S(2)}, u32[]{:S(2)}) collective-permute-start(bf16[2,1024,128]{2,1,0:T(8,128)(2,1)} %get-tuple-element.21), channel_id=1, source_target_pairs={{0,8},{8,0},{1,9},{9,1},{2,10},{10,2},{3,11},{11,3},{4,12},{12,4},... | collective-permute-start | bytes 1572872 | tf_op jit(solution)/shard_map/ppermute | solution.py:258
  85.2 25.4 %collective-permute-start.13 = (bf16[2,1024,128]{2,1,0:T(8,128)(2,1)}, bf16[2,1024,128]{2,1,0:T(8,128)(2,1)}, u32[]{:S(2)}, u32[]{:S(2)}) collective-permute-start(bf16[2,1024,128]{2,1,0:T(8,128)(2,1)} %add_convert_fusion.1), channel_id=1, source_target_pairs={{0,128},{128,0},{1,129},{129,1},{2,130},{130,2},{3,131},{131,3},{4... | collective-permute-start | bytes 1572872 | tf_op jit(solution)/shard_map/ppermute | solution.py:258
  111.6 21.1 %all-to-all-start.2 = ((bf16[8,256,256]{2,1,0:T(8,128)(2,1)}), bf16[8,256,256]{2,1,0:T(8,128)(2,1)S(1)}, u32[]{:S(2)}, u32[]{:S(2)}) async-start(bf16[8,256,256]{2,1,0:T(8,128)(2,1)} %broadcast_in_dim.41), calls=%async_computation.2 | async-start | bytes 2097152 | tf_op jit(solution)/shard_map/all_to_all | solution.py:316
